TPU v7x, 128 devices: a whole 4x4x4 slice. The times are simulated.
128 devices in a mesh: agent: 4 (over x_lo, core), tile: 32 (over x_hi, y, z).
Axes of the slice: x: 4 (x_hi: 2, x_lo: 2; x = x_hi * 2 + x_lo), y: 4, z: 4, core: 2. Of those that a mesh axis runs over, the one named last changes fastest.
Arguments:
- states: float32 [4, 4, 512, 512], P('agent', None, 'tile'), may hold values from -6 to 6
- sinogram: float32 [256, 4, 128], P('tile'), may hold values from -6 to 6
- blocks: bfloat16 [8192, 128, 128], P('tile'), may hold values from -0.09375 to 0.09375
- block_angle: int32 [8192], P('tile'), may hold values from 0 to 63
- block_detector: int32 [8192], P('tile'), may hold values from 0 to 3
- block_tile: int32 [8192], P('tile'), may hold values from 0 to 63
- conv_first: bfloat16 [3, 3, 3, 32], replicated, may hold values from -3 to 3
- conv_hidden: bfloat16 [3, 2, 3, 3, 32, 32], replicated, may hold values from -0.5 to 0.5
- conv_last: bfloat16 [3, 3, 3, 32], replicated, may hold values from -0.375 to 0.375
Outputs:
- new_states: float32 [4, 4, 512, 512], P('agent', None, 'tile')
Inputs may be any that keep to these rules, and one draw needn't show every extreme that they name: `block_angle`: each block's angle index. `block_detector`: each block's detector block. `block_tile`: tile index among the 64 pixel tiles of the block's device.
All inputs are finite; a program needn't handle non-finite values.
Results may differ from a plain program's by a relative error of at most 0.0051.
Values may be sent and summed in bfloat16 or wider, within the bound.
No kernel may reach another device: no remote copies, remote signals or barrier semaphores. Data moves between devices by JAX's collectives and lax.ppermute only.
A program may use at most 128 MiB of HBM per device.

v0:
```python
import functools

import jax
import jax.numpy as jnp
import numpy as np
from jax import lax
from jax.experimental import pallas as pl
from jax.experimental.pallas import tpu as pltpu
from jax.sharding import PartitionSpec as P

DATA_STEPS = 2
F32, BF16 = jnp.float32, jnp.bfloat16
VMEM_LIMIT = 32 << 20
TOGETHER = 4
UNROLL = 16
SPAN = 6


def params():
    return pltpu.CompilerParams(vmem_limit_bytes=VMEM_LIMIT)


def in_vmem():
    return pl.BlockSpec(memory_space=pltpu.VMEM)


def in_smem():
    return pl.BlockSpec(memory_space=pltpu.SMEM)


def low_rows():
    return lax.broadcasted_iota(jnp.int32, (8, 128), 0) < 4


def four_blocks(blk, b):
    size = blk.shape[1]
    left = blk[pl.ds(b, 2)].reshape(2 * size, size)
    right = blk[pl.ds(b + 2, 2)].reshape(2 * size, size)
    return jnp.concatenate([left, right], axis=1)


def row(ref, index):
    return ref[pl.ds(index, 8, stride=0), :]


def add_rows(acc, index, value):
    acc[index] = acc[index] + value


def project_blocks(ray_ref, tile_ref, pix, blk, acc):
    low = low_rows()
    zero = jnp.zeros((8, 128), F32)

    def body(i, carry):
        outs = []
        for u in range(UNROLL):
            b = (i * UNROLL + u) * TOGETHER
            t = [row(pix, tile_ref[b + k]) for k in range(TOGETHER)]
            upper = jnp.concatenate([jnp.where(low, t[0], t[1]), zero], axis=0)
            lower = jnp.concatenate([zero, jnp.where(low, t[2], t[3])], axis=0)
            lhs = jnp.concatenate([upper.astype(BF16), lower.astype(BF16)], axis=1)
            outs.append(
                lax.dot_general(
                    lhs, four_blocks(blk, b), (((1,), (1,)), ((), ())), preferred_element_type=F32
                )
            )
        for u in range(UNROLL):
            b = (i * UNROLL + u) * TOGETHER
            out = outs[u]
            add_rows(acc, ray_ref[b], jnp.where(low, out[0:8, 0:128], 0.0))
            add_rows(acc, ray_ref[b + 1], jnp.where(low, 0.0, out[0:8, 128:256]))
            add_rows(acc, ray_ref[b + 2], jnp.where(low, out[8:16, 0:128], 0.0))
            add_rows(acc, ray_ref[b + 3], jnp.where(low, 0.0, out[8:16, 128:256]))
        return carry

    lax.fori_loop(0, blk.shape[0] // (TOGETHER * UNROLL), body, 0)


def back_blocks(ray_ref, tile_ref, res, blk, acc):
    low = low_rows()

    def body(i, carry):
        outs = []
        for u in range(UNROLL):
            b = (i * UNROLL + u) * TOGETHER
            t = [row(res, ray_ref[b + k]) for k in range(TOGETHER)]
            left = jnp.concatenate([jnp.where(low, t[0], 0.0), jnp.where(low, t[2], 0.0)], axis=0)
            right = jnp.concatenate([jnp.where(low, 0.0, t[1]), jnp.where(low, 0.0, t[3])], axis=0)
            lhs = jnp.concatenate([left.astype(BF16), right.astype(BF16)], axis=1)
            outs.append(jnp.dot(lhs, four_blocks(blk, b), preferred_element_type=F32))
        for u in range(UNROLL):
            b = (i * UNROLL + u) * TOGETHER
            upper, lower = outs[u][0:8, 0:128], outs[u][8:16, 128:256]
            add_rows(acc, tile_ref[b], jnp.where(low, upper, 0.0))
            add_rows(acc, tile_ref[b + 1], jnp.where(low, 0.0, upper))
            add_rows(acc, tile_ref[b + 2], jnp.where(low, lower, 0.0))
            add_rows(acc, tile_ref[b + 3], jnp.where(low, 0.0, lower))
        return carry

    lax.fori_loop(0, blk.shape[0] // (TOGETHER * UNROLL), body, 0)


def tiles_of(x_shape):
    wide = x_shape[1] // 128
    return [(r, c, slice(c * 128, c * 128 + 128)) for r in range(x_shape[0]) for c in range(wide)]


def load_pixels(value, pix):
    wide = value.shape[1] // 128
    for r, c, columns in tiles_of(value.shape):
        pix[r * wide + c : r * wide + c + 1] = value[r : r + 1, columns]


def moved_by(x, back):
    wide = x.shape[1] // 128
    rows = back.shape[0]
    columns = []
    for c in range(wide):
        own = pl.ds(c, rows // wide, stride=wide)
        columns.append(back[own, 0, :] + back[own, 4, :])
    return x - 0.8 * jnp.concatenate(columns, axis=1)


def store_rays(place_ref, sino_ref, acc, total, o_ref):
    total[0 : acc.shape[0]] = acc[:, 0, :] + acc[:, 4, :]
    own = sino_ref.shape[0]
    mine = pl.ds(pl.multiple_of(place_ref[1] * own, own), own)
    for z in range(sino_ref.shape[1]):

        @pl.when(place_ref[0] == z)
        def _():
            total[mine] = total[mine] - sino_ref[:, z, :]

    o_ref[...] = total[0 : acc.shape[0]].astype(o_ref.dtype)


def project_kernel(place_ref, ray_ref, tile_ref, x_ref, sino_ref, blk, o_ref, pix, acc, total):
    load_pixels(x_ref[...], pix)
    acc[...] = jnp.zeros_like(acc)
    project_blocks(ray_ref, tile_ref, pix, blk, acc)
    store_rays(place_ref, sino_ref, acc, total, o_ref)


def project(place, ray_index, tile_index, x, sinogram, blocks, ray_total):
    tiles = x.size // 128
    return pl.pallas_call(
        project_kernel,
        out_shape=jax.ShapeDtypeStruct((ray_total, 128), BF16),
        in_specs=[in_smem()] * 3 + [in_vmem()] * 3,
        out_specs=in_vmem(),
        scratch_shapes=[
            pltpu.VMEM((tiles + 8, 128), F32),
            pltpu.VMEM((ray_total, 8, 128), F32),
            pltpu.VMEM((ray_total + 8, 128), F32),
        ],
        compiler_params=params(),
        name="project",
    )(place, ray_index, tile_index, x, sinogram, blocks)


def back_project_kernel(
    place_ref, ray_ref, tile_ref, r_ref, x_ref, sino_ref, blk, x_out, o_ref, res, pix, back, acc
):
    res[0 : r_ref.shape[0]] = r_ref[...].astype(F32)
    back[...] = jnp.zeros_like(back)
    back_blocks(ray_ref, tile_ref, res, blk, back)
    moved = moved_by(x_ref[...], back)
    x_out[...] = moved
    load_pixels(moved, pix)
    acc[...] = jnp.zeros_like(acc)
    project_blocks(ray_ref, tile_ref, pix, blk, acc)
    store_rays(place_ref, sino_ref, acc, res, o_ref)


def back_project(place, ray_index, tile_index, residual, x, sinogram, blocks):
    ray_total = residual.shape[0]
    tiles = x.size // 128
    return pl.pallas_call(
        back_project_kernel,
        out_shape=(
            jax.ShapeDtypeStruct(x.shape, F32),
            jax.ShapeDtypeStruct(residual.shape, BF16),
        ),
        in_specs=[in_smem()] * 3 + [in_vmem()] * 4,
        out_specs=(in_vmem(), in_vmem()),
        scratch_shapes=[
            pltpu.VMEM((ray_total + 8, 128), F32),
            pltpu.VMEM((tiles + 8, 128), F32),
            pltpu.VMEM((tiles, 8, 128), F32),
            pltpu.VMEM((ray_total, 8, 128), F32),
        ],
        compiler_params=params(),
        name="back_project",
    )(place, ray_index, tile_index, residual, x, sinogram, blocks)


def back_kernel(ray_ref, tile_ref, r_ref, x_ref, start_ref, blk, o_ref, res, back):
    res[0 : r_ref.shape[0]] = r_ref[...].astype(F32)
    back[...] = jnp.zeros_like(back)
    back_blocks(ray_ref, tile_ref, res, blk, back)
    o_ref[...] = 2.0 * moved_by(x_ref[...], back) - start_ref[...]


def back_reflect(ray_index, tile_index, residual, x, start, blocks):
    ray_total = residual.shape[0]
    tiles = x.size // 128
    return pl.pallas_call(
        back_kernel,
        out_shape=jax.ShapeDtypeStruct(x.shape, F32),
        in_specs=[in_smem()] * 2 + [in_vmem()] * 4,
        out_specs=in_vmem(),
        scratch_shapes=[
            pltpu.VMEM((ray_total + 8, 128), F32),
            pltpu.VMEM((tiles, 8, 128), F32),
        ],
        compiler_params=params(),
        name="back_reflect",
    )(ray_index, tile_index, residual, x, start, blocks)


def lanes(parts, count, height, width):
    empty = jnp.zeros((height, width), F32)
    return jnp.concatenate([parts.get(n, empty) for n in range(count)], axis=1)


def slice_band(first, hidden, last, o, zf, zh, zl, turn):
    turn[...] = jnp.zeros_like(turn)
    for j in range(3):
        for z in range(4):
            near = {y: z - y + 1 for y in range(4) if 0 <= z - y + 1 < 3}
            n = j * 4 + z
            parts = {y: first[o, i, j : j + 1, :].astype(F32) for y, i in near.items()}
            turn[n : n + 1, 0:128] = lanes(parts, 4, 1, 32)
    zf[...] = jnp.transpose(turn[0:128, 0:128])[:, 0:16].astype(BF16)
    for layer in range(hidden.shape[1]):
        for j in range(3):
            for z in range(4):
                near = {y: z - y + 1 for y in range(4) if 0 <= z - y + 1 < 3}
                parts = {y: hidden[o, layer, i, j].astype(F32) for y, i in near.items()}
                turn[z * 32 : z * 32 + 32, 0:128] = lanes(parts, 4, 32, 32)
            zh[layer, :, j * 128 : j * 128 + 128] = jnp.transpose(turn[0:128, 0:128]).astype(BF16)
    rows = []
    for y in range(4):
        parts = {
            j * 4 + z: last[o, z - y + 1, j : j + 1, :].astype(F32)
            for j in range(3)
            for z in range(4)
            if 0 <= z - y + 1 < 3
        }
        rows.append(lanes(parts, 12, 1, 32))
    zl[...] = jnp.concatenate(rows + [jnp.zeros((4, 384), F32)], axis=0).astype(BF16)


def widen(zh, zl, zw, zm):
    for layer in range(zh.shape[0]):
        zw[layer, 0:128, 0:384] = zh[layer]
        zw[layer, 0:128, 384:512] = jnp.zeros((128, 128), BF16)
        zw[layer, 128:256, 0:128] = jnp.zeros((128, 128), BF16)
        zw[layer, 128:256, 128:512] = zh[layer]
    plain = zl[...].astype(F32)
    rows = []
    for z in range(4):
        for a in range(4):
            parts = {a + n: plain[z : z + 1, n * 128 : n * 128 + 128] for n in range(3)}
            rows.append(lanes(parts, 6, 1, 128))
    zm[...] = jnp.concatenate(rows, axis=0).astype(BF16)


def row_band(first, hidden, last, af, ah, al, turn):
    turn[...] = jnp.zeros_like(turn)
    for j in range(3):
        for y in range(SPAN + 2):
            parts = {m: first[0, y - m, j : j + 1, :].astype(F32) for m in range(SPAN) if 0 <= y - m < 3}
            n = j * (SPAN + 2) + y
            turn[n : n + 1] = lanes(parts, 8, 1, 32)
    af[...] = jnp.transpose(turn[0:128])[0 : SPAN * 32, 0:32].astype(BF16)
    for layer in range(hidden.shape[1]):
        for j in range(3):
            for y in range(SPAN + 2):
                parts = {m: hidden[0, layer, y - m, j].astype(F32) for m in range(SPAN) if 0 <= y - m < 3}
                turn[y * 32 : y * 32 + 32] = lanes(parts, 8, 32, 32)
            ah[layer, j] = jnp.transpose(turn[...])[0 : SPAN * 32].astype(BF16)
    for j in range(3):
        rows = []
        for m in range(SPAN):
            parts = {m + i: last[0, i, j : j + 1, :].astype(F32) for i in range(3)}
            rows.append(lanes(parts, 8, 1, 32))
        rows.append(jnp.zeros((2, 256), F32))
        al[j] = jnp.concatenate(rows, axis=0).astype(BF16)


def prepare_kernel(
    place_ref, before, cur, after, first, hidden, last, rim, zf, zh, zl, zw, zm, af, ah, al, turn
):
    depth = before.shape[1]
    rows = cur.shape[1]
    rim[:, 0:depth] = before[...].astype(BF16).astype(F32)
    rim[:, depth : depth + rows] = cur[...].astype(BF16).astype(F32)
    rim[:, depth + rows :] = after[...].astype(BF16).astype(F32)

    @pl.when(place_ref[0] == 1)
    def _():
        row_band(first, hidden, last, af, ah, al, turn)

    @pl.when(place_ref[0] == 2)
    def _():
        slice_band(first, hidden, last, 1, zf, zh, zl, turn)
        widen(zh, zl, zw, zm)

    @pl.when(place_ref[0] == 3)
    def _():
        slice_band(first, hidden, last, 2, zf, zh, zl, turn)


def prepare(place, before, current, after, first, hidden, last):
    layers = hidden.shape[1]
    slices, rows, columns = current.shape
    rim = jax.ShapeDtypeStruct((slices, rows + 2 * before.shape[1], columns), F32)
    shapes = [
        (128, 16),
        (layers, 128, 384),
        (8, 384),
        (layers, 256, 512),
        (16, 768),
        (SPAN * 32, 32),
        (layers, 3, SPAN * 32, 256),
        (3, 8, 256),
    ]
    return pl.pallas_call(
        prepare_kernel,
        out_shape=[rim] + [jax.ShapeDtypeStruct(s, BF16) for s in shapes],
        in_specs=[in_smem()] + [in_vmem()] * 6,
        out_specs=[in_vmem()] * 9,
        scratch_shapes=[pltpu.VMEM((256, 256), F32)],
        compiler_params=params(),
        name="prepare",
    )(place, before, current, after, first, hidden, last)


def side_by_side(value):
    columns = value.shape[1]
    place = lax.broadcasted_iota(jnp.int32, value.shape, 1)
    before = jnp.where(place == 0, 0.0, pltpu.roll(value, 1, axis=1))
    after = jnp.where(place == columns - 1, 0.0, pltpu.roll(value, columns - 1, axis=1))
    return before, value, after


def relu_rows(value, keep):
    value = jnp.maximum(value, 0.0)
    return value if keep is None else jnp.where(keep, value, 0.0)


def sagittal_piece(part, columns, rows, above, below, rim, wf, wh, wl, o_ref, ha, hb):
    width = wf.shape[0]
    depth = wh.shape[0] + 1
    across = slice(part * columns, (part + 1) * columns)

    def kept(layer, y):
        reach = depth - layer
        return above if y < reach else below if y >= reach + rows else None

    empty = jnp.zeros((4, columns), F32)
    for y in range(rows + 2 * depth):
        taps = [rim[:, y + j, across] for j in range(3)] + [empty]
        taps = jnp.concatenate(taps, axis=0).astype(BF16)
        value = jnp.dot(wf[...], taps, preferred_element_type=F32)
        ha[y * width : (y + 1) * width] = relu_rows(value, kept(0, y)).astype(BF16)
    source, target = ha, hb
    for layer in range(wh.shape[0]):
        for y in range(0, rows + 2 * (depth - 1 - layer), 2):
            value = jnp.dot(
                wh[layer], source[y * width : (y + 4) * width], preferred_element_type=F32
            )
            for k in range(2):
                part_k = value[k * width : (k + 1) * width]
                target[(y + k) * width : (y + k + 1) * width] = relu_rows(
                    part_k, kept(layer + 1, y + k)
                ).astype(BF16)
        source, target = target, source
    for y in range(0, rows, 4):
        net = jnp.dot(wl[...], source[y * width : (y + 6) * width], preferred_element_type=F32)
        for z in range(4):
            o_ref[z, y : y + 4, across] = net[z * 4 : z * 4 + 4]


def coronal_piece(start, count, depth, rim, wf, wh, wl, o_ref, h):
    columns = rim.shape[2]
    width = wf.shape[0]
    empty = jnp.zeros((4, columns), F32)
    values = []
    for r in range(count):
        taps = jnp.concatenate([*side_by_side(rim[:, depth + start + r, :]), empty], axis=0)
        values.append(jnp.dot(wf[...], taps.astype(BF16), preferred_element_type=F32))
    for layer in range(wh.shape[0] + 1):
        matrix = wh[layer] if layer < wh.shape[0] else wl[...]
        for r in range(count):
            for j, moved in enumerate(side_by_side(jnp.maximum(values[r], 0.0))):
                h[r, j * width : (j + 1) * width] = moved.astype(BF16)
            values[r] = jnp.dot(matrix, h[r], preferred_element_type=F32)
    for r in range(count):
        o_ref[:, start + r, :] = values[r][0:4]


def spans(rows):
    starts = list(range(0, rows - SPAN, SPAN))
    return starts + [rows - SPAN]


def axial_piece(z, rows, above, below, rim, wf, wh, wl, o_ref, ha, hb):
    channels = wh.shape[3] // (SPAN + 2)
    depth = wh.shape[0] + 1

    def put(target, layer, start, value):
        value = jnp.maximum(value, 0.0)
        reach = depth - layer
        parts = []
        for k in range(SPAN):
            part = value[k * channels : (k + 1) * channels]
            y = start + k
            if y < reach:
                part = jnp.where(above, part, 0.0)
            elif y >= reach + rows:
                part = jnp.where(below, part, 0.0)
            parts.append(part)
        value = jnp.concatenate(parts, axis=0)
        for j, moved in enumerate(side_by_side(value)):
            target[j, start * channels : (start + SPAN) * channels] = moved.astype(BF16)

    def over_columns(matrices, source, start):
        total = None
        for j in range(3):
            window = source[j, start * channels : (start + SPAN + 2) * channels]
            part = jnp.dot(matrices[j], window, preferred_element_type=F32)
            total = part if total is None else total + part
        return total

    around = side_by_side(rim[z])
    empty = jnp.zeros((SPAN + 2, rim.shape[2]), F32)
    for start in spans(rows + 2 * depth):
        taps = [moved[start : start + SPAN + 2] for moved in around] + [empty]
        taps = jnp.concatenate(taps, axis=0).astype(BF16)
        put(ha, 0, start, jnp.dot(wf[...], taps, preferred_element_type=F32))
    source, target = ha, hb
    for layer in range(wh.shape[0]):
        for start in spans(rows + 2 * (depth - 1 - layer)):
            put(target, layer + 1, start, over_columns(wh[layer], source, start))
        source, target = target, source
    for start in spans(rows):
        o_ref[z, start : start + SPAN] = over_columns(wl[...], source, start)[0:SPAN]


def piece_kernel(
    k, place_ref, net, rim, zf, zh, zl, zw, zm, af, ah, al, o_ref, sa, sb, ca, xa, xb
):
    rows = o_ref.shape[1]
    depth = (rim.shape[1] - rows) // 2
    above, below = place_ref[1] > 0, place_ref[1] < place_ref[2] - 1
    o_ref[...] = net[...]

    @pl.when(place_ref[0] == 1)
    def _():
        axial_piece(k, rows, above, below, rim, af, ah, al, o_ref, xa, xb)

    if k < 2:

        @pl.when(place_ref[0] == 2)
        def _():
            half = o_ref.shape[2] // 2
            sagittal_piece(k, half, rows, above, below, rim, zf, zw, zm, o_ref, sa, sb)

    @pl.when(place_ref[0] == 3)
    def _():
        coronal_piece(k * (rows // 4), rows // 4, depth, rim, zf, zh, zl, o_ref, ca)


def piece(k, place, net, prepared):
    slices, rows, columns = net.shape
    reach = rows + 6
    return pl.pallas_call(
        functools.partial(piece_kernel, k),
        out_shape=jax.ShapeDtypeStruct(net.shape, F32),
        in_specs=[in_smem()] + [in_vmem()] * (1 + len(prepared)),
        out_specs=in_vmem(),
        scratch_shapes=[pltpu.VMEM((reach * 128, columns // 2), BF16)] * 2
        + [pltpu.VMEM((rows // 4, 384, columns), BF16)]
        + [pltpu.VMEM((3, reach * 32, columns), BF16)] * 2,
        compiler_params=params(),
        name=f"piece_{k}",
    )(place, net, *prepared)


def swapped(groups, k):
    return [(g[n], g[(n + k) % len(g)]) for g in groups for n in range(len(g))]


def stage_groups(count):
    near = 4
    strided = 4
    far = count // (near * strided)
    at = lambda f, s, n: (f * strided + s) * near + n
    return [
        [[at(f, s, n) for f in range(far)] for s in range(strided) for n in range(near)],
        [[at(f, s, n) for s in range(strided)] for f in range(far) for n in range(near)],
        [[at(f, s, n) for n in range(near)] for f in range(far) for s in range(strided)],
    ]


def added_up(values, groups):
    total = values.astype(F32)
    for k in range(1, len(groups[0])):
        total = total + lax.ppermute(values, "tile", swapped(groups, k)).astype(F32)
    return total.astype(values.dtype)


def rims(cells, depth):
    agents, count = 4, lax.axis_size("tile")
    pairs = [(a * count + t, a * count + t + 1) for a in (1, 2) for t in range(count - 1)]
    both = ("agent", "tile")
    before = lax.ppermute(cells[:, cells.shape[1] - depth :], both, pairs)
    after = lax.ppermute(cells[:, 0:depth], both, [(b, a) for a, b in pairs])
    return before, after


def own_slice(current, agent_place):
    start = current[0]
    for k in range(1, current.shape[0]):
        got = lax.ppermute(current[k], "agent", [(0, k)])
        start = jnp.where(agent_place == k, got, start)
    return start


def per_device(
    states,
    sinogram,
    blocks,
    block_angle,
    block_detector,
    block_tile,
    conv_first,
    conv_hidden,
    conv_last,
):
    current = states[0]
    tile_count = lax.axis_size("tile")
    tile_place = lax.axis_index("tile")
    agent_place = lax.axis_index("agent")
    place = jnp.stack([agent_place, tile_place, jnp.int32(tile_count)]).astype(jnp.int32)
    ray_total = sinogram.shape[0] * tile_count
    ray_index = block_angle * (current.shape[2] // 128) + block_detector

    start = own_slice(current, agent_place)
    before, after = rims(current, conv_hidden.shape[1] + 2)
    sums = project(place, ray_index, block_tile, start, sinogram, blocks, ray_total)

    groups = stage_groups(tile_count)
    net = jnp.zeros_like(current)
    x_data = start
    prepared = None
    k = 0
    for step in range(DATA_STEPS):
        for n, group in enumerate(groups):
            tied = lax.optimization_barrier((sums, net, before, after))
            sums, net, before, after = tied
            if n == 0 and step == 0:
                prepared = prepare(place, before, current, after, conv_first, conv_hidden, conv_last)
            elif n > 0:
                net = piece(k, place, net, prepared)
                k += 1
            sums = added_up(sums, group)
        if step < DATA_STEPS - 1:
            x_data, sums = back_project(place, ray_index, block_tile, sums, x_data, sinogram, blocks)
    reflect_data = back_reflect(ray_index, block_tile, sums, x_data, start, blocks)

    sent = jnp.concatenate([reflect_data[None], current - 2.0 * net], axis=0).astype(BF16)
    everything = lax.all_gather(sent, "agent").astype(F32)
    reflect_data = everything[:, 0]
    average = (reflect_data + everything[1, 1:] + everything[2, 1:] + everything[3, 1:]) / 4.0
    own = jnp.where(agent_place == 0, 0.5 * (current - reflect_data), net)
    return (average + own)[None]


def solution(mesh):
    placed = (
        P("agent", None, "tile", None),
        P("tile", None, None),
        P("tile", None, None),
        P("tile"),
        P("tile"),
        P("tile"),
        P(),
        P(),
        P(),
    )
    return jax.shard_map(
        per_device,
        mesh=mesh,
        in_specs=placed,
        out_specs=P("agent", None, "tile", None),
        check_vma=False,
    )
```

profile of v0, /device:TPU:1, one launch (start us, length us, event | category | flops | bytes accessed | tf_op | source)
XLA Modules:
  0.0 97.7 jit_solution(8950812030046557265)
XLA Ops:
  0.0 0.0 copy-start.10
  0.0 0.0 copy-start.9
  0.0 1.0 fusion.9
  1.0 1.3 %collective-permute-start.4 = (f32[4,4,512]{2,1,0:T(4,128)S(1)}, f32[4,4,512]{2,1,0:T(4,128)S(1)}, u32[]{:S(2)}, u32[]{:S(2)}) collective-permute-start(f32[4,4,512]{2,1,0:T(4,128)S(1)} %get-tuple-element.55), channel_id=1, source_target_pairs={{33,32},{34,33},{35,34},{36,35},{37,36},{38,37},{39,38},{40,39},{4... | collective-permute-start | bytes 98312 | tf_op jit(solution)/shard_map/ppermute | solution.py:520
  2.3 5.0 %collective-permute-start.3 = (f32[4,4,512]{2,1,0:T(4,128)S(1)}, f32[4,4,512]{2,1,0:T(4,128)S(1)}, u32[]{:S(2)}, u32[]{:S(2)}) collective-permute-start(f32[4,4,512]{2,1,0:T(4,128)S(1)} %get-tuple-element.56), channel_id=1, source_target_pairs={{32,33},{33,34},{34,35},{35,36},{36,37},{37,38},{38,39},{39,40},{4... | collective-permute-start | bytes 98312 | tf_op jit(solution)/shard_map/ppermute | solution.py:519
  7.3 0.8 slice_bitcast_fusion.4
  8.1 1.3 %collective-permute-start.2 = (f32[16,512]{1,0:T(8,128)S(1)}, f32[16,512]{1,0:T(8,128)S(1)}, u32[]{:S(2)}, u32[]{:S(2)}) collective-permute-start(f32[16,512]{1,0:T(8,128)S(1)} %get-tuple-element.57), channel_id=1, source_target_pairs={{0,32},{1,33},{2,34},{3,35},{4,36},{5,37},{6,38},{7,39},{8,40},{9,... | collective-permute-start | bytes 98312 | tf_op jit(solution)/shard_map/ppermute | solution.py:527
  9.4 0.7 collective-permute-start.1
  10.1 0.7 collective-permute-start
  10.8 0.7 multiply_add_fusion.ray_ref
  11.5 0.1 pad_add_fusion.place_ref
  11.5 0.0 collective-permute-done.2
  11.5 0.0 collective-permute-done.1
  11.5 0.0 collective-permute-done
  11.5 0.8 fusion.8.x_ref.start_ref
  12.3 0.0 copy-start
  12.3 3.4 %copy-done = bf16[256,128,128]{2,1,0:T(8,128)(2,1)S(1)} copy-done((bf16[256,128,128]{2,1,0:T(8,128)(2,1)S(1)}, bf16[256,128,128]{2,1,0:T(8,128)(2,1)}, u32[]{:S(2)}) %copy-start) | copy-done | bytes 8388632
  15.7 0.7 copy-done.5
  16.4 0.7 copy-done.7
  17.1 3.5 %project.1 = bf16[256,128]{1,0:T(8,128)(2,1)S(1)} custom-call(s32[3]{0:T(128)S(1)} %pad_add_fusion.place_ref, s32[256]{0:T(256)S(1)} %multiply_add_fusion.ray_ref, s32[256]{0:T(256)S(1)} %copy-done.7, f32[16,512]{1,0:T(8,128)S(1)} %fusion.8.x_ref.start_ref, f32[8,4,128]{2,1,0:T(4,128)S(1)} %copy-done.5, bf16[256,128,128]{2,1,0:T(8,128)(2,1)S(1)} %copy-done), custom_call_target="tpu_custom_call" | custom-call | tf_op jit(solution)/shard_map/project/pallas_call | solution.py:146
  20.6 0.0 collective-permute-done.4.after
  20.6 0.0 collective-permute-done.3.before
  20.7 7.3 %collective-permute-start.5 = (bf16[256,128]{1,0:T(8,128)(2,1)S(1)}, bf16[256,128]{1,0:T(8,128)(2,1)S(1)}, u32[]{:S(2)}, u32[]{:S(2)}) collective-permute-start(bf16[256,128]{1,0:T(8,128)(2,1)S(1)} %project.1), channel_id=1, source_target_pairs={{0,16},{16,0},{1,17},{17,1},{2,18},{18,2},{3,19},{19,3},{4,20},{20... | collective-permute-start | bytes 196616 | tf_op jit(solution)/shard_map/ppermute | solution.py:511
  28.0 1.7 %collective-permute-done.5 = bf16[256,128]{1,0:T(8,128)(2,1)S(1)} collective-permute-done((bf16[256,128]{1,0:T(8,128)(2,1)S(1)}, bf16[256,128]{1,0:T(8,128)(2,1)S(1)}, u32[]{:S(2)}, u32[]{:S(2)}) %collective-permute-start.5) | collective-permute-done | bytes 65568 | tf_op jit(solution)/shard_map/ppermute | solution.py:511
  29.7 0.8 collective-permute-start.8
  30.5 0.1 collective-permute-start.7
  30.5 0.7 collective-permute-start.6
  31.2 0.0 copy-done.3
  31.2 1.0 %copy-done.4 = bf16[3,2,3,3,32,32]{5,4,3,2,1,0:T(8,128)(2,1)S(1)} copy-done((bf16[3,2,3,3,32,32]{5,4,3,2,1,0:T(8,128)(2,1)S(1)}, bf16[3,2,3,3,32,32]{5,4,3,2,1,0:T(8,128)(2,1)}, u32[]{:S(2)}) %copy-start.4) | copy-done | bytes 110616
  32.3 1.1 %prepare.1 = (f32[4,24,512]{2,1,0:T(8,128)S(1)}, bf16[128,16]{1,0:T(8,128)(2,1)S(1)}, bf16[2,128,384]{2,1,0:T(8,128)(2,1)S(1)}, bf16[8,384]{1,0:T(8,128)(2,1)S(1...) custom-call(s32[3]{0:T(128)S(1)} %pad_add_fusion.place_ref, ...), custom_call_target="tpu_custom_call" | custom-call | tf_op jit(solution)/shard_map/prepare/pallas_call | solution.py:329
  33.4 2.6 %piece_0.1.net = f32[4,16,512]{2,1,0:T(8,128)S(1)} custom-call(s32[3]{0:T(128)S(1)} %pad_add_fusion.place_ref, f32[4,16,512]{2,1,0:T(8,128)S(1)} %broadcast_in_dim.7.net, f32[4,24,512]{2,1,0:T(8,128)S(1)} %get-tuple-element.36.rim, bf16[128,16]{1,0:T(8,128)(2,1)S(1)} %get-tuple-element.37.zf, bf16[2,128,384]{2,1,0:T(8,128)(2,1)S(1)} %get-tuple-element.38.zh, ...), custom_call_target="tpu_custom_call" | custom-call | tf_op jit(solution)/shard_map/piece_0/pallas_call | solution.py:479
  36.0 0.0 collective-permute-done.8
  36.0 0.0 collective-permute-done.7
  36.0 0.0 collective-permute-done.6
  36.1 7.0 %collective-permute-start.11 = (bf16[256,128]{1,0:T(8,128)(2,1)S(1)}, bf16[256,128]{1,0:T(8,128)(2,1)S(1)}, u32[]{:S(2)}, u32[]{:S(2)}) collective-permute-start(bf16[256,128]{1,0:T(8,128)(2,1)S(1)} %add_convert_fusion.4), channel_id=1, source_target_pairs={{0,3},{1,0},{2,1},{3,2},{4,7},{5,4},{6,5},{7,6},{8,11},{9,8},{10,9... | collective-permute-start | bytes 196616 | tf_op jit(solution)/shard_map/ppermute | solution.py:511
  43.0 0.0 collective-permute-start.10
  43.1 0.7 collective-permute-start.9
  43.7 2.7 %piece_1.1.net = f32[4,16,512]{2,1,0:T(8,128)S(1)} custom-call(s32[3]{0:T(128)S(1)} %pad_add_fusion.place_ref, f32[4,16,512]{2,1,0:T(8,128)S(1)} %piece_0.1.net, f32[4,24,512]{2,1,0:T(8,128)S(1)} %get-tuple-element.36.rim, bf16[128,16]{1,0:T(8,128)(2,1)S(1)} %get-tuple-element.37.zf, bf16[2,128,384]{2,1,0:T(8,128)(2,1)S(1)} %get-tuple-element.38.zh, ...), custom_call_target="tpu_custom_call" | custom-call | tf_op jit(solution)/shard_map/piece_1/pallas_call | solution.py:479
  46.4 0.0 collective-permute-done.11
  46.4 1.4 %collective-permute-done.10 = bf16[256,128]{1,0:T(8,128)(2,1)S(1)} collective-permute-done((bf16[256,128]{1,0:T(8,128)(2,1)S(1)}, bf16[256,128]{1,0:T(8,128)(2,1)S(1)}, u32[]{:S(2)}, u32[]{:S(2)}) %collective-permute-start.10) | collective-permute-done | bytes 65568 | tf_op jit(solution)/shard_map/ppermute | solution.py:511
  47.8 0.3 collective-permute-done.9
  48.2 5.3 %back_project.1 = (f32[16,512]{1,0:T(8,128)S(1)}, bf16[256,128]{1,0:T(8,128)(2,1)S(1)}) custom-call(s32[3]{0:T(128)S(1)} %pad_add_fusion.place_ref, s32[256]{0:T(256)S(1)} %multiply_add_fusion.ray_ref, s32[256]{0:T(256)S(1)} %copy-done.8, bf16[256,128]{1,0:T(8,128)(2,1)S(1)} %add_convert_fusion.3.r_ref, f32[16,512]{1,0:T(8,128)S(1)} %fusion.8.x_ref.start_ref, ...), custom_call_target="tpu_custom_call" | custom-call | tf_op jit(solution)/shard_map/back_project/pallas_call | solution.py:178
  53.5 0.1 collective-permute-start.12
  53.6 4.6 %collective-permute-done.12 = bf16[256,128]{1,0:T(8,128)(2,1)S(1)} collective-permute-done((bf16[256,128]{1,0:T(8,128)(2,1)S(1)}, bf16[256,128]{1,0:T(8,128)(2,1)S(1)}, u32[]{:S(2)}, u32[]{:S(2)}) %collective-permute-start.12) | collective-permute-done | bytes 65568 | tf_op jit(solution)/shard_map/ppermute | solution.py:511
  58.2 2.1 %collective-permute-start.15 = (bf16[256,128]{1,0:T(8,128)(2,1)S(1)}, bf16[256,128]{1,0:T(8,128)(2,1)S(1)}, u32[]{:S(2)}, u32[]{:S(2)}) collective-permute-start(bf16[256,128]{1,0:T(8,128)(2,1)S(1)} %add_convert_fusion.2), channel_id=1, source_target_pairs={{0,12},{4,0},{8,4},{12,8},{1,13},{5,1},{9,5},{13,9},{2,14},{6,2},{... | collective-permute-start | bytes 196616 | tf_op jit(solution)/shard_map/ppermute | solution.py:511
  60.3 1.8 %collective-permute-start.14 = (bf16[256,128]{1,0:T(8,128)(2,1)S(1)}, bf16[256,128]{1,0:T(8,128)(2,1)S(1)}, u32[]{:S(2)}, u32[]{:S(2)}) collective-permute-start(bf16[256,128]{1,0:T(8,128)(2,1)S(1)} %add_convert_fusion.2), channel_id=1, source_target_pairs={{0,8},{4,12},{8,0},{12,4},{1,9},{5,13},{9,1},{13,5},{2,10},{6,14},... | collective-permute-start | bytes 196616 | tf_op jit(solution)/shard_map/ppermute | solution.py:511
  62.0 0.0 collective-permute-start.13
  62.0 2.6 %piece_2.1.net = f32[4,16,512]{2,1,0:T(8,128)S(1)} custom-call(s32[3]{0:T(128)S(1)} %pad_add_fusion.place_ref, f32[4,16,512]{2,1,0:T(8,128)S(1)} %piece_1.1.net, f32[4,24,512]{2,1,0:T(8,128)S(1)} %get-tuple-element.36.rim, bf16[128,16]{1,0:T(8,128)(2,1)S(1)} %get-tuple-element.37.zf, bf16[2,128,384]{2,1,0:T(8,128)(2,1)S(1)} %get-tuple-element.38.zh, ...), custom_call_target="tpu_custom_call" | custom-call | tf_op jit(solution)/shard_map/piece_2/pallas_call | solution.py:479
  64.6 0.0 collective-permute-done.15
  64.6 0.3 collective-permute-done.14
  64.9 1.8 %collective-permute-done.13 = bf16[256,128]{1,0:T(8,128)(2,1)S(1)} collective-permute-done((bf16[256,128]{1,0:T(8,128)(2,1)S(1)}, bf16[256,128]{1,0:T(8,128)(2,1)S(1)}, u32[]{:S(2)}, u32[]{:S(2)}) %collective-permute-start.13) | collective-permute-done | bytes 65568 | tf_op jit(solution)/shard_map/ppermute | solution.py:511
  66.7 0.6 collective-permute-start.18
  67.3 1.2 %collective-permute-start.17 = (bf16[256,128]{1,0:T(8,128)(2,1)S(1)}, bf16[256,128]{1,0:T(8,128)(2,1)S(1)}, u32[]{:S(2)}, u32[]{:S(2)}) collective-permute-start(bf16[256,128]{1,0:T(8,128)(2,1)S(1)} %add_convert_fusion.1), channel_id=1, source_target_pairs={{0,2},{1,3},{2,0},{3,1},{4,6},{5,7},{6,4},{7,5},{8,10},{9,11},{10,... | collective-permute-start | bytes 196616 | tf_op jit(solution)/shard_map/ppermute | solution.py:511
  68.6 0.0 collective-permute-start.16
  68.6 2.6 %piece_3.1 = f32[4,16,512]{2,1,0:T(8,128)S(1)} custom-call(s32[3]{0:T(128)S(1)} %pad_add_fusion.place_ref, f32[4,16,512]{2,1,0:T(8,128)S(1)} %piece_2.1.net, f32[4,24,512]{2,1,0:T(8,128)S(1)} %get-tuple-element.36.rim, bf16[128,16]{1,0:T(8,128)(2,1)S(1)} %get-tuple-element.37.zf, bf16[2,128,384]{2,1,0:T(8,128)(2,1)S(1)} %get-tuple-element.38.zh, ...), custom_call_target="tpu_custom_call" | custom-call | tf_op jit(solution)/shard_map/piece_3/pallas_call | solution.py:479
  71.2 0.0 collective-permute-done.18
  71.2 0.8 collective-permute-done.17
  71.9 0.9 collective-permute-done.16
  72.9 0.0 copy-start.2
  72.9 3.4 %copy-done.2 = bf16[256,128,128]{2,1,0:T(8,128)(2,1)S(1)} copy-done((bf16[256,128,128]{2,1,0:T(8,128)(2,1)S(1)}, bf16[256,128,128]{2,1,0:T(8,128)(2,1)}, u32[]{:S(2)}) %copy-start.2) | copy-done | bytes 8388632
  76.3 2.4 %back_reflect.1 = f32[16,512]{1,0:T(8,128)S(1)} custom-call(s32[256]{0:T(256)S(1)} %multiply_add_fusion.ray_ref, s32[256]{0:T(256)S(1)} %copy-done.8, bf16[256,128]{1,0:T(8,128)(2,1)S(1)} %add_convert_fusion.r_ref, f32[16,512]{1,0:T(8,128)S(1)} %get-tuple-element.53.x_ref, f32[16,512]{1,0:T(8,128)S(1)} %fusion.8.x_ref.start_ref, ...), custom_call_target="tpu_custom_call" | custom-call | tf_op jit(solution)/shard_map/back_reflect/pallas_call | solution.py:207
  78.8 18.2 %all_gather.4 = bf16[4,5,16,512]{3,2,1,0:T(8,128)(2,1)S(1)} all-gather(bf16[1,5,16,512]{3,2,1,0:T(8,128)(2,1)S(1)} %pad_maximum_fusion), channel_id=1, replica_groups=mesh['agent'=4,'tile'=32] {'agent'}, dimensions={0}, use_global_device_ids=true | all-gather | bytes 409600 | tf_op jit(solution)/shard_map/all_gather | solution.py:575
  96.9 0.1 convert_element_type.115
  97.0 0.7 fusion.3
  (22 shorter events, 0.3 us)
Async XLA Ops:
  0.0 31.2 %copy-start.3 = (f32[1,4,16,512]{3,2,1,0:T(8,128)S(1)}, f32[1,4,16,512]{3,2,1,0:T(8,128)}, u32[]{:S(2)}) copy-start(f32[1,4,16,512]{3,2,1,0:T(8,128)} %param.9) | copy-start | bytes 393220
  0.0 48.1 %copy-start.8 = (s32[256]{0:T(256)S(1)}, s32[256]{0:T(256)}, u32[]{:S(2)}) copy-start(s32[256]{0:T(256)} %tile_ref.5) | copy-start | bytes 3076
  0.0 48.1 %copy-start.6 = (f32[8,4,128]{2,1,0:T(4,128)S(1)}, f32[8,4,128]{2,1,0:T(4,128)}, u32[]{:S(2)}) copy-start(f32[8,4,128]{2,1,0:T(4,128)} %sino_ref.3) | copy-start | bytes 49156
  0.0 31.2 %copy-start.10 = (bf16[3,3,3,32]{3,2,1,0:T(4,128)(2,1)S(1)}, bf16[3,3,3,32]{3,2,1,0:T(4,128)(2,1)}, u32[]{:S(2)}) copy-start(bf16[3,3,3,32]{3,2,1,0:T(4,128)(2,1)} %last.1) | copy-start | bytes 5188
  0.0 31.2 %copy-start.9 = (bf16[3,3,3,32]{3,2,1,0:T(4,128)(2,1)S(1)}, bf16[3,3,3,32]{3,2,1,0:T(4,128)(2,1)}, u32[]{:S(2)}) copy-start(bf16[3,3,3,32]{3,2,1,0:T(4,128)(2,1)} %first.1) | copy-start | bytes 5188
  1.0 19.6 %collective-permute-start.4 = (f32[4,4,512]{2,1,0:T(4,128)S(1)}, f32[4,4,512]{2,1,0:T(4,128)S(1)}, u32[]{:S(2)}, u32[]{:S(2)}) collective-permute-start(f32[4,4,512]{2,1,0:T(4,128)S(1)} %get-tuple-element.55), channel_id=1, source_target_pairs={{33,32},{34,33},{35,34},{36,35},{37,36},{38,37},{39,38},{40,39},{4... | collective-permute-start | bytes 98312 | tf_op jit(solution)/shard_map/ppermute | solution.py:520
  2.3 18.3 %collective-permute-start.3 = (f32[4,4,512]{2,1,0:T(4,128)S(1)}, f32[4,4,512]{2,1,0:T(4,128)S(1)}, u32[]{:S(2)}, u32[]{:S(2)}) collective-permute-start(f32[4,4,512]{2,1,0:T(4,128)S(1)} %get-tuple-element.56), channel_id=1, source_target_pairs={{32,33},{33,34},{34,35},{35,36},{36,37},{37,38},{38,39},{39,40},{4... | collective-permute-start | bytes 98312 | tf_op jit(solution)/shard_map/ppermute | solution.py:519
  8.1 3.4 %collective-permute-start.2 = (f32[16,512]{1,0:T(8,128)S(1)}, f32[16,512]{1,0:T(8,128)S(1)}, u32[]{:S(2)}, u32[]{:S(2)}) collective-permute-start(f32[16,512]{1,0:T(8,128)S(1)} %get-tuple-element.57), channel_id=1, source_target_pairs={{0,32},{1,33},{2,34},{3,35},{4,36},{5,37},{6,38},{7,39},{8,40},{9,... | collective-permute-start | bytes 98312 | tf_op jit(solution)/shard_map/ppermute | solution.py:527
  9.4 2.1 %collective-permute-start.1 = (f32[16,512]{1,0:T(8,128)S(1)}, f32[16,512]{1,0:T(8,128)S(1)}, u32[]{:S(2)}, u32[]{:S(2)}) collective-permute-start(f32[16,512]{1,0:T(8,128)S(1)} %get-tuple-element.58), channel_id=1, source_target_pairs={{0,64},{1,65},{2,66},{3,67},{4,68},{5,69},{6,70},{7,71},{8,72},{9,... | collective-permute-start | bytes 98312 | tf_op jit(solution)/shard_map/ppermute | solution.py:527
  10.1 1.5 %collective-permute-start = (f32[16,512]{1,0:T(8,128)S(1)}, f32[16,512]{1,0:T(8,128)S(1)}, u32[]{:S(2)}, u32[]{:S(2)}) collective-permute-start(f32[16,512]{1,0:T(8,128)S(1)} %get-tuple-element.59), channel_id=1, source_target_pairs={{0,96},{1,97},{2,98},{3,99},{4,100},{5,101},{6,102},{7,103},{8,104... | collective-permute-start | bytes 98312 | tf_op jit(solution)/shard_map/ppermute | solution.py:527
  12.3 3.4 %copy-start = (bf16[256,128,128]{2,1,0:T(8,128)(2,1)S(1)}, bf16[256,128,128]{2,1,0:T(8,128)(2,1)}, u32[]{:S(2)}) copy-start(bf16[256,128,128]{2,1,0:T(8,128)(2,1)} %blk.5) | copy-start | bytes 25165828
  15.7 0.7 copy-start.5
  16.4 0.7 copy-start.7
  17.1 31.0 %copy-start.1 = (bf16[256,128,128]{2,1,0:T(8,128)(2,1)S(1)}, bf16[256,128,128]{2,1,0:T(8,128)(2,1)}, u32[]{:S(2)}) copy-start(bf16[256,128,128]{2,1,0:T(8,128)(2,1)} %blk.5) | copy-start | bytes 25165828
  20.7 9.0 %collective-permute-start.5 = (bf16[256,128]{1,0:T(8,128)(2,1)S(1)}, bf16[256,128]{1,0:T(8,128)(2,1)S(1)}, u32[]{:S(2)}, u32[]{:S(2)}) collective-permute-start(bf16[256,128]{1,0:T(8,128)(2,1)S(1)} %project.1), channel_id=1, source_target_pairs={{0,16},{16,0},{1,17},{17,1},{2,18},{18,2},{3,19},{19,3},{4,20},{20... | collective-permute-start | bytes 196616 | tf_op jit(solution)/shard_map/ppermute | solution.py:511
  29.7 6.3 %collective-permute-start.8 = (bf16[256,128]{1,0:T(8,128)(2,1)S(1)}, bf16[256,128]{1,0:T(8,128)(2,1)S(1)}, u32[]{:S(2)}, u32[]{:S(2)}) collective-permute-start(bf16[256,128]{1,0:T(8,128)(2,1)S(1)} %add_convert_fusion.5), channel_id=1, source_target_pairs={{0,12},{4,0},{8,4},{12,8},{1,13},{5,1},{9,5},{13,9},{2,14},{6,2},{... | collective-permute-start | bytes 196616 | tf_op jit(solution)/shard_map/ppermute | solution.py:511
  30.5 5.5 %collective-permute-start.7 = (bf16[256,128]{1,0:T(8,128)(2,1)S(1)}, bf16[256,128]{1,0:T(8,128)(2,1)S(1)}, u32[]{:S(2)}, u32[]{:S(2)}) collective-permute-start(bf16[256,128]{1,0:T(8,128)(2,1)S(1)} %add_convert_fusion.5), channel_id=1, source_target_pairs={{0,8},{4,12},{8,0},{12,4},{1,9},{5,13},{9,1},{13,5},{2,10},{6,14},... | collective-permute-start | bytes 196616 | tf_op jit(solution)/shard_map/ppermute | solution.py:511
  30.5 5.5 %collective-permute-start.6 = (bf16[256,128]{1,0:T(8,128)(2,1)S(1)}, bf16[256,128]{1,0:T(8,128)(2,1)S(1)}, u32[]{:S(2)}, u32[]{:S(2)}) collective-permute-start(bf16[256,128]{1,0:T(8,128)(2,1)S(1)} %add_convert_fusion.5), channel_id=1, source_target_pairs={{0,4},{4,8},{8,12},{12,0},{1,5},{5,9},{9,13},{13,1},{2,6},{6,10},{... | collective-permute-start | bytes 196616 | tf_op jit(solution)/shard_map/ppermute | solution.py:511
  31.2 1.0 %copy-start.4 = (bf16[3,2,3,3,32,32]{5,4,3,2,1,0:T(8,128)(2,1)S(1)}, bf16[3,2,3,3,32,32]{5,4,3,2,1,0:T(8,128)(2,1)}, u32[]{:S(2)}) copy-start(bf16[3,2,3,3,32,32]{5,4,3,2,1,0:T(8,128)(2,1)} %hidden.1) | copy-start | bytes 331780
  36.1 10.3 %collective-permute-start.11 = (bf16[256,128]{1,0:T(8,128)(2,1)S(1)}, bf16[256,128]{1,0:T(8,128)(2,1)S(1)}, u32[]{:S(2)}, u32[]{:S(2)}) collective-permute-start(bf16[256,128]{1,0:T(8,128)(2,1)S(1)} %add_convert_fusion.4), channel_id=1, source_target_pairs={{0,3},{1,0},{2,1},{3,2},{4,7},{5,4},{6,5},{7,6},{8,11},{9,8},{10,9... | collective-permute-start | bytes 196616 | tf_op jit(solution)/shard_map/ppermute | solution.py:511
  43.0 4.7 %collective-permute-start.10 = (bf16[256,128]{1,0:T(8,128)(2,1)S(1)}, bf16[256,128]{1,0:T(8,128)(2,1)S(1)}, u32[]{:S(2)}, u32[]{:S(2)}) collective-permute-start(bf16[256,128]{1,0:T(8,128)(2,1)S(1)} %add_convert_fusion.4), channel_id=1, source_target_pairs={{0,2},{1,3},{2,0},{3,1},{4,6},{5,7},{6,4},{7,5},{8,10},{9,11},{10,... | collective-permute-start | bytes 196616 | tf_op jit(solution)/shard_map/ppermute | solution.py:511
  43.1 5.0 %collective-permute-start.9 = (bf16[256,128]{1,0:T(8,128)(2,1)S(1)}, bf16[256,128]{1,0:T(8,128)(2,1)S(1)}, u32[]{:S(2)}, u32[]{:S(2)}) collective-permute-start(bf16[256,128]{1,0:T(8,128)(2,1)S(1)} %add_convert_fusion.4), channel_id=1, source_target_pairs={{0,1},{1,2},{2,3},{3,0},{4,5},{5,6},{6,7},{7,4},{8,9},{9,10},{10,1... | collective-permute-start | bytes 196616 | tf_op jit(solution)/shard_map/ppermute | solution.py:511
  53.5 4.7 %collective-permute-start.12 = (bf16[256,128]{1,0:T(8,128)(2,1)S(1)}, bf16[256,128]{1,0:T(8,128)(2,1)S(1)}, u32[]{:S(2)}, u32[]{:S(2)}) collective-permute-start(bf16[256,128]{1,0:T(8,128)(2,1)S(1)} %get-tuple-element.48), channel_id=1, source_target_pairs={{0,16},{16,0},{1,17},{17,1},{2,18},{18,2},{3,19},{19,3},{4,20},{20... | collective-permute-start | bytes 196616 | tf_op jit(solution)/shard_map/ppermute | solution.py:511
  58.2 6.4 %collective-permute-start.15 = (bf16[256,128]{1,0:T(8,128)(2,1)S(1)}, bf16[256,128]{1,0:T(8,128)(2,1)S(1)}, u32[]{:S(2)}, u32[]{:S(2)}) collective-permute-start(bf16[256,128]{1,0:T(8,128)(2,1)S(1)} %add_convert_fusion.2), channel_id=1, source_target_pairs={{0,12},{4,0},{8,4},{12,8},{1,13},{5,1},{9,5},{13,9},{2,14},{6,2},{... | collective-permute-start | bytes 196616 | tf_op jit(solution)/shard_map/ppermute | solution.py:511
  60.3 4.6 %collective-permute-start.14 = (bf16[256,128]{1,0:T(8,128)(2,1)S(1)}, bf16[256,128]{1,0:T(8,128)(2,1)S(1)}, u32[]{:S(2)}, u32[]{:S(2)}) collective-permute-start(bf16[256,128]{1,0:T(8,128)(2,1)S(1)} %add_convert_fusion.2), channel_id=1, source_target_pairs={{0,8},{4,12},{8,0},{12,4},{1,9},{5,13},{9,1},{13,5},{2,10},{6,14},... | collective-permute-start | bytes 196616 | tf_op jit(solution)/shard_map/ppermute | solution.py:511
  62.0 4.6 %collective-permute-start.13 = (bf16[256,128]{1,0:T(8,128)(2,1)S(1)}, bf16[256,128]{1,0:T(8,128)(2,1)S(1)}, u32[]{:S(2)}, u32[]{:S(2)}) collective-permute-start(bf16[256,128]{1,0:T(8,128)(2,1)S(1)} %add_convert_fusion.2), channel_id=1, source_target_pairs={{0,4},{4,8},{8,12},{12,0},{1,5},{5,9},{9,13},{13,1},{2,6},{6,10},{... | collective-permute-start | bytes 196616 | tf_op jit(solution)/shard_map/ppermute | solution.py:511
  66.7 4.5 %collective-permute-start.18 = (bf16[256,128]{1,0:T(8,128)(2,1)S(1)}, bf16[256,128]{1,0:T(8,128)(2,1)S(1)}, u32[]{:S(2)}, u32[]{:S(2)}) collective-permute-start(bf16[256,128]{1,0:T(8,128)(2,1)S(1)} %add_convert_fusion.1), channel_id=1, source_target_pairs={{0,3},{1,0},{2,1},{3,2},{4,7},{5,4},{6,5},{7,6},{8,11},{9,8},{10,9... | collective-permute-start | bytes 196616 | tf_op jit(solution)/shard_map/ppermute | solution.py:511
  67.3 4.6 %collective-permute-start.17 = (bf16[256,128]{1,0:T(8,128)(2,1)S(1)}, bf16[256,128]{1,0:T(8,128)(2,1)S(1)}, u32[]{:S(2)}, u32[]{:S(2)}) collective-permute-start(bf16[256,128]{1,0:T(8,128)(2,1)S(1)} %add_convert_fusion.1), channel_id=1, source_target_pairs={{0,2},{1,3},{2,0},{3,1},{4,6},{5,7},{6,4},{7,5},{8,10},{9,11},{10,... | collective-permute-start | bytes 196616 | tf_op jit(solution)/shard_map/ppermute | solution.py:511
  68.6 4.3 %collective-permute-start.16 = (bf16[256,128]{1,0:T(8,128)(2,1)S(1)}, bf16[256,128]{1,0:T(8,128)(2,1)S(1)}, u32[]{:S(2)}, u32[]{:S(2)}) collective-permute-start(bf16[256,128]{1,0:T(8,128)(2,1)S(1)} %add_convert_fusion.1), channel_id=1, source_target_pairs={{0,1},{1,2},{2,3},{3,0},{4,5},{5,6},{6,7},{7,4},{8,9},{9,10},{10,1... | collective-permute-start | bytes 196616 | tf_op jit(solution)/shard_map/ppermute | solution.py:511
  72.9 3.4 %copy-start.2 = (bf16[256,128,128]{2,1,0:T(8,128)(2,1)S(1)}, bf16[256,128,128]{2,1,0:T(8,128)(2,1)}, u32[]{:S(2)}) copy-start(bf16[256,128,128]{2,1,0:T(8,128)(2,1)} %blk.5) | copy-start | bytes 25165828
where the time goes:
time: 98.3 us; the launch traced here: 97.7 us
  starting transfers between devices  31.2 us (32%)
  Pallas kernels  22.7 us (23%)
  blocking collectives  18.2 us (19%)
  waiting for transfers between devices  11.7 us (12%)
  local copies, waits for them, and re-layouts  11 us (11%)
  other arithmetic  2.58 us (3%)
    ppermute x14, starting transfers between devices, added_up(): total = total + lax.ppermute(values, 'tile', swapped(groups, k)).astype(F32)  22.3 us
    all_gather x1, blocking collectives, per_device(): everything = lax.all_gather(sent, 'agent').astype(F32)  18.2 us
    ppermute x14, waiting for transfers between devices, added_up(): total = total + lax.ppermute(values, 'tile', swapped(groups, k)).astype(F32)  11.7 us
    pallas_call x4, Pallas kernels, piece(): pl.pallas_call(functools.partial(piece_kernel, k), out_shape=jax.ShapeDty...  10.4 us
    unnamed x22, local copies, waits for them, and re-layouts  9.18 us
    pallas_call x1, Pallas kernels, back_project(): pl.pallas_call(back_project_kernel, out_shape=(jax.ShapeDtypeStruct(x.sha...  5.31 us
    ppermute x1, starting transfers between devices, rims(): before = lax.ppermute(cells[:, cells.shape[1] - depth:], both, pairs)  5 us
    pallas_call x1, Pallas kernels, project(): pl.pallas_call(project_kernel, out_shape=jax.ShapeDtypeStruct((ray_total,...  3.52 us
  transfers between devices with their start and end apart: 19, of which 8 were waited for; matrix products, arithmetic and copies ran while one was open for 2% of the time, Pallas kernels for 15%

commit v1 on v0

--- a/solution.py
+++ b/solution.py
@@ -24,6 +24,10 @@
     return pl.BlockSpec(memory_space=pltpu.VMEM)
 
 
+def near(x):
+    return pltpu.with_memory_space_constraint(x, pltpu.VMEM)
+
+
 def in_smem():
     return pl.BlockSpec(memory_space=pltpu.SMEM)
 
@@ -47,11 +51,13 @@
     acc[index] = acc[index] + value
 
 
-def project_blocks(ray_ref, tile_ref, pix, blk, acc):
+def project_blocks(ray_of, tile_ref, pix, blk, acc, ready=None):
     low = low_rows()
     zero = jnp.zeros((8, 128), F32)
 
     def body(i, carry):
+        if ready is not None:
+            ready(i)
         outs = []
         for u in range(UNROLL):
             b = (i * UNROLL + u) * TOGETHER
@@ -67,10 +73,10 @@
         for u in range(UNROLL):
             b = (i * UNROLL + u) * TOGETHER
             out = outs[u]
-            add_rows(acc, ray_ref[b], jnp.where(low, out[0:8, 0:128], 0.0))
-            add_rows(acc, ray_ref[b + 1], jnp.where(low, 0.0, out[0:8, 128:256]))
-            add_rows(acc, ray_ref[b + 2], jnp.where(low, out[8:16, 0:128], 0.0))
-            add_rows(acc, ray_ref[b + 3], jnp.where(low, 0.0, out[8:16, 128:256]))
+            add_rows(acc, ray_of(b), jnp.where(low, out[0:8, 0:128], 0.0))
+            add_rows(acc, ray_of(b + 1), jnp.where(low, 0.0, out[0:8, 128:256]))
+            add_rows(acc, ray_of(b + 2), jnp.where(low, out[8:16, 0:128], 0.0))
+            add_rows(acc, ray_of(b + 3), jnp.where(low, 0.0, out[8:16, 128:256]))
         return carry
 
     lax.fori_loop(0, blk.shape[0] // (TOGETHER * UNROLL), body, 0)
@@ -134,28 +140,113 @@
     o_ref[...] = total[0 : acc.shape[0]].astype(o_ref.dtype)
 
 
-def project_kernel(place_ref, ray_ref, tile_ref, x_ref, sino_ref, blk, o_ref, pix, acc, total):
-    load_pixels(x_ref[...], pix)
+def project_kernel(
+    place_ref,
+    angle_in,
+    detector_in,
+    tile_in,
+    states_in,
+    got_1,
+    got_2,
+    got_3,
+    sino_in,
+    blk_in,
+    o_ref,
+    start_ref,
+    blk,
+    angle,
+    detector,
+    tile,
+    first_slice,
+    sino,
+    pix,
+    acc,
+    total,
+    small_sems,
+    block_sems,
+):
+    small = [
+        pltpu.make_async_copy(source, target, small_sems.at[n])
+        for n, (source, target) in enumerate(
+            [
+                (states_in.at[0, 0], first_slice),
+                (angle_in, angle),
+                (detector_in, detector),
+                (tile_in, tile),
+                (sino_in, sino),
+            ]
+        )
+    ]
+    for copy in small:
+        copy.start()
+    chunk = TOGETHER * UNROLL
+
+    def chunk_copy(i):
+        part = pl.ds(i * chunk, chunk)
+        return pltpu.make_async_copy(blk_in.at[part], blk.at[part], block_sems.at[i])
+
+    for i in range(blk.shape[0] // chunk):
+        chunk_copy(i).start()
     acc[...] = jnp.zeros_like(acc)
-    project_blocks(ray_ref, tile_ref, pix, blk, acc)
-    store_rays(place_ref, sino_ref, acc, total, o_ref)
-
-
-def project(place, ray_index, tile_index, x, sinogram, blocks, ray_total):
-    tiles = x.size // 128
+    for copy in small:
+        copy.wait()
+    start_ref[...] = got_1[...] + got_2[...] + got_3[...]
+
+    @pl.when(place_ref[0] == 0)
+    def _():
+        start_ref[...] = first_slice[...]
+
+    load_pixels(start_ref[...], pix)
+    wide = first_slice.shape[1] // 128
+    project_blocks(
+        lambda b: angle[b] * wide + detector[b],
+        tile,
+        pix,
+        blk,
+        acc,
+        lambda i: chunk_copy(i).wait(),
+    )
+    store_rays(place_ref, sino, acc, total, o_ref)
+
+
+def project(place, angle, detector, tile, states, got, sinogram, blocks, ray_total):
+    shape = got[0].shape
+    count = blocks.shape[0]
+    far = pl.BlockSpec(memory_space=pltpu.HBM)
+    stay = lambda x: pltpu.with_memory_space_constraint(x, pltpu.HBM)
     return pl.pallas_call(
         project_kernel,
-        out_shape=jax.ShapeDtypeStruct((ray_total, 128), BF16),
-        in_specs=[in_smem()] * 3 + [in_vmem()] * 3,
-        out_specs=in_vmem(),
+        out_shape=(
+            jax.ShapeDtypeStruct((ray_total, 128), BF16),
+            jax.ShapeDtypeStruct(shape, F32),
+            pltpu.VMEM(blocks.shape, BF16),
+        ),
+        in_specs=[in_smem()] + [far] * 4 + [in_vmem()] * 3 + [far] * 2,
+        out_specs=(in_vmem(),) * 3,
         scratch_shapes=[
-            pltpu.VMEM((tiles + 8, 128), F32),
+            pltpu.SMEM((count,), jnp.int32),
+            pltpu.SMEM((count,), jnp.int32),
+            pltpu.SMEM((count,), jnp.int32),
+            pltpu.VMEM(shape, F32),
+            pltpu.VMEM(sinogram.shape, F32),
+            pltpu.VMEM((shape[0] * shape[1] // 128 + 8, 128), F32),
             pltpu.VMEM((ray_total, 8, 128), F32),
             pltpu.VMEM((ray_total + 8, 128), F32),
+            pltpu.SemaphoreType.DMA((5,)),
+            pltpu.SemaphoreType.DMA((count // (TOGETHER * UNROLL),)),
         ],
         compiler_params=params(),
         name="project",
-    )(place, ray_index, tile_index, x, sinogram, blocks)
+    )(
+        place,
+        stay(angle),
+        stay(detector),
+        stay(tile),
+        stay(states),
+        *got,
+        stay(sinogram),
+        stay(blocks),
+    )
 
 
 def back_project_kernel(
@@ -168,7 +259,7 @@
     x_out[...] = moved
     load_pixels(moved, pix)
     acc[...] = jnp.zeros_like(acc)
-    project_blocks(ray_ref, tile_ref, pix, blk, acc)
+    project_blocks(lambda b: ray_ref[b], tile_ref, pix, blk, acc)
     store_rays(place_ref, sino_ref, acc, res, o_ref)
 
 
@@ -191,23 +282,25 @@
         ],
         compiler_params=params(),
         name="back_project",
-    )(place, ray_index, tile_index, residual, x, sinogram, blocks)
-
-
-def back_kernel(ray_ref, tile_ref, r_ref, x_ref, start_ref, blk, o_ref, res, back):
+    )(place, ray_index, tile_index, residual, x, sinogram, near(blocks))
+
+
+def back_kernel(ray_ref, tile_ref, r_ref, x_ref, start_ref, cur_ref, net_ref, blk, o_ref, res, back):
     res[0 : r_ref.shape[0]] = r_ref[...].astype(F32)
     back[...] = jnp.zeros_like(back)
+    for z in range(net_ref.shape[0]):
+        o_ref[z + 1] = (cur_ref[z] - 2.0 * net_ref[z]).astype(o_ref.dtype)
     back_blocks(ray_ref, tile_ref, res, blk, back)
-    o_ref[...] = 2.0 * moved_by(x_ref[...], back) - start_ref[...]
-
-
-def back_reflect(ray_index, tile_index, residual, x, start, blocks):
+    o_ref[0] = (2.0 * moved_by(x_ref[...], back) - start_ref[...]).astype(o_ref.dtype)
+
+
+def back_reflect(ray_index, tile_index, residual, x, start, current, net, blocks):
     ray_total = residual.shape[0]
     tiles = x.size // 128
     return pl.pallas_call(
         back_kernel,
-        out_shape=jax.ShapeDtypeStruct(x.shape, F32),
-        in_specs=[in_smem()] * 2 + [in_vmem()] * 4,
+        out_shape=jax.ShapeDtypeStruct((1 + net.shape[0], *x.shape), BF16),
+        in_specs=[in_smem()] * 2 + [in_vmem()] * 6,
         out_specs=in_vmem(),
         scratch_shapes=[
             pltpu.VMEM((ray_total + 8, 128), F32),
@@ -215,7 +308,34 @@
         ],
         compiler_params=params(),
         name="back_reflect",
-    )(ray_index, tile_index, residual, x, start, blocks)
+    )(ray_index, tile_index, residual, x, start, current, net, near(blocks))
+
+
+def finish_kernel(place_ref, all_ref, cur_ref, net_ref, o_ref):
+    for z in range(o_ref.shape[0]):
+        data = all_ref[z, 0].astype(F32)
+        total = data
+        for k in range(1, all_ref.shape[0]):
+            total = total + all_ref[k, 1 + z].astype(F32)
+
+        @pl.when(place_ref[0] == 0)
+        def _():
+            o_ref[z] = 0.25 * total + 0.5 * (cur_ref[z] - data)
+
+        @pl.when(place_ref[0] != 0)
+        def _():
+            o_ref[z] = 0.25 * total + net_ref[z]
+
+
+def finish(place, everything, current, net):
+    return pl.pallas_call(
+        finish_kernel,
+        out_shape=jax.ShapeDtypeStruct(current.shape, F32),
+        in_specs=[in_smem()] + [in_vmem()] * 3,
+        out_specs=in_vmem(),
+        compiler_params=params(),
+        name="finish",
+    )(place, everything, current, net)
 
 
 def lanes(parts, count, height, width):
@@ -312,10 +432,11 @@
         slice_band(first, hidden, last, 2, zf, zh, zl, turn)
 
 
-def prepare(place, before, current, after, first, hidden, last):
+def prepare(place, rim, current, first, hidden, last):
+    before, after = rim
     layers = hidden.shape[1]
     slices, rows, columns = current.shape
-    rim = jax.ShapeDtypeStruct((slices, rows + 2 * before.shape[1], columns), F32)
+    whole = jax.ShapeDtypeStruct((slices, rows + 2 * before.shape[1], columns), F32)
     shapes = [
         (128, 16),
         (layers, 128, 384),
@@ -328,7 +449,7 @@
     ]
     return pl.pallas_call(
         prepare_kernel,
-        out_shape=[rim] + [jax.ShapeDtypeStruct(s, BF16) for s in shapes],
+        out_shape=[whole] + [jax.ShapeDtypeStruct(s, BF16) for s in shapes],
         in_specs=[in_smem()] + [in_vmem()] * 6,
         out_specs=[in_vmem()] * 9,
         scratch_shapes=[pltpu.VMEM((256, 256), F32)],
@@ -450,7 +571,7 @@
 
 
 def piece_kernel(
-    k, place_ref, net, rim, zf, zh, zl, zw, zm, af, ah, al, o_ref, sa, sb, ca, xa, xb
+    k, place_ref, blk, net, rim, zf, zh, zl, zw, zm, af, ah, al, o_ref, sa, sb, ca, xa, xb
 ):
     rows = o_ref.shape[1]
     depth = (rim.shape[1] - rows) // 2
@@ -473,20 +594,20 @@
         coronal_piece(k * (rows // 4), rows // 4, depth, rim, zf, zh, zl, o_ref, ca)
 
 
-def piece(k, place, net, prepared):
+def piece(k, place, blocks, net, prepared):
     slices, rows, columns = net.shape
     reach = rows + 6
     return pl.pallas_call(
         functools.partial(piece_kernel, k),
         out_shape=jax.ShapeDtypeStruct(net.shape, F32),
-        in_specs=[in_smem()] + [in_vmem()] * (1 + len(prepared)),
+        in_specs=[in_smem()] + [in_vmem()] * (2 + len(prepared)),
         out_specs=in_vmem(),
         scratch_shapes=[pltpu.VMEM((reach * 128, columns // 2), BF16)] * 2
         + [pltpu.VMEM((rows // 4, 384, columns), BF16)]
         + [pltpu.VMEM((3, reach * 32, columns), BF16)] * 2,
         compiler_params=params(),
         name=f"piece_{k}",
-    )(place, net, *prepared)
+    )(place, near(blocks), net, *prepared)
 
 
 def swapped(groups, k):
@@ -521,12 +642,8 @@
     return before, after
 
 
-def own_slice(current, agent_place):
-    start = current[0]
-    for k in range(1, current.shape[0]):
-        got = lax.ppermute(current[k], "agent", [(0, k)])
-        start = jnp.where(agent_place == k, got, start)
-    return start
+def slices_sent(current):
+    return [lax.ppermute(current[k], "agent", [(0, k)]) for k in range(1, current.shape[0])]
 
 
 def per_device(
@@ -548,35 +665,34 @@
     ray_total = sinogram.shape[0] * tile_count
     ray_index = block_angle * (current.shape[2] // 128) + block_detector
 
-    start = own_slice(current, agent_place)
-    before, after = rims(current, conv_hidden.shape[1] + 2)
-    sums = project(place, ray_index, block_tile, start, sinogram, blocks, ray_total)
+    got = slices_sent(current)
+    sums, start, blocks_here = project(
+        place, block_angle, block_detector, block_tile, states, got, sinogram, blocks, ray_total
+    )
 
     groups = stage_groups(tile_count)
     net = jnp.zeros_like(current)
     x_data = start
-    prepared = None
-    k = 0
+    prepared, rim, k = None, None, 0
     for step in range(DATA_STEPS):
         for n, group in enumerate(groups):
-            tied = lax.optimization_barrier((sums, net, before, after))
-            sums, net, before, after = tied
+            sums, net = lax.optimization_barrier((sums, net))
             if n == 0 and step == 0:
-                prepared = prepare(place, before, current, after, conv_first, conv_hidden, conv_last)
+                around, sums = lax.optimization_barrier((current, sums))
+                rim = rims(around, conv_hidden.shape[1] + 2)
             elif n > 0:
-                net = piece(k, place, net, prepared)
+                if prepared is None:
+                    prepared = prepare(place, rim, current, conv_first, conv_hidden, conv_last)
+                net = piece(k, place, blocks_here, net, prepared)
                 k += 1
             sums = added_up(sums, group)
         if step < DATA_STEPS - 1:
-            x_data, sums = back_project(place, ray_index, block_tile, sums, x_data, sinogram, blocks)
-    reflect_data = back_reflect(ray_index, block_tile, sums, x_data, start, blocks)
-
-    sent = jnp.concatenate([reflect_data[None], current - 2.0 * net], axis=0).astype(BF16)
-    everything = lax.all_gather(sent, "agent").astype(F32)
-    reflect_data = everything[:, 0]
-    average = (reflect_data + everything[1, 1:] + everything[2, 1:] + everything[3, 1:]) / 4.0
-    own = jnp.where(agent_place == 0, 0.5 * (current - reflect_data), net)
-    return (average + own)[None]
+            x_data, sums = back_project(
+                place, ray_index, block_tile, sums, x_data, sinogram, blocks_here
+            )
+    sent = back_reflect(ray_index, block_tile, sums, x_data, start, current, net, blocks_here)
+    everything = lax.all_gather(sent, "agent")
+    return finish(place, everything, current, net)[None]
 
 
 def solution(mesh):

time: 98.3 us -> 92.3 us (0.939)
  local copies, waits for them, and re-layouts: 11 us -> 0.92 us
  Pallas kernels: 22.7 us -> 26.8 us
  blocking collectives: 18.2 us -> 14.7 us
  starting transfers between devices: 31.2 us -> 34.5 us
  waiting for transfers between devices: 11.7 us -> 14.2 us
  other arithmetic: 2.58 us -> 0.29 us
    unnamed x22 -> x16, local copies, waits for them, and re-layouts: 9.18 us -> 0.04 us
    ppermute x3, waiting for transfers between devices: 0.01 us -> 4.89 us  [slices_sent(): lax.ppermute(current[k], 'agent', [(0, k)])]
    ppermute x14, starting transfers between devices: 22.3 us -> 26.4 us  [added_up(): total = total + lax.ppermute(values, 'tile', swapped(groups, k)).astype(F32)]
    pallas_call x3 -> x4, Pallas kernels: 7.08 us -> 10.9 us  [the longest x1 6.12 us: project(): pl.pallas_call(project_kernel, out_shape=(jax.ShapeDtypeStruct((ray_total...]
    all_gather x1, blocking collectives: 18.2 us -> 14.7 us  [per_device(): everything = lax.all_gather(sent, 'agent')]
    ppermute x14, waiting for transfers between devices: 11.7 us -> 8.31 us  [added_up(): total = total + lax.ppermute(values, 'tile', swapped(groups, k)).astype(F32)]
    ppermute x1, waiting for transfers between devices: 0.01 us -> 0.99 us  [rims(): before = lax.ppermute(cells[:, cells.shape[1] - depth:], both, pairs)]
  transfers between devices with their start and end apart: 19 -> 19, of which waited for: 8 -> 10; matrix products, arithmetic and copies ran while one was open for 2% -> 0% of each run, Pallas kernels for 15% -> 13%
where the time goes in v1:
time: 92.3 us; the launch traced here: 91.6 us
  starting transfers between devices  34.5 us (37%)
  Pallas kernels  26.8 us (29%)
  blocking collectives  14.7 us (16%)
  waiting for transfers between devices  14.2 us (15%)
    ppermute x14, starting transfers between devices, added_up(): total = total + lax.ppermute(values, 'tile', swapped(groups, k)).astype(F32)  26.4 us
    all_gather x1, blocking collectives, per_device(): everything = lax.all_gather(sent, 'agent')  14.7 us
    pallas_call x4, Pallas kernels, piece(): pl.pallas_call(functools.partial(piece_kernel, k), out_shape=jax.ShapeDty...  10.6 us
    ppermute x14, waiting for transfers between devices, added_up(): total = total + lax.ppermute(values, 'tile', swapped(groups, k)).astype(F32)  8.31 us
    pallas_call x1, Pallas kernels, project(): pl.pallas_call(project_kernel, out_shape=(jax.ShapeDtypeStruct((ray_total...  6.12 us
    pallas_call x1, Pallas kernels, back_project(): pl.pallas_call(back_project_kernel, out_shape=(jax.ShapeDtypeStruct(x.sha...  5.29 us
    ppermute x3, waiting for transfers between devices, slices_sent(): lax.ppermute(current[k], 'agent', [(0, k)])  4.89 us
    ppermute x1, starting transfers between devices, rims(): before = lax.ppermute(cells[:, cells.shape[1] - depth:], both, pairs)  4.17 us
  transfers between devices with their start and end apart: 19, of which 10 were waited for; matrix products, arithmetic and copies ran while one was open for 0% of the time, Pallas kernels for 13%

profile of v1, /device:TPU:1, one launch (start us, length us, event | category | flops | bytes accessed | tf_op | source)
XLA Modules:
  0.0 91.6 jit_solution(4690164249640122899)
XLA Ops:
  0.0 0.0 copy-start
  0.0 0.0 copy-start.4
  0.0 0.0 copy-start.1
  0.0 0.0 copy-start.3
  0.0 0.9 slice_bitcast_fusion
  0.9 0.7 collective-permute-start.2
  1.5 0.7 collective-permute-start.1
  2.2 1.3 %collective-permute-start = (f32[16,512]{1,0:T(8,128)S(1)}, f32[16,512]{1,0:T(8,128)S(1)}, u32[]{:S(2)}, u32[]{:S(2)}) collective-permute-start(f32[16,512]{1,0:T(8,128)S(1)} %get-tuple-element.65), channel_id=1, source_target_pairs={{0,32},{1,33},{2,34},{3,35},{4,36},{5,37},{6,38},{7,39},{8,40},{9,... | collective-permute-start | bytes 98312 | tf_op jit(solution)/shard_map/ppermute | solution.py:646
  3.5 0.1 pad_add_fusion.place_ref
  3.6 0.0 collective-permute-done.2.got_3
  3.6 0.0 collective-permute-done.1.got_2
  3.6 4.9 %collective-permute-done.got_1 = f32[16,512]{1,0:T(8,128)S(1)} collective-permute-done((f32[16,512]{1,0:T(8,128)S(1)}, f32[16,512]{1,0:T(8,128)S(1)}, u32[]{:S(2)}, u32[]{:S(2)}) %collective-permute-start) | collective-permute-done | bytes 32800 | tf_op jit(solution)/shard_map/ppermute | solution.py:646
  8.5 6.1 %project.1 = (bf16[256,128]{1,0:T(8,128)(2,1)S(1)}, f32[16,512]{1,0:T(8,128)S(1)}, bf16[256,128,128]{2,1,0:T(8,128)(2,1)S(1)}) custom-call(s32[3]{0:T(128)S(1)} %pad_add_fusion.place_ref, s32[256]{0:T(256)} %angle_in.1, s32[256]{0:T(256)} %detector_in.1, s32[256]{0:T(256)} %tile_ref.3, f32[1,4,16,512]{3,2,1,0:T(8,128)} %states_in.1, ...), custom_call_target="tpu_custom_call" | custom-call | tf_op jit(solution)/shard_map/project/pallas_call | solution.py:217
  14.6 2.5 %collective-permute-start.3 = (bf16[256,128]{1,0:T(8,128)(2,1)S(1)}, bf16[256,128]{1,0:T(8,128)(2,1)S(1)}, u32[]{:S(2)}, u32[]{:S(2)}) collective-permute-start(bf16[256,128]{1,0:T(8,128)(2,1)S(1)} %get-tuple-element.35), channel_id=1, source_target_pairs={{0,16},{16,0},{1,17},{17,1},{2,18},{18,2},{3,19},{19,3},{4,20},{20... | collective-permute-start | bytes 196616 | tf_op jit(solution)/shard_map/ppermute | solution.py:632
  17.2 2.6 %collective-permute-done.3 = bf16[256,128]{1,0:T(8,128)(2,1)S(1)} collective-permute-done((bf16[256,128]{1,0:T(8,128)(2,1)S(1)}, bf16[256,128]{1,0:T(8,128)(2,1)S(1)}, u32[]{:S(2)}, u32[]{:S(2)}) %collective-permute-start.3) | collective-permute-done | bytes 65568 | tf_op jit(solution)/shard_map/ppermute | solution.py:632
  19.8 2.8 %collective-permute-start.6 = (bf16[256,128]{1,0:T(8,128)(2,1)S(1)}, bf16[256,128]{1,0:T(8,128)(2,1)S(1)}, u32[]{:S(2)}, u32[]{:S(2)}) collective-permute-start(bf16[256,128]{1,0:T(8,128)(2,1)S(1)} %add_convert_fusion.5), channel_id=1, source_target_pairs={{0,12},{4,0},{8,4},{12,8},{1,13},{5,1},{9,5},{13,9},{2,14},{6,2},{... | collective-permute-start | bytes 196616 | tf_op jit(solution)/shard_map/ppermute | solution.py:632
  22.6 0.4 collective-permute-start.5
  22.9 0.7 collective-permute-start.4
  23.6 0.0 copy-done
  23.6 1.3 %collective-permute-start.8 = (f32[4,4,512]{2,1,0:T(4,128)S(1)}, f32[4,4,512]{2,1,0:T(4,128)S(1)}, u32[]{:S(2)}, u32[]{:S(2)}) collective-permute-start(f32[4,4,512]{2,1,0:T(4,128)S(1)} %get-tuple-element.61), channel_id=1, source_target_pairs={{33,32},{34,33},{35,34},{36,35},{37,36},{38,37},{39,38},{40,39},{4... | collective-permute-start | bytes 98312 | tf_op jit(solution)/shard_map/ppermute | solution.py:641
  24.9 4.2 %collective-permute-start.7 = (f32[4,4,512]{2,1,0:T(4,128)S(1)}, f32[4,4,512]{2,1,0:T(4,128)S(1)}, u32[]{:S(2)}, u32[]{:S(2)}) collective-permute-start(f32[4,4,512]{2,1,0:T(4,128)S(1)} %get-tuple-element.62), channel_id=1, source_target_pairs={{32,33},{33,34},{34,35},{35,36},{36,37},{37,38},{38,39},{39,40},{4... | collective-permute-start | bytes 98312 | tf_op jit(solution)/shard_map/ppermute | solution.py:640
  29.1 0.0 collective-permute-done.8.after
  29.1 1.0 %collective-permute-done.7.before = f32[4,4,512]{2,1,0:T(4,128)S(1)} collective-permute-done((f32[4,4,512]{2,1,0:T(4,128)S(1)}, f32[4,4,512]{2,1,0:T(4,128)S(1)}, u32[]{:S(2)}, u32[]{:S(2)}) %collective-permute-start.7) | collective-permute-done | bytes 32800 | tf_op jit(solution)/shard_map/ppermute | solution.py:640
  30.1 0.0 copy-done.4
  30.1 0.0 copy-done.1
  30.1 0.0 copy-done.3
  30.1 1.1 %prepare.1 = (f32[4,24,512]{2,1,0:T(8,128)S(1)}, bf16[128,16]{1,0:T(8,128)(2,1)S(1)}, bf16[2,128,384]{2,1,0:T(8,128)(2,1)S(1)}, bf16[8,384]{1,0:T(8,128)(2,1)S(1...) custom-call(s32[3]{0:T(128)S(1)} %pad_add_fusion.place_ref, ...), custom_call_target="tpu_custom_call" | custom-call | tf_op jit(solution)/shard_map/prepare/pallas_call | solution.py:450
  31.3 0.0 copy-start.2
  31.3 0.0 copy-start.5
  31.3 2.6 %piece_0.1.net = f32[4,16,512]{2,1,0:T(8,128)S(1)} custom-call(s32[3]{0:T(128)S(1)} %pad_add_fusion.place_ref, bf16[256,128,128]{2,1,0:T(8,128)(2,1)S(1)} %get-tuple-element.38.blk, f32[4,16,512]{2,1,0:T(8,128)S(1)} %broadcast_in_dim.6.net, f32[4,24,512]{2,1,0:T(8,128)S(1)} %get-tuple-element.41.rim, bf16[128,16]{1,0:T(8,128)(2,1)S(1)} %get-tuple-element.42.zf, ...), custom_call_target="tpu_custom_call" | custom-call | tf_op jit(solution)/shard_map/piece_0/pallas_call | solution.py:600
  33.9 0.0 collective-permute-done.6
  33.9 0.0 collective-permute-done.5
  34.0 0.0 collective-permute-done.4
  34.0 5.8 %collective-permute-start.11 = (bf16[256,128]{1,0:T(8,128)(2,1)S(1)}, bf16[256,128]{1,0:T(8,128)(2,1)S(1)}, u32[]{:S(2)}, u32[]{:S(2)}) collective-permute-start(bf16[256,128]{1,0:T(8,128)(2,1)S(1)} %add_convert_fusion.4), channel_id=1, source_target_pairs={{0,3},{1,0},{2,1},{3,2},{4,7},{5,4},{6,5},{7,6},{8,11},{9,8},{10,9... | collective-permute-start | bytes 196616 | tf_op jit(solution)/shard_map/ppermute | solution.py:632
  39.8 0.0 collective-permute-start.10
  39.8 0.7 collective-permute-start.9
  40.4 0.0 copy-done.6
  40.4 0.0 copy-done.7
  40.5 2.7 %piece_1.1.net = f32[4,16,512]{2,1,0:T(8,128)S(1)} custom-call(s32[3]{0:T(128)S(1)} %pad_add_fusion.place_ref, bf16[256,128,128]{2,1,0:T(8,128)(2,1)S(1)} %get-tuple-element.38.blk, f32[4,16,512]{2,1,0:T(8,128)S(1)} %piece_0.1.net, f32[4,24,512]{2,1,0:T(8,128)S(1)} %get-tuple-element.41.rim, bf16[128,16]{1,0:T(8,128)(2,1)S(1)} %get-tuple-element.42.zf, ...), custom_call_target="tpu_custom_call" | custom-call | tf_op jit(solution)/shard_map/piece_1/pallas_call | solution.py:600
  43.2 0.0 collective-permute-done.11
  43.2 1.3 %collective-permute-done.10 = bf16[256,128]{1,0:T(8,128)(2,1)S(1)} collective-permute-done((bf16[256,128]{1,0:T(8,128)(2,1)S(1)}, bf16[256,128]{1,0:T(8,128)(2,1)S(1)}, u32[]{:S(2)}, u32[]{:S(2)}) %collective-permute-start.10) | collective-permute-done | bytes 65568 | tf_op jit(solution)/shard_map/ppermute | solution.py:632
  44.5 0.3 collective-permute-done.9
  44.8 0.0 copy-done.2
  44.9 0.0 copy-done.5
  44.9 5.3 %back_project.1 = (f32[16,512]{1,0:T(8,128)S(1)}, bf16[256,128]{1,0:T(8,128)(2,1)S(1)}) custom-call(s32[3]{0:T(128)S(1)} %pad_add_fusion.place_ref, s32[256]{0:T(256)S(1)} %multiply_add_fusion.ray_ref, s32[256]{0:T(256)S(1)} %copy-done.5, bf16[256,128]{1,0:T(8,128)(2,1)S(1)} %add_convert_fusion.3.r_ref, f32[16,512]{1,0:T(8,128)S(1)} %get-tuple-element.51.x_ref.start_ref, ...), custom_call_target="tpu_custom_call" | custom-call | tf_op jit(solution)/shard_map/back_project/pallas_call | solution.py:269
  50.2 9.0 %collective-permute-start.12 = (bf16[256,128]{1,0:T(8,128)(2,1)S(1)}, bf16[256,128]{1,0:T(8,128)(2,1)S(1)}, u32[]{:S(2)}, u32[]{:S(2)}) collective-permute-start(bf16[256,128]{1,0:T(8,128)(2,1)S(1)} %get-tuple-element.54), channel_id=1, source_target_pairs={{0,16},{16,0},{1,17},{17,1},{2,18},{18,2},{3,19},{19,3},{4,20},{20... | collective-permute-start | bytes 196616 | tf_op jit(solution)/shard_map/ppermute | solution.py:632
  59.2 1.7 %collective-permute-done.12 = bf16[256,128]{1,0:T(8,128)(2,1)S(1)} collective-permute-done((bf16[256,128]{1,0:T(8,128)(2,1)S(1)}, bf16[256,128]{1,0:T(8,128)(2,1)S(1)}, u32[]{:S(2)}, u32[]{:S(2)}) %collective-permute-start.12) | collective-permute-done | bytes 65568 | tf_op jit(solution)/shard_map/ppermute | solution.py:632
  60.8 0.1 collective-permute-start.15
  60.9 0.1 collective-permute-start.14
  61.0 1.4 %collective-permute-start.13 = (bf16[256,128]{1,0:T(8,128)(2,1)S(1)}, bf16[256,128]{1,0:T(8,128)(2,1)S(1)}, u32[]{:S(2)}, u32[]{:S(2)}) collective-permute-start(bf16[256,128]{1,0:T(8,128)(2,1)S(1)} %add_convert_fusion.2), channel_id=1, source_target_pairs={{0,4},{4,8},{8,12},{12,0},{1,5},{5,9},{9,13},{13,1},{2,6},{6,10},{... | collective-permute-start | bytes 196616 | tf_op jit(solution)/shard_map/ppermute | solution.py:632
  62.4 2.6 %piece_2.1.net = f32[4,16,512]{2,1,0:T(8,128)S(1)} custom-call(s32[3]{0:T(128)S(1)} %pad_add_fusion.place_ref, bf16[256,128,128]{2,1,0:T(8,128)(2,1)S(1)} %get-tuple-element.38.blk, f32[4,16,512]{2,1,0:T(8,128)S(1)} %piece_1.1.net, f32[4,24,512]{2,1,0:T(8,128)S(1)} %get-tuple-element.41.rim, bf16[128,16]{1,0:T(8,128)(2,1)S(1)} %get-tuple-element.42.zf, ...), custom_call_target="tpu_custom_call" | custom-call | tf_op jit(solution)/shard_map/piece_2/pallas_call | solution.py:600
  65.0 0.0 collective-permute-done.15
  65.0 0.6 collective-permute-done.14
  65.6 0.8 collective-permute-done.13
  66.5 1.4 %collective-permute-start.18 = (bf16[256,128]{1,0:T(8,128)(2,1)S(1)}, bf16[256,128]{1,0:T(8,128)(2,1)S(1)}, u32[]{:S(2)}, u32[]{:S(2)}) collective-permute-start(bf16[256,128]{1,0:T(8,128)(2,1)S(1)} %add_convert_fusion.1), channel_id=1, source_target_pairs={{0,3},{1,0},{2,1},{3,2},{4,7},{5,4},{6,5},{7,6},{8,11},{9,8},{10,9... | collective-permute-start | bytes 196616 | tf_op jit(solution)/shard_map/ppermute | solution.py:632
  67.8 0.9 %collective-permute-start.17 = (bf16[256,128]{1,0:T(8,128)(2,1)S(1)}, bf16[256,128]{1,0:T(8,128)(2,1)S(1)}, u32[]{:S(2)}, u32[]{:S(2)}) collective-permute-start(bf16[256,128]{1,0:T(8,128)(2,1)S(1)} %add_convert_fusion.1), channel_id=1, source_target_pairs={{0,2},{1,3},{2,0},{3,1},{4,6},{5,7},{6,4},{7,5},{8,10},{9,11},{10,... | collective-permute-start | bytes 196616 | tf_op jit(solution)/shard_map/ppermute | solution.py:632
  68.8 0.8 collective-permute-start.16
  69.5 2.6 %piece_3.1.net_ref = f32[4,16,512]{2,1,0:T(8,128)S(1)} custom-call(s32[3]{0:T(128)S(1)} %pad_add_fusion.place_ref, bf16[256,128,128]{2,1,0:T(8,128)(2,1)S(1)} %get-tuple-element.38.blk, f32[4,16,512]{2,1,0:T(8,128)S(1)} %piece_2.1.net, f32[4,24,512]{2,1,0:T(8,128)S(1)} %get-tuple-element.41.rim, bf16[128,16]{1,0:T(8,128)(2,1)S(1)} %get-tuple-element.42.zf, ...), custom_call_target="tpu_custom_call" | custom-call | tf_op jit(solution)/shard_map/piece_3/pallas_call | solution.py:600
  72.2 0.0 collective-permute-done.18
  72.2 0.3 collective-permute-done.17
  72.5 0.7 collective-permute-done.16
  73.2 2.4 %back_reflect.1 = bf16[5,16,512]{2,1,0:T(8,128)(2,1)S(1)} custom-call(s32[256]{0:T(256)S(1)} %multiply_add_fusion.ray_ref, s32[256]{0:T(256)S(1)} %copy-done.5, bf16[256,128]{1,0:T(8,128)(2,1)S(1)} %add_convert_fusion.r_ref, f32[16,512]{1,0:T(8,128)S(1)} %get-tuple-element.59.x_ref, f32[16,512]{1,0:T(8,128)S(1)} %get-tuple-element.51.x_ref.start_ref, ...), custom_call_target="tpu_custom_call" | custom-call | tf_op jit(solution)/shard_map/back_reflect/pallas_call | solution.py:300
  75.6 14.7 %all-gather = bf16[20,16,512]{2,1,0:T(8,128)(2,1)S(1)} all-gather(bf16[5,16,512]{2,1,0:T(8,128)(2,1)S(1)} %back_reflect.1), channel_id=2, replica_groups=mesh['agent'=4,'tile'=32] {'agent'}, dimensions={0}, use_global_device_ids=true | all-gather | bytes 409600 | tf_op jit(solution)/shard_map/all_gather | solution.py:694
  90.4 1.3 %finish.1 = f32[4,16,512]{2,1,0:T(8,128)} custom-call(s32[3]{0:T(128)S(1)} %pad_add_fusion.place_ref, bf16[4,5,16,512]{3,2,1,0:T(8,128)(2,1)S(1)} %bitcast.15, f32[4,16,512]{2,1,0:T(8,128)S(1)} %bitcast.14, f32[4,16,512]{2,1,0:T(8,128)S(1)} %piece_3.1.net_ref), custom_call_target="tpu_custom_call" | custom-call | tf_op jit(solution)/shard_map/finish/pallas_call | solution.py:331
  (11 shorter events, 0.2 us)
Async XLA Ops:
  0.0 23.6 %copy-start = (f32[1,4,16,512]{3,2,1,0:T(8,128)S(1)}, f32[1,4,16,512]{3,2,1,0:T(8,128)}, u32[]{:S(2)}) copy-start(f32[1,4,16,512]{3,2,1,0:T(8,128)} %states_in.1) | copy-start | bytes 393220
  0.0 30.1 %copy-start.4 = (bf16[3,3,3,32]{3,2,1,0:T(4,128)(2,1)S(1)}, bf16[3,3,3,32]{3,2,1,0:T(4,128)(2,1)}, u32[]{:S(2)}) copy-start(bf16[3,3,3,32]{3,2,1,0:T(4,128)(2,1)} %last.1) | copy-start | bytes 5188
  0.0 30.1 %copy-start.1 = (bf16[3,2,3,3,32,32]{5,4,3,2,1,0:T(8,128)(2,1)S(1)}, bf16[3,2,3,3,32,32]{5,4,3,2,1,0:T(8,128)(2,1)}, u32[]{:S(2)}) copy-start(bf16[3,2,3,3,32,32]{5,4,3,2,1,0:T(8,128)(2,1)} %hidden.1) | copy-start | bytes 331780
  0.0 30.1 %copy-start.3 = (bf16[3,3,3,32]{3,2,1,0:T(4,128)(2,1)S(1)}, bf16[3,3,3,32]{3,2,1,0:T(4,128)(2,1)}, u32[]{:S(2)}) copy-start(bf16[3,3,3,32]{3,2,1,0:T(4,128)(2,1)} %first.1) | copy-start | bytes 5188
  0.9 2.7 %collective-permute-start.2 = (f32[16,512]{1,0:T(8,128)S(1)}, f32[16,512]{1,0:T(8,128)S(1)}, u32[]{:S(2)}, u32[]{:S(2)}) collective-permute-start(f32[16,512]{1,0:T(8,128)S(1)} %get-tuple-element.63), channel_id=1, source_target_pairs={{0,96},{1,97},{2,98},{3,99},{4,100},{5,101},{6,102},{7,103},{8,104... | collective-permute-start | bytes 98312 | tf_op jit(solution)/shard_map/ppermute | solution.py:646
  1.5 2.1 %collective-permute-start.1 = (f32[16,512]{1,0:T(8,128)S(1)}, f32[16,512]{1,0:T(8,128)S(1)}, u32[]{:S(2)}, u32[]{:S(2)}) collective-permute-start(f32[16,512]{1,0:T(8,128)S(1)} %get-tuple-element.64), channel_id=1, source_target_pairs={{0,64},{1,65},{2,66},{3,67},{4,68},{5,69},{6,70},{7,71},{8,72},{9,... | collective-permute-start | bytes 98312 | tf_op jit(solution)/shard_map/ppermute | solution.py:646
  2.2 6.3 %collective-permute-start = (f32[16,512]{1,0:T(8,128)S(1)}, f32[16,512]{1,0:T(8,128)S(1)}, u32[]{:S(2)}, u32[]{:S(2)}) collective-permute-start(f32[16,512]{1,0:T(8,128)S(1)} %get-tuple-element.65), channel_id=1, source_target_pairs={{0,32},{1,33},{2,34},{3,35},{4,36},{5,37},{6,38},{7,39},{8,40},{9,... | collective-permute-start | bytes 98312 | tf_op jit(solution)/shard_map/ppermute | solution.py:646
  3.6 36.9 %copy-start.6 = (s32[256]{0:T(256)S(1)}, s32[256]{0:T(256)}, u32[]{:S(2)}) copy-start(s32[256]{0:T(256)} %detector_in.1) | copy-start | bytes 3076
  3.6 36.9 %copy-start.7 = (s32[256]{0:T(256)S(1)}, s32[256]{0:T(256)}, u32[]{:S(2)}) copy-start(s32[256]{0:T(256)} %angle_in.1) | copy-start | bytes 3076
  14.6 5.1 %collective-permute-start.3 = (bf16[256,128]{1,0:T(8,128)(2,1)S(1)}, bf16[256,128]{1,0:T(8,128)(2,1)S(1)}, u32[]{:S(2)}, u32[]{:S(2)}) collective-permute-start(bf16[256,128]{1,0:T(8,128)(2,1)S(1)} %get-tuple-element.35), channel_id=1, source_target_pairs={{0,16},{16,0},{1,17},{17,1},{2,18},{18,2},{3,19},{19,3},{4,20},{20... | collective-permute-start | bytes 196616 | tf_op jit(solution)/shard_map/ppermute | solution.py:632
  19.8 14.2 %collective-permute-start.6 = (bf16[256,128]{1,0:T(8,128)(2,1)S(1)}, bf16[256,128]{1,0:T(8,128)(2,1)S(1)}, u32[]{:S(2)}, u32[]{:S(2)}) collective-permute-start(bf16[256,128]{1,0:T(8,128)(2,1)S(1)} %add_convert_fusion.5), channel_id=1, source_target_pairs={{0,12},{4,0},{8,4},{12,8},{1,13},{5,1},{9,5},{13,9},{2,14},{6,2},{... | collective-permute-start | bytes 196616 | tf_op jit(solution)/shard_map/ppermute | solution.py:632
  22.6 11.4 %collective-permute-start.5 = (bf16[256,128]{1,0:T(8,128)(2,1)S(1)}, bf16[256,128]{1,0:T(8,128)(2,1)S(1)}, u32[]{:S(2)}, u32[]{:S(2)}) collective-permute-start(bf16[256,128]{1,0:T(8,128)(2,1)S(1)} %add_convert_fusion.5), channel_id=1, source_target_pairs={{0,8},{4,12},{8,0},{12,4},{1,9},{5,13},{9,1},{13,5},{2,10},{6,14},... | collective-permute-start | bytes 196616 | tf_op jit(solution)/shard_map/ppermute | solution.py:632
  22.9 11.0 %collective-permute-start.4 = (bf16[256,128]{1,0:T(8,128)(2,1)S(1)}, bf16[256,128]{1,0:T(8,128)(2,1)S(1)}, u32[]{:S(2)}, u32[]{:S(2)}) collective-permute-start(bf16[256,128]{1,0:T(8,128)(2,1)S(1)} %add_convert_fusion.5), channel_id=1, source_target_pairs={{0,4},{4,8},{8,12},{12,0},{1,5},{5,9},{9,13},{13,1},{2,6},{6,10},{... | collective-permute-start | bytes 196616 | tf_op jit(solution)/shard_map/ppermute | solution.py:632
  23.6 5.5 %collective-permute-start.8 = (f32[4,4,512]{2,1,0:T(4,128)S(1)}, f32[4,4,512]{2,1,0:T(4,128)S(1)}, u32[]{:S(2)}, u32[]{:S(2)}) collective-permute-start(f32[4,4,512]{2,1,0:T(4,128)S(1)} %get-tuple-element.61), channel_id=1, source_target_pairs={{33,32},{34,33},{35,34},{36,35},{37,36},{38,37},{39,38},{40,39},{4... | collective-permute-start | bytes 98312 | tf_op jit(solution)/shard_map/ppermute | solution.py:641
  24.9 5.2 %collective-permute-start.7 = (f32[4,4,512]{2,1,0:T(4,128)S(1)}, f32[4,4,512]{2,1,0:T(4,128)S(1)}, u32[]{:S(2)}, u32[]{:S(2)}) collective-permute-start(f32[4,4,512]{2,1,0:T(4,128)S(1)} %get-tuple-element.62), channel_id=1, source_target_pairs={{32,33},{33,34},{34,35},{35,36},{36,37},{37,38},{38,39},{39,40},{4... | collective-permute-start | bytes 98312 | tf_op jit(solution)/shard_map/ppermute | solution.py:640
  31.3 13.6 %copy-start.2 = (f32[8,4,128]{2,1,0:T(4,128)S(1)}, f32[8,4,128]{2,1,0:T(4,128)}, u32[]{:S(2)}) copy-start(f32[8,4,128]{2,1,0:T(4,128)} %sino_ref.1) | copy-start | bytes 49156
  31.3 13.6 %copy-start.5 = (s32[256]{0:T(256)S(1)}, s32[256]{0:T(256)}, u32[]{:S(2)}) copy-start(s32[256]{0:T(256)} %tile_ref.3) | copy-start | bytes 3076
  34.0 9.2 %collective-permute-start.11 = (bf16[256,128]{1,0:T(8,128)(2,1)S(1)}, bf16[256,128]{1,0:T(8,128)(2,1)S(1)}, u32[]{:S(2)}, u32[]{:S(2)}) collective-permute-start(bf16[256,128]{1,0:T(8,128)(2,1)S(1)} %add_convert_fusion.4), channel_id=1, source_target_pairs={{0,3},{1,0},{2,1},{3,2},{4,7},{5,4},{6,5},{7,6},{8,11},{9,8},{10,9... | collective-permute-start | bytes 196616 | tf_op jit(solution)/shard_map/ppermute | solution.py:632
  39.8 4.7 %collective-permute-start.10 = (bf16[256,128]{1,0:T(8,128)(2,1)S(1)}, bf16[256,128]{1,0:T(8,128)(2,1)S(1)}, u32[]{:S(2)}, u32[]{:S(2)}) collective-permute-start(bf16[256,128]{1,0:T(8,128)(2,1)S(1)} %add_convert_fusion.4), channel_id=1, source_target_pairs={{0,2},{1,3},{2,0},{3,1},{4,6},{5,7},{6,4},{7,5},{8,10},{9,11},{10,... | collective-permute-start | bytes 196616 | tf_op jit(solution)/shard_map/ppermute | solution.py:632
  39.8 5.0 %collective-permute-start.9 = (bf16[256,128]{1,0:T(8,128)(2,1)S(1)}, bf16[256,128]{1,0:T(8,128)(2,1)S(1)}, u32[]{:S(2)}, u32[]{:S(2)}) collective-permute-start(bf16[256,128]{1,0:T(8,128)(2,1)S(1)} %add_convert_fusion.4), channel_id=1, source_target_pairs={{0,1},{1,2},{2,3},{3,0},{4,5},{5,6},{6,7},{7,4},{8,9},{9,10},{10,1... | collective-permute-start | bytes 196616 | tf_op jit(solution)/shard_map/ppermute | solution.py:632
  50.2 10.6 %collective-permute-start.12 = (bf16[256,128]{1,0:T(8,128)(2,1)S(1)}, bf16[256,128]{1,0:T(8,128)(2,1)S(1)}, u32[]{:S(2)}, u32[]{:S(2)}) collective-permute-start(bf16[256,128]{1,0:T(8,128)(2,1)S(1)} %get-tuple-element.54), channel_id=1, source_target_pairs={{0,16},{16,0},{1,17},{17,1},{2,18},{18,2},{3,19},{19,3},{4,20},{20... | collective-permute-start | bytes 196616 | tf_op jit(solution)/shard_map/ppermute | solution.py:632
  60.8 4.2 %collective-permute-start.15 = (bf16[256,128]{1,0:T(8,128)(2,1)S(1)}, bf16[256,128]{1,0:T(8,128)(2,1)S(1)}, u32[]{:S(2)}, u32[]{:S(2)}) collective-permute-start(bf16[256,128]{1,0:T(8,128)(2,1)S(1)} %add_convert_fusion.2), channel_id=1, source_target_pairs={{0,12},{4,0},{8,4},{12,8},{1,13},{5,1},{9,5},{13,9},{2,14},{6,2},{... | collective-permute-start | bytes 196616 | tf_op jit(solution)/shard_map/ppermute | solution.py:632
  60.9 4.7 %collective-permute-start.14 = (bf16[256,128]{1,0:T(8,128)(2,1)S(1)}, bf16[256,128]{1,0:T(8,128)(2,1)S(1)}, u32[]{:S(2)}, u32[]{:S(2)}) collective-permute-start(bf16[256,128]{1,0:T(8,128)(2,1)S(1)} %add_convert_fusion.2), channel_id=1, source_target_pairs={{0,8},{4,12},{8,0},{12,4},{1,9},{5,13},{9,1},{13,5},{2,10},{6,14},... | collective-permute-start | bytes 196616 | tf_op jit(solution)/shard_map/ppermute | solution.py:632
  61.0 5.4 %collective-permute-start.13 = (bf16[256,128]{1,0:T(8,128)(2,1)S(1)}, bf16[256,128]{1,0:T(8,128)(2,1)S(1)}, u32[]{:S(2)}, u32[]{:S(2)}) collective-permute-start(bf16[256,128]{1,0:T(8,128)(2,1)S(1)} %add_convert_fusion.2), channel_id=1, source_target_pairs={{0,4},{4,8},{8,12},{12,0},{1,5},{5,9},{9,13},{13,1},{2,6},{6,10},{... | collective-permute-start | bytes 196616 | tf_op jit(solution)/shard_map/ppermute | solution.py:632
  66.5 5.7 %collective-permute-start.18 = (bf16[256,128]{1,0:T(8,128)(2,1)S(1)}, bf16[256,128]{1,0:T(8,128)(2,1)S(1)}, u32[]{:S(2)}, u32[]{:S(2)}) collective-permute-start(bf16[256,128]{1,0:T(8,128)(2,1)S(1)} %add_convert_fusion.1), channel_id=1, source_target_pairs={{0,3},{1,0},{2,1},{3,2},{4,7},{5,4},{6,5},{7,6},{8,11},{9,8},{10,9... | collective-permute-start | bytes 196616 | tf_op jit(solution)/shard_map/ppermute | solution.py:632
  67.8 4.6 %collective-permute-start.17 = (bf16[256,128]{1,0:T(8,128)(2,1)S(1)}, bf16[256,128]{1,0:T(8,128)(2,1)S(1)}, u32[]{:S(2)}, u32[]{:S(2)}) collective-permute-start(bf16[256,128]{1,0:T(8,128)(2,1)S(1)} %add_convert_fusion.1), channel_id=1, source_target_pairs={{0,2},{1,3},{2,0},{3,1},{4,6},{5,7},{6,4},{7,5},{8,10},{9,11},{10,... | collective-permute-start | bytes 196616 | tf_op jit(solution)/shard_map/ppermute | solution.py:632
  68.8 4.4 %collective-permute-start.16 = (bf16[256,128]{1,0:T(8,128)(2,1)S(1)}, bf16[256,128]{1,0:T(8,128)(2,1)S(1)}, u32[]{:S(2)}, u32[]{:S(2)}) collective-permute-start(bf16[256,128]{1,0:T(8,128)(2,1)S(1)} %add_convert_fusion.1), channel_id=1, source_target_pairs={{0,1},{1,2},{2,3},{3,0},{4,5},{5,6},{6,7},{7,4},{8,9},{9,10},{10,1... | collective-permute-start | bytes 196616 | tf_op jit(solution)/shard_map/ppermute | solution.py:632

commit v2 on v1

--- a/solution.py
+++ b/solution.py
@@ -13,6 +13,7 @@
 VMEM_LIMIT = 32 << 20
 TOGETHER = 4
 UNROLL = 16
+CHUNK = 64
 SPAN = 6
 
 
@@ -179,22 +180,32 @@
     ]
     for copy in small:
         copy.start()
-    chunk = TOGETHER * UNROLL
+    chunk = CHUNK
 
     def chunk_copy(i):
         part = pl.ds(i * chunk, chunk)
         return pltpu.make_async_copy(blk_in.at[part], blk.at[part], block_sems.at[i])
 
-    for i in range(blk.shape[0] // chunk):
+    ahead = 2
+    count = blk.shape[0] // chunk
+    for i in range(ahead):
         chunk_copy(i).start()
+
+    def ready(i):
+        chunk_copy(i).wait()
+
+        @pl.when(i + ahead < count)
+        def _():
+            chunk_copy(i + ahead).start()
+
     acc[...] = jnp.zeros_like(acc)
     for copy in small:
         copy.wait()
-    start_ref[...] = got_1[...] + got_2[...] + got_3[...]
-
-    @pl.when(place_ref[0] == 0)
-    def _():
-        start_ref[...] = first_slice[...]
+    for k, value in enumerate((first_slice, got_1, got_2, got_3)):
+
+        @pl.when(place_ref[0] == k)
+        def _():
+            start_ref[...] = value[...]
 
     load_pixels(start_ref[...], pix)
     wide = first_slice.shape[1] // 128
@@ -204,7 +215,7 @@
         pix,
         blk,
         acc,
-        lambda i: chunk_copy(i).wait(),
+        ready,
     )
     store_rays(place_ref, sino, acc, total, o_ref)
 
@@ -233,7 +244,7 @@
             pltpu.VMEM((ray_total, 8, 128), F32),
             pltpu.VMEM((ray_total + 8, 128), F32),
             pltpu.SemaphoreType.DMA((5,)),
-            pltpu.SemaphoreType.DMA((count // (TOGETHER * UNROLL),)),
+            pltpu.SemaphoreType.DMA((count // CHUNK,)),
         ],
         compiler_params=params(),
         name="project",
@@ -410,13 +421,25 @@
 
 
 def prepare_kernel(
-    place_ref, before, cur, after, first, hidden, last, rim, zf, zh, zl, zw, zm, af, ah, al, turn
+    place_ref, got_1, got_2, got_3, cur, first, hidden, last, rim, zf, zh, zl, zw, zm, af, ah, al, turn
 ):
-    depth = before.shape[1]
-    rows = cur.shape[1]
-    rim[:, 0:depth] = before[...].astype(BF16).astype(F32)
+    slices, rows = cur.shape[0:2]
+    depth = got_3.shape[0] // slices
     rim[:, depth : depth + rows] = cur[...].astype(BF16).astype(F32)
-    rim[:, depth + rows :] = after[...].astype(BF16).astype(F32)
+
+    def rims(before, after):
+        for z in range(slices):
+            part = slice(z * depth, z * depth + depth)
+            rim[z, 0:depth] = before[part].astype(BF16).astype(F32)
+            rim[z, depth + rows :] = after[part].astype(BF16).astype(F32)
+
+    @pl.when(place_ref[0] == 1)
+    def _():
+        rims(got_2, got_3)
+
+    @pl.when(place_ref[0] == 2)
+    def _():
+        rims(got_1, got_3)
 
     @pl.when(place_ref[0] == 1)
     def _():
@@ -432,11 +455,11 @@
         slice_band(first, hidden, last, 2, zf, zh, zl, turn)
 
 
-def prepare(place, rim, current, first, hidden, last):
-    before, after = rim
+def prepare(place, got, current, first, hidden, last):
     layers = hidden.shape[1]
     slices, rows, columns = current.shape
-    whole = jax.ShapeDtypeStruct((slices, rows + 2 * before.shape[1], columns), F32)
+    depth = got[0].shape[0] // slices
+    whole = jax.ShapeDtypeStruct((slices, rows + 2 * depth, columns), F32)
     shapes = [
         (128, 16),
         (layers, 128, 384),
@@ -450,12 +473,12 @@
     return pl.pallas_call(
         prepare_kernel,
         out_shape=[whole] + [jax.ShapeDtypeStruct(s, BF16) for s in shapes],
-        in_specs=[in_smem()] + [in_vmem()] * 6,
+        in_specs=[in_smem()] + [in_vmem()] * 7,
         out_specs=[in_vmem()] * 9,
         scratch_shapes=[pltpu.VMEM((256, 256), F32)],
         compiler_params=params(),
         name="prepare",
-    )(place, before, current, after, first, hidden, last)
+    )(place, *got, current, first, hidden, last)
 
 
 def side_by_side(value):
@@ -633,17 +656,31 @@
     return total.astype(values.dtype)
 
 
-def rims(cells, depth):
-    agents, count = 4, lax.axis_size("tile")
-    pairs = [(a * count + t, a * count + t + 1) for a in (1, 2) for t in range(count - 1)]
+def first_transfers(current, agent_place, depth):
+    count = lax.axis_size("tile")
+    rows = current.shape[1]
+    head = jnp.concatenate([part[0:depth] for part in current], axis=0)
+    tail = jnp.concatenate([part[rows - depth :] for part in current], axis=0)
+
+    def slices_to(k):
+        return [(t, k * count + t) for t in range(count)]
+
+    def onward(a):
+        return [(a * count + t, a * count + t + 1) for t in range(count - 1)]
+
+    def backward(a):
+        return [(b, a) for a, b in onward(a)]
+
+    is_data = agent_place == 0
     both = ("agent", "tile")
-    before = lax.ppermute(cells[:, cells.shape[1] - depth :], both, pairs)
-    after = lax.ppermute(cells[:, 0:depth], both, [(b, a) for a, b in pairs])
-    return before, after
-
-
-def slices_sent(current):
-    return [lax.ppermute(current[k], "agent", [(0, k)]) for k in range(1, current.shape[0])]
+    got = []
+    for k, rim, pairs in (
+        (1, tail, onward(2)),
+        (2, tail, onward(1)),
+        (3, head, backward(1) + backward(2)),
+    ):
+        got.append(lax.ppermute(jnp.where(is_data, current[k], rim), both, slices_to(k) + pairs))
+    return got
 
 
 def per_device(
@@ -665,7 +702,7 @@
     ray_total = sinogram.shape[0] * tile_count
     ray_index = block_angle * (current.shape[2] // 128) + block_detector
 
-    got = slices_sent(current)
+    got = first_transfers(current, agent_place, conv_hidden.shape[1] + 2)
     sums, start, blocks_here = project(
         place, block_angle, block_detector, block_tile, states, got, sinogram, blocks, ray_total
     )
@@ -673,16 +710,13 @@
     groups = stage_groups(tile_count)
     net = jnp.zeros_like(current)
     x_data = start
-    prepared, rim, k = None, None, 0
+    prepared, k = None, 0
     for step in range(DATA_STEPS):
         for n, group in enumerate(groups):
             sums, net = lax.optimization_barrier((sums, net))
             if n == 0 and step == 0:
-                around, sums = lax.optimization_barrier((current, sums))
-                rim = rims(around, conv_hidden.shape[1] + 2)
+                prepared = prepare(place, got, current, conv_first, conv_hidden, conv_last)
             elif n > 0:
-                if prepared is None:
-                    prepared = prepare(place, rim, current, conv_first, conv_hidden, conv_last)
                 net = piece(k, place, blocks_here, net, prepared)
                 k += 1
             sums = added_up(sums, group)

time: 92.3 us -> 87 us (0.943)
  starting transfers between devices: 34.5 us -> 28.5 us
  waiting for transfers between devices: 14.2 us -> 16.5 us
  blocking collectives: 14.7 us -> 13.4 us
    ppermute x14, starting transfers between devices: 26.4 us -> 21.5 us  [added_up(): total = total + lax.ppermute(values, 'tile', swapped(groups, k)).astype(F32)]
    ppermute x14, waiting for transfers between devices: 8.31 us -> 13.1 us  [added_up(): total = total + lax.ppermute(values, 'tile', swapped(groups, k)).astype(F32)]
    ppermute x5 -> x3, waiting for transfers between devices: 5.88 us -> 3.46 us  [first_transfers(): lax.ppermute(jnp.where(is_data, current[k], rim), both, slices_to(k) + pa...]
    all_gather x1, blocking collectives: 14.7 us -> 13.4 us  [per_device(): everything = lax.all_gather(sent, 'agent')]
    ppermute x5 -> x3, starting transfers between devices: 8.07 us -> 6.96 us  [first_transfers(): lax.ppermute(jnp.where(is_data, current[k], rim), both, slices_to(k) + pa...]
  transfers between devices with their start and end apart: 19 -> 17, of which waited for: 10 -> 12; matrix products, arithmetic and copies ran while one was open for 0% -> 0% of each run, Pallas kernels for 13% -> 14%
where the time goes in v2:
time: 87 us; the launch traced here: 86.8 us
  starting transfers between devices  28.5 us (33%)
  Pallas kernels  26.2 us (30%)
  waiting for transfers between devices  16.5 us (19%)
  blocking collectives  13.4 us (15%)
  other arithmetic  1.1 us (1%)
  local copies, waits for them, and re-layouts  0.92 us (1%)
    ppermute x14, starting transfers between devices, added_up(): total = total + lax.ppermute(values, 'tile', swapped(groups, k)).astype(F32)  21.5 us
    all_gather x1, blocking collectives, per_device(): everything = lax.all_gather(sent, 'agent')  13.4 us
    ppermute x14, waiting for transfers between devices, added_up(): total = total + lax.ppermute(values, 'tile', swapped(groups, k)).astype(F32)  13.1 us
    pallas_call x4, Pallas kernels, piece(): pl.pallas_call(functools.partial(piece_kernel, k), out_shape=jax.ShapeDty...  10.6 us
    ppermute x3, starting transfers between devices, first_transfers(): lax.ppermute(jnp.where(is_data, current[k], rim), both, slices_to(k) + pa...  6.96 us
    pallas_call x1, Pallas kernels, project(): pl.pallas_call(project_kernel, out_shape=(jax.ShapeDtypeStruct((ray_total...  5.49 us
    pallas_call x1, Pallas kernels, back_project(): pl.pallas_call(back_project_kernel, out_shape=(jax.ShapeDtypeStruct(x.sha...  5.29 us
    ppermute x3, waiting for transfers between devices, first_transfers(): lax.ppermute(jnp.where(is_data, current[k], rim), both, slices_to(k) + pa...  3.46 us
  transfers between devices with their start and end apart: 17, of which 12 were waited for; matrix products, arithmetic and copies ran while one was open for 0% of the time, Pallas kernels for 14%

profile of v2, /device:TPU:1, one launch (start us, length us, event | category | flops | bytes accessed | tf_op | source)
XLA Modules:
  0.0 86.8 jit_solution(13113733606004437134)
XLA Ops:
  0.0 0.0 copy-start
  0.0 0.0 copy-start.4
  0.0 0.0 copy-start.1
  0.0 0.0 copy-start.3
  0.0 0.9 %slice_bitcast_fusion.3 = (f32[4,512]{1,0:T(4,128)S(1)}, f32[4,512]{1,0:T(4,128)S(1)}, f32[4,512]{1,0:T(4,128)S(1)}, f32[4,512]{1,0:T(4,128)S(1)}, f32[4,512]{1,...) fusion(f32[1,4,16,512]{3,2,1,0:T(8,128)} %states_in.1), kind=kLoop, calls=%fused_computation.13 | loop fusion | bytes 131072 | tf_op jit(solution)/shard_map/slice | solution.py:662
  0.9 0.8 bitcast_select_fusion
  1.7 4.4 %collective-permute-start.1 = (f32[16,512]{1,0:T(8,128)S(1)}, f32[16,512]{1,0:T(8,128)S(1)}, u32[]{:S(2)}, u32[]{:S(2)}) collective-permute-start(f32[16,512]{1,0:T(8,128)S(1)} %get-tuple-element.57), channel_id=1, source_target_pairs={{0,64},{1,65},{2,66},{3,67},{4,68},{5,69},{6,70},{7,71},{8,72},{9,... | collective-permute-start | bytes 98312 | tf_op jit(solution)/shard_map/ppermute | solution.py:682
  6.1 1.3 %collective-permute-start = (f32[16,512]{1,0:T(8,128)S(1)}, f32[16,512]{1,0:T(8,128)S(1)}, u32[]{:S(2)}, u32[]{:S(2)}) collective-permute-start(f32[16,512]{1,0:T(8,128)S(1)} %get-tuple-element.58), channel_id=1, source_target_pairs={{0,32},{1,33},{2,34},{3,35},{4,36},{5,37},{6,38},{7,39},{8,40},{9,... | collective-permute-start | bytes 98312 | tf_op jit(solution)/shard_map/ppermute | solution.py:682
  7.4 1.3 %collective-permute-start.2 = (f32[16,512]{1,0:T(8,128)S(1)}, f32[16,512]{1,0:T(8,128)S(1)}, u32[]{:S(2)}, u32[]{:S(2)}) collective-permute-start(f32[16,512]{1,0:T(8,128)S(1)} %get-tuple-element.59), channel_id=1, source_target_pairs={{0,96},{1,97},{2,98},{3,99},{4,100},{5,101},{6,102},{7,103},{8,104... | collective-permute-start | bytes 98312 | tf_op jit(solution)/shard_map/ppermute | solution.py:682
  8.7 0.1 pad_add_fusion.place_ref
  8.8 0.0 copy-start.6
  8.8 0.0 copy-start.7
  8.8 0.0 collective-permute-done.1.got_2
  8.8 0.4 collective-permute-done.got_1
  9.2 3.0 %collective-permute-done.2.got_3 = f32[16,512]{1,0:T(8,128)S(1)} collective-permute-done((f32[16,512]{1,0:T(8,128)S(1)}, f32[16,512]{1,0:T(8,128)S(1)}, u32[]{:S(2)}, u32[]{:S(2)}) %collective-permute-start.2) | collective-permute-done | bytes 32800 | tf_op jit(solution)/shard_map/ppermute | solution.py:682
  12.3 5.5 %project.1 = (bf16[256,128]{1,0:T(8,128)(2,1)S(1)}, f32[16,512]{1,0:T(8,128)S(1)}, bf16[256,128,128]{2,1,0:T(8,128)(2,1)S(1)}) custom-call(s32[3]{0:T(128)S(1)} %pad_add_fusion.place_ref, s32[256]{0:T(256)} %angle_in.1, s32[256]{0:T(256)} %detector_in.1, s32[256]{0:T(256)} %tile_ref.3, f32[1,4,16,512]{3,2,1,0:T(8,128)} %states_in.1, ...), custom_call_target="tpu_custom_call" | custom-call | tf_op jit(solution)/shard_map/project/pallas_call | solution.py:228
  17.8 6.5 %collective-permute-start.3 = (bf16[256,128]{1,0:T(8,128)(2,1)S(1)}, bf16[256,128]{1,0:T(8,128)(2,1)S(1)}, u32[]{:S(2)}, u32[]{:S(2)}) collective-permute-start(bf16[256,128]{1,0:T(8,128)(2,1)S(1)} %get-tuple-element.32), channel_id=1, source_target_pairs={{0,16},{16,0},{1,17},{17,1},{2,18},{18,2},{3,19},{19,3},{4,20},{20... | collective-permute-start | bytes 196616 | tf_op jit(solution)/shard_map/ppermute | solution.py:655
  24.2 1.7 %collective-permute-done.3 = bf16[256,128]{1,0:T(8,128)(2,1)S(1)} collective-permute-done((bf16[256,128]{1,0:T(8,128)(2,1)S(1)}, bf16[256,128]{1,0:T(8,128)(2,1)S(1)}, u32[]{:S(2)}, u32[]{:S(2)}) %collective-permute-start.3) | collective-permute-done | bytes 65568 | tf_op jit(solution)/shard_map/ppermute | solution.py:655
  25.9 0.1 collective-permute-start.6
  26.0 0.1 collective-permute-start.5
  26.1 1.4 %collective-permute-start.4 = (bf16[256,128]{1,0:T(8,128)(2,1)S(1)}, bf16[256,128]{1,0:T(8,128)(2,1)S(1)}, u32[]{:S(2)}, u32[]{:S(2)}) collective-permute-start(bf16[256,128]{1,0:T(8,128)(2,1)S(1)} %add_convert_fusion.5), channel_id=1, source_target_pairs={{0,4},{4,8},{8,12},{12,0},{1,5},{5,9},{9,13},{13,1},{2,6},{6,10},{... | collective-permute-start | bytes 196616 | tf_op jit(solution)/shard_map/ppermute | solution.py:655
  27.4 0.0 copy-done
  27.4 0.0 copy-done.4
  27.4 0.0 copy-done.1
  27.4 0.0 copy-done.3
  27.4 1.2 %prepare.1 = (f32[4,24,512]{2,1,0:T(8,128)S(1)}, bf16[128,16]{1,0:T(8,128)(2,1)S(1)}, bf16[2,128,384]{2,1,0:T(8,128)(2,1)S(1)}, bf16[8,384]{1,0:T(8,128)(2,1)S(1...) custom-call(s32[3]{0:T(128)S(1)} %pad_add_fusion.place_ref, ...), custom_call_target="tpu_custom_call" | custom-call | tf_op jit(solution)/shard_map/prepare/pallas_call | solution.py:473
  28.6 0.0 copy-start.2
  28.6 0.0 copy-start.5
  28.7 2.6 %piece_0.1.net = f32[4,16,512]{2,1,0:T(8,128)S(1)} custom-call(s32[3]{0:T(128)S(1)} %pad_add_fusion.place_ref, bf16[256,128,128]{2,1,0:T(8,128)(2,1)S(1)} %get-tuple-element.35.blk, f32[4,16,512]{2,1,0:T(8,128)S(1)} %broadcast_in_dim.6.net, f32[4,24,512]{2,1,0:T(8,128)S(1)} %get-tuple-element.37.rim, bf16[128,16]{1,0:T(8,128)(2,1)S(1)} %get-tuple-element.38.zf, ...), custom_call_target="tpu_custom_call" | custom-call | tf_op jit(solution)/shard_map/piece_0/pallas_call | solution.py:623
  31.3 0.0 collective-permute-done.6
  31.3 0.1 collective-permute-done.5
  31.4 1.7 %collective-permute-done.4 = bf16[256,128]{1,0:T(8,128)(2,1)S(1)} collective-permute-done((bf16[256,128]{1,0:T(8,128)(2,1)S(1)}, bf16[256,128]{1,0:T(8,128)(2,1)S(1)}, u32[]{:S(2)}, u32[]{:S(2)}) %collective-permute-start.4) | collective-permute-done | bytes 65568 | tf_op jit(solution)/shard_map/ppermute | solution.py:655
  33.1 6.3 %collective-permute-start.9 = (bf16[256,128]{1,0:T(8,128)(2,1)S(1)}, bf16[256,128]{1,0:T(8,128)(2,1)S(1)}, u32[]{:S(2)}, u32[]{:S(2)}) collective-permute-start(bf16[256,128]{1,0:T(8,128)(2,1)S(1)} %add_convert_fusion.4), channel_id=1, source_target_pairs={{0,3},{1,0},{2,1},{3,2},{4,7},{5,4},{6,5},{7,6},{8,11},{9,8},{10,9... | collective-permute-start | bytes 196616 | tf_op jit(solution)/shard_map/ppermute | solution.py:655
  39.4 0.0 collective-permute-start.8
  39.4 0.7 collective-permute-start.7
  40.1 0.0 copy-done.6
  40.1 0.0 copy-done.7
  40.1 2.7 %piece_1.1.net = f32[4,16,512]{2,1,0:T(8,128)S(1)} custom-call(s32[3]{0:T(128)S(1)} %pad_add_fusion.place_ref, bf16[256,128,128]{2,1,0:T(8,128)(2,1)S(1)} %get-tuple-element.35.blk, f32[4,16,512]{2,1,0:T(8,128)S(1)} %piece_0.1.net, f32[4,24,512]{2,1,0:T(8,128)S(1)} %get-tuple-element.37.rim, bf16[128,16]{1,0:T(8,128)(2,1)S(1)} %get-tuple-element.38.zf, ...), custom_call_target="tpu_custom_call" | custom-call | tf_op jit(solution)/shard_map/piece_1/pallas_call | solution.py:623
  42.8 0.0 collective-permute-done.9
  42.8 1.3 %collective-permute-done.8 = bf16[256,128]{1,0:T(8,128)(2,1)S(1)} collective-permute-done((bf16[256,128]{1,0:T(8,128)(2,1)S(1)}, bf16[256,128]{1,0:T(8,128)(2,1)S(1)}, u32[]{:S(2)}, u32[]{:S(2)}) %collective-permute-start.8) | collective-permute-done | bytes 65568 | tf_op jit(solution)/shard_map/ppermute | solution.py:655
  44.2 0.3 collective-permute-done.7
  44.5 0.0 copy-done.2
  44.5 0.0 copy-done.5
  44.5 5.3 %back_project.1 = (f32[16,512]{1,0:T(8,128)S(1)}, bf16[256,128]{1,0:T(8,128)(2,1)S(1)}) custom-call(s32[3]{0:T(128)S(1)} %pad_add_fusion.place_ref, s32[256]{0:T(256)S(1)} %multiply_add_fusion.ray_ref, s32[256]{0:T(256)S(1)} %copy-done.5, bf16[256,128]{1,0:T(8,128)(2,1)S(1)} %add_convert_fusion.3.r_ref, f32[16,512]{1,0:T(8,128)S(1)} %get-tuple-element.47.x_ref.start_ref, ...), custom_call_target="tpu_custom_call" | custom-call | tf_op jit(solution)/shard_map/back_project/pallas_call | solution.py:280
  49.8 1.3 %collective-permute-start.10 = (bf16[256,128]{1,0:T(8,128)(2,1)S(1)}, bf16[256,128]{1,0:T(8,128)(2,1)S(1)}, u32[]{:S(2)}, u32[]{:S(2)}) collective-permute-start(bf16[256,128]{1,0:T(8,128)(2,1)S(1)} %get-tuple-element.50), channel_id=1, source_target_pairs={{0,16},{16,0},{1,17},{17,1},{2,18},{18,2},{3,19},{19,3},{4,20},{20... | collective-permute-start | bytes 196616 | tf_op jit(solution)/shard_map/ppermute | solution.py:655
  51.2 3.4 %collective-permute-done.10 = bf16[256,128]{1,0:T(8,128)(2,1)S(1)} collective-permute-done((bf16[256,128]{1,0:T(8,128)(2,1)S(1)}, bf16[256,128]{1,0:T(8,128)(2,1)S(1)}, u32[]{:S(2)}, u32[]{:S(2)}) %collective-permute-start.10) | collective-permute-done | bytes 65568 | tf_op jit(solution)/shard_map/ppermute | solution.py:655
  54.5 1.6 %collective-permute-start.13 = (bf16[256,128]{1,0:T(8,128)(2,1)S(1)}, bf16[256,128]{1,0:T(8,128)(2,1)S(1)}, u32[]{:S(2)}, u32[]{:S(2)}) collective-permute-start(bf16[256,128]{1,0:T(8,128)(2,1)S(1)} %add_convert_fusion.2), channel_id=1, source_target_pairs={{0,12},{4,0},{8,4},{12,8},{1,13},{5,1},{9,5},{13,9},{2,14},{6,2},{... | collective-permute-start | bytes 196616 | tf_op jit(solution)/shard_map/ppermute | solution.py:655
  56.1 1.8 %collective-permute-start.12 = (bf16[256,128]{1,0:T(8,128)(2,1)S(1)}, bf16[256,128]{1,0:T(8,128)(2,1)S(1)}, u32[]{:S(2)}, u32[]{:S(2)}) collective-permute-start(bf16[256,128]{1,0:T(8,128)(2,1)S(1)} %add_convert_fusion.2), channel_id=1, source_target_pairs={{0,8},{4,12},{8,0},{12,4},{1,9},{5,13},{9,1},{13,5},{2,10},{6,14},... | collective-permute-start | bytes 196616 | tf_op jit(solution)/shard_map/ppermute | solution.py:655
  57.9 0.0 collective-permute-start.11
  57.9 2.6 %piece_2.1.net = f32[4,16,512]{2,1,0:T(8,128)S(1)} custom-call(s32[3]{0:T(128)S(1)} %pad_add_fusion.place_ref, bf16[256,128,128]{2,1,0:T(8,128)(2,1)S(1)} %get-tuple-element.35.blk, f32[4,16,512]{2,1,0:T(8,128)S(1)} %piece_1.1.net, f32[4,24,512]{2,1,0:T(8,128)S(1)} %get-tuple-element.37.rim, bf16[128,16]{1,0:T(8,128)(2,1)S(1)} %get-tuple-element.38.zf, ...), custom_call_target="tpu_custom_call" | custom-call | tf_op jit(solution)/shard_map/piece_2/pallas_call | solution.py:623
  60.5 0.0 collective-permute-done.13
  60.5 0.8 collective-permute-done.12
  61.3 1.3 %collective-permute-done.11 = bf16[256,128]{1,0:T(8,128)(2,1)S(1)} collective-permute-done((bf16[256,128]{1,0:T(8,128)(2,1)S(1)}, bf16[256,128]{1,0:T(8,128)(2,1)S(1)}, u32[]{:S(2)}, u32[]{:S(2)}) %collective-permute-start.11) | collective-permute-done | bytes 65568 | tf_op jit(solution)/shard_map/ppermute | solution.py:655
  62.7 0.3 collective-permute-start.16
  62.9 1.6 %collective-permute-start.15 = (bf16[256,128]{1,0:T(8,128)(2,1)S(1)}, bf16[256,128]{1,0:T(8,128)(2,1)S(1)}, u32[]{:S(2)}, u32[]{:S(2)}) collective-permute-start(bf16[256,128]{1,0:T(8,128)(2,1)S(1)} %add_convert_fusion.1), channel_id=1, source_target_pairs={{0,2},{1,3},{2,0},{3,1},{4,6},{5,7},{6,4},{7,5},{8,10},{9,11},{10,... | collective-permute-start | bytes 196616 | tf_op jit(solution)/shard_map/ppermute | solution.py:655
  64.5 0.0 collective-permute-start.14
  64.5 2.6 %piece_3.1.net_ref = f32[4,16,512]{2,1,0:T(8,128)S(1)} custom-call(s32[3]{0:T(128)S(1)} %pad_add_fusion.place_ref, bf16[256,128,128]{2,1,0:T(8,128)(2,1)S(1)} %get-tuple-element.35.blk, f32[4,16,512]{2,1,0:T(8,128)S(1)} %piece_2.1.net, f32[4,24,512]{2,1,0:T(8,128)S(1)} %get-tuple-element.37.rim, bf16[128,16]{1,0:T(8,128)(2,1)S(1)} %get-tuple-element.38.zf, ...), custom_call_target="tpu_custom_call" | custom-call | tf_op jit(solution)/shard_map/piece_3/pallas_call | solution.py:623
  67.1 0.0 collective-permute-done.16
  67.1 0.4 collective-permute-done.15
  67.5 2.1 %collective-permute-done.14 = bf16[256,128]{1,0:T(8,128)(2,1)S(1)} collective-permute-done((bf16[256,128]{1,0:T(8,128)(2,1)S(1)}, bf16[256,128]{1,0:T(8,128)(2,1)S(1)}, u32[]{:S(2)}, u32[]{:S(2)}) %collective-permute-start.14) | collective-permute-done | bytes 65568 | tf_op jit(solution)/shard_map/ppermute | solution.py:655
  69.7 2.4 %back_reflect.1 = bf16[5,16,512]{2,1,0:T(8,128)(2,1)S(1)} custom-call(s32[256]{0:T(256)S(1)} %multiply_add_fusion.ray_ref, s32[256]{0:T(256)S(1)} %copy-done.5, bf16[256,128]{1,0:T(8,128)(2,1)S(1)} %add_convert_fusion.r_ref, f32[16,512]{1,0:T(8,128)S(1)} %get-tuple-element.55.x_ref, f32[16,512]{1,0:T(8,128)S(1)} %get-tuple-element.47.x_ref.start_ref, ...), custom_call_target="tpu_custom_call" | custom-call | tf_op jit(solution)/shard_map/back_reflect/pallas_call | solution.py:311
  72.1 13.4 %all-gather = bf16[20,16,512]{2,1,0:T(8,128)(2,1)S(1)} all-gather(bf16[5,16,512]{2,1,0:T(8,128)(2,1)S(1)} %back_reflect.1), channel_id=2, replica_groups=mesh['agent'=4,'tile'=32] {'agent'}, dimensions={0}, use_global_device_ids=true | all-gather | bytes 409600 | tf_op jit(solution)/shard_map/all_gather | solution.py:728
  85.5 1.3 %finish.1 = f32[4,16,512]{2,1,0:T(8,128)} custom-call(s32[3]{0:T(128)S(1)} %pad_add_fusion.place_ref, bf16[4,5,16,512]{3,2,1,0:T(8,128)(2,1)S(1)} %bitcast.30, f32[4,16,512]{2,1,0:T(8,128)S(1)} %bitcast.29, f32[4,16,512]{2,1,0:T(8,128)S(1)} %piece_3.1.net_ref), custom_call_target="tpu_custom_call" | custom-call | tf_op jit(solution)/shard_map/finish/pallas_call | solution.py:342
  (8 shorter events, 0.2 us)
Async XLA Ops:
  0.0 27.4 %copy-start = (f32[1,4,16,512]{3,2,1,0:T(8,128)S(1)}, f32[1,4,16,512]{3,2,1,0:T(8,128)}, u32[]{:S(2)}) copy-start(f32[1,4,16,512]{3,2,1,0:T(8,128)} %states_in.1) | copy-start | bytes 393220
  0.0 27.4 %copy-start.4 = (bf16[3,3,3,32]{3,2,1,0:T(4,128)(2,1)S(1)}, bf16[3,3,3,32]{3,2,1,0:T(4,128)(2,1)}, u32[]{:S(2)}) copy-start(bf16[3,3,3,32]{3,2,1,0:T(4,128)(2,1)} %last.1) | copy-start | bytes 5188
  0.0 27.4 %copy-start.1 = (bf16[3,2,3,3,32,32]{5,4,3,2,1,0:T(8,128)(2,1)S(1)}, bf16[3,2,3,3,32,32]{5,4,3,2,1,0:T(8,128)(2,1)}, u32[]{:S(2)}) copy-start(bf16[3,2,3,3,32,32]{5,4,3,2,1,0:T(8,128)(2,1)} %hidden.1) | copy-start | bytes 331780
  0.0 27.4 %copy-start.3 = (bf16[3,3,3,32]{3,2,1,0:T(4,128)(2,1)S(1)}, bf16[3,3,3,32]{3,2,1,0:T(4,128)(2,1)}, u32[]{:S(2)}) copy-start(bf16[3,3,3,32]{3,2,1,0:T(4,128)(2,1)} %first.1) | copy-start | bytes 5188
  1.7 7.1 %collective-permute-start.1 = (f32[16,512]{1,0:T(8,128)S(1)}, f32[16,512]{1,0:T(8,128)S(1)}, u32[]{:S(2)}, u32[]{:S(2)}) collective-permute-start(f32[16,512]{1,0:T(8,128)S(1)} %get-tuple-element.57), channel_id=1, source_target_pairs={{0,64},{1,65},{2,66},{3,67},{4,68},{5,69},{6,70},{7,71},{8,72},{9,... | collective-permute-start | bytes 98312 | tf_op jit(solution)/shard_map/ppermute | solution.py:682
  6.1 3.1 %collective-permute-start = (f32[16,512]{1,0:T(8,128)S(1)}, f32[16,512]{1,0:T(8,128)S(1)}, u32[]{:S(2)}, u32[]{:S(2)}) collective-permute-start(f32[16,512]{1,0:T(8,128)S(1)} %get-tuple-element.58), channel_id=1, source_target_pairs={{0,32},{1,33},{2,34},{3,35},{4,36},{5,37},{6,38},{7,39},{8,40},{9,... | collective-permute-start | bytes 98312 | tf_op jit(solution)/shard_map/ppermute | solution.py:682
  7.4 4.8 %collective-permute-start.2 = (f32[16,512]{1,0:T(8,128)S(1)}, f32[16,512]{1,0:T(8,128)S(1)}, u32[]{:S(2)}, u32[]{:S(2)}) collective-permute-start(f32[16,512]{1,0:T(8,128)S(1)} %get-tuple-element.59), channel_id=1, source_target_pairs={{0,96},{1,97},{2,98},{3,99},{4,100},{5,101},{6,102},{7,103},{8,104... | collective-permute-start | bytes 98312 | tf_op jit(solution)/shard_map/ppermute | solution.py:682
  8.8 31.3 %copy-start.6 = (s32[256]{0:T(256)S(1)}, s32[256]{0:T(256)}, u32[]{:S(2)}) copy-start(s32[256]{0:T(256)} %detector_in.1) | copy-start | bytes 3076
  8.8 31.3 %copy-start.7 = (s32[256]{0:T(256)S(1)}, s32[256]{0:T(256)}, u32[]{:S(2)}) copy-start(s32[256]{0:T(256)} %angle_in.1) | copy-start | bytes 3076
  17.8 8.1 %collective-permute-start.3 = (bf16[256,128]{1,0:T(8,128)(2,1)S(1)}, bf16[256,128]{1,0:T(8,128)(2,1)S(1)}, u32[]{:S(2)}, u32[]{:S(2)}) collective-permute-start(bf16[256,128]{1,0:T(8,128)(2,1)S(1)} %get-tuple-element.32), channel_id=1, source_target_pairs={{0,16},{16,0},{1,17},{17,1},{2,18},{18,2},{3,19},{19,3},{4,20},{20... | collective-permute-start | bytes 196616 | tf_op jit(solution)/shard_map/ppermute | solution.py:655
  25.9 5.4 %collective-permute-start.6 = (bf16[256,128]{1,0:T(8,128)(2,1)S(1)}, bf16[256,128]{1,0:T(8,128)(2,1)S(1)}, u32[]{:S(2)}, u32[]{:S(2)}) collective-permute-start(bf16[256,128]{1,0:T(8,128)(2,1)S(1)} %add_convert_fusion.5), channel_id=1, source_target_pairs={{0,12},{4,0},{8,4},{12,8},{1,13},{5,1},{9,5},{13,9},{2,14},{6,2},{... | collective-permute-start | bytes 196616 | tf_op jit(solution)/shard_map/ppermute | solution.py:655
  26.0 5.4 %collective-permute-start.5 = (bf16[256,128]{1,0:T(8,128)(2,1)S(1)}, bf16[256,128]{1,0:T(8,128)(2,1)S(1)}, u32[]{:S(2)}, u32[]{:S(2)}) collective-permute-start(bf16[256,128]{1,0:T(8,128)(2,1)S(1)} %add_convert_fusion.5), channel_id=1, source_target_pairs={{0,8},{4,12},{8,0},{12,4},{1,9},{5,13},{9,1},{13,5},{2,10},{6,14},... | collective-permute-start | bytes 196616 | tf_op jit(solution)/shard_map/ppermute | solution.py:655
  26.1 7.0 %collective-permute-start.4 = (bf16[256,128]{1,0:T(8,128)(2,1)S(1)}, bf16[256,128]{1,0:T(8,128)(2,1)S(1)}, u32[]{:S(2)}, u32[]{:S(2)}) collective-permute-start(bf16[256,128]{1,0:T(8,128)(2,1)S(1)} %add_convert_fusion.5), channel_id=1, source_target_pairs={{0,4},{4,8},{8,12},{12,0},{1,5},{5,9},{9,13},{13,1},{2,6},{6,10},{... | collective-permute-start | bytes 196616 | tf_op jit(solution)/shard_map/ppermute | solution.py:655
  28.6 15.9 %copy-start.2 = (f32[8,4,128]{2,1,0:T(4,128)S(1)}, f32[8,4,128]{2,1,0:T(4,128)}, u32[]{:S(2)}) copy-start(f32[8,4,128]{2,1,0:T(4,128)} %sino_ref.1) | copy-start | bytes 49156
  28.6 15.9 %copy-start.5 = (s32[256]{0:T(256)S(1)}, s32[256]{0:T(256)}, u32[]{:S(2)}) copy-start(s32[256]{0:T(256)} %tile_ref.3) | copy-start | bytes 3076
  33.1 9.7 %collective-permute-start.9 = (bf16[256,128]{1,0:T(8,128)(2,1)S(1)}, bf16[256,128]{1,0:T(8,128)(2,1)S(1)}, u32[]{:S(2)}, u32[]{:S(2)}) collective-permute-start(bf16[256,128]{1,0:T(8,128)(2,1)S(1)} %add_convert_fusion.4), channel_id=1, source_target_pairs={{0,3},{1,0},{2,1},{3,2},{4,7},{5,4},{6,5},{7,6},{8,11},{9,8},{10,9... | collective-permute-start | bytes 196616 | tf_op jit(solution)/shard_map/ppermute | solution.py:655
  39.4 4.7 %collective-permute-start.8 = (bf16[256,128]{1,0:T(8,128)(2,1)S(1)}, bf16[256,128]{1,0:T(8,128)(2,1)S(1)}, u32[]{:S(2)}, u32[]{:S(2)}) collective-permute-start(bf16[256,128]{1,0:T(8,128)(2,1)S(1)} %add_convert_fusion.4), channel_id=1, source_target_pairs={{0,2},{1,3},{2,0},{3,1},{4,6},{5,7},{6,4},{7,5},{8,10},{9,11},{10,... | collective-permute-start | bytes 196616 | tf_op jit(solution)/shard_map/ppermute | solution.py:655
  39.4 5.0 %collective-permute-start.7 = (bf16[256,128]{1,0:T(8,128)(2,1)S(1)}, bf16[256,128]{1,0:T(8,128)(2,1)S(1)}, u32[]{:S(2)}, u32[]{:S(2)}) collective-permute-start(bf16[256,128]{1,0:T(8,128)(2,1)S(1)} %add_convert_fusion.4), channel_id=1, source_target_pairs={{0,1},{1,2},{2,3},{3,0},{4,5},{5,6},{6,7},{7,4},{8,9},{9,10},{10,1... | collective-permute-start | bytes 196616 | tf_op jit(solution)/shard_map/ppermute | solution.py:655
  49.8 4.7 %collective-permute-start.10 = (bf16[256,128]{1,0:T(8,128)(2,1)S(1)}, bf16[256,128]{1,0:T(8,128)(2,1)S(1)}, u32[]{:S(2)}, u32[]{:S(2)}) collective-permute-start(bf16[256,128]{1,0:T(8,128)(2,1)S(1)} %get-tuple-element.50), channel_id=1, source_target_pairs={{0,16},{16,0},{1,17},{17,1},{2,18},{18,2},{3,19},{19,3},{4,20},{20... | collective-permute-start | bytes 196616 | tf_op jit(solution)/shard_map/ppermute | solution.py:655
  54.5 6.0 %collective-permute-start.13 = (bf16[256,128]{1,0:T(8,128)(2,1)S(1)}, bf16[256,128]{1,0:T(8,128)(2,1)S(1)}, u32[]{:S(2)}, u32[]{:S(2)}) collective-permute-start(bf16[256,128]{1,0:T(8,128)(2,1)S(1)} %add_convert_fusion.2), channel_id=1, source_target_pairs={{0,12},{4,0},{8,4},{12,8},{1,13},{5,1},{9,5},{13,9},{2,14},{6,2},{... | collective-permute-start | bytes 196616 | tf_op jit(solution)/shard_map/ppermute | solution.py:655
  56.1 5.1 %collective-permute-start.12 = (bf16[256,128]{1,0:T(8,128)(2,1)S(1)}, bf16[256,128]{1,0:T(8,128)(2,1)S(1)}, u32[]{:S(2)}, u32[]{:S(2)}) collective-permute-start(bf16[256,128]{1,0:T(8,128)(2,1)S(1)} %add_convert_fusion.2), channel_id=1, source_target_pairs={{0,8},{4,12},{8,0},{12,4},{1,9},{5,13},{9,1},{13,5},{2,10},{6,14},... | collective-permute-start | bytes 196616 | tf_op jit(solution)/shard_map/ppermute | solution.py:655
  57.9 4.7 %collective-permute-start.11 = (bf16[256,128]{1,0:T(8,128)(2,1)S(1)}, bf16[256,128]{1,0:T(8,128)(2,1)S(1)}, u32[]{:S(2)}, u32[]{:S(2)}) collective-permute-start(bf16[256,128]{1,0:T(8,128)(2,1)S(1)} %add_convert_fusion.2), channel_id=1, source_target_pairs={{0,4},{4,8},{8,12},{12,0},{1,5},{5,9},{9,13},{13,1},{2,6},{6,10},{... | collective-permute-start | bytes 196616 | tf_op jit(solution)/shard_map/ppermute | solution.py:655
  62.7 4.5 %collective-permute-start.16 = (bf16[256,128]{1,0:T(8,128)(2,1)S(1)}, bf16[256,128]{1,0:T(8,128)(2,1)S(1)}, u32[]{:S(2)}, u32[]{:S(2)}) collective-permute-start(bf16[256,128]{1,0:T(8,128)(2,1)S(1)} %add_convert_fusion.1), channel_id=1, source_target_pairs={{0,3},{1,0},{2,1},{3,2},{4,7},{5,4},{6,5},{7,6},{8,11},{9,8},{10,9... | collective-permute-start | bytes 196616 | tf_op jit(solution)/shard_map/ppermute | solution.py:655
  62.9 4.6 %collective-permute-start.15 = (bf16[256,128]{1,0:T(8,128)(2,1)S(1)}, bf16[256,128]{1,0:T(8,128)(2,1)S(1)}, u32[]{:S(2)}, u32[]{:S(2)}) collective-permute-start(bf16[256,128]{1,0:T(8,128)(2,1)S(1)} %add_convert_fusion.1), channel_id=1, source_target_pairs={{0,2},{1,3},{2,0},{3,1},{4,6},{5,7},{6,4},{7,5},{8,10},{9,11},{10,... | collective-permute-start | bytes 196616 | tf_op jit(solution)/shard_map/ppermute | solution.py:655
  64.5 5.2 %collective-permute-start.14 = (bf16[256,128]{1,0:T(8,128)(2,1)S(1)}, bf16[256,128]{1,0:T(8,128)(2,1)S(1)}, u32[]{:S(2)}, u32[]{:S(2)}) collective-permute-start(bf16[256,128]{1,0:T(8,128)(2,1)S(1)} %add_convert_fusion.1), channel_id=1, source_target_pairs={{0,1},{1,2},{2,3},{3,0},{4,5},{5,6},{6,7},{7,4},{8,9},{9,10},{10,1... | collective-permute-start | bytes 196616 | tf_op jit(solution)/shard_map/ppermute | solution.py:655

commit v3 on v1

--- a/solution.py
+++ b/solution.py
@@ -13,6 +13,8 @@
 VMEM_LIMIT = 32 << 20
 TOGETHER = 4
 UNROLL = 16
+CHUNK = 64
+PIECES = ((0,), (1, 2), (3,))
 SPAN = 6
 
 
@@ -179,22 +181,32 @@
     ]
     for copy in small:
         copy.start()
-    chunk = TOGETHER * UNROLL
+    chunk = CHUNK
 
     def chunk_copy(i):
         part = pl.ds(i * chunk, chunk)
         return pltpu.make_async_copy(blk_in.at[part], blk.at[part], block_sems.at[i])
 
-    for i in range(blk.shape[0] // chunk):
+    ahead = 2
+    count = blk.shape[0] // chunk
+    for i in range(ahead):
         chunk_copy(i).start()
+
+    def ready(i):
+        chunk_copy(i).wait()
+
+        @pl.when(i + ahead < count)
+        def _():
+            chunk_copy(i + ahead).start()
+
     acc[...] = jnp.zeros_like(acc)
     for copy in small:
         copy.wait()
-    start_ref[...] = got_1[...] + got_2[...] + got_3[...]
-
-    @pl.when(place_ref[0] == 0)
-    def _():
-        start_ref[...] = first_slice[...]
+    for k, value in enumerate((first_slice, got_1, got_2, got_3)):
+
+        @pl.when(place_ref[0] == k)
+        def _():
+            start_ref[...] = value[...]
 
     load_pixels(start_ref[...], pix)
     wide = first_slice.shape[1] // 128
@@ -204,7 +216,7 @@
         pix,
         blk,
         acc,
-        lambda i: chunk_copy(i).wait(),
+        ready,
     )
     store_rays(place_ref, sino, acc, total, o_ref)
 
@@ -233,7 +245,7 @@
             pltpu.VMEM((ray_total, 8, 128), F32),
             pltpu.VMEM((ray_total + 8, 128), F32),
             pltpu.SemaphoreType.DMA((5,)),
-            pltpu.SemaphoreType.DMA((count // (TOGETHER * UNROLL),)),
+            pltpu.SemaphoreType.DMA((count // CHUNK,)),
         ],
         compiler_params=params(),
         name="project",
@@ -410,7 +422,7 @@
 
 
 def prepare_kernel(
-    place_ref, before, cur, after, first, hidden, last, rim, zf, zh, zl, zw, zm, af, ah, al, turn
+    place_ref, before, after, cur, first, hidden, last, rim, zf, zh, zl, zw, zm, af, ah, al, turn
 ):
     depth = before.shape[1]
     rows = cur.shape[1]
@@ -433,10 +445,10 @@
 
 
 def prepare(place, rim, current, first, hidden, last):
-    before, after = rim
     layers = hidden.shape[1]
     slices, rows, columns = current.shape
-    whole = jax.ShapeDtypeStruct((slices, rows + 2 * before.shape[1], columns), F32)
+    depth = rim[0].shape[1]
+    whole = jax.ShapeDtypeStruct((slices, rows + 2 * depth, columns), F32)
     shapes = [
         (128, 16),
         (layers, 128, 384),
@@ -455,7 +467,7 @@
         scratch_shapes=[pltpu.VMEM((256, 256), F32)],
         compiler_params=params(),
         name="prepare",
-    )(place, before, current, after, first, hidden, last)
+    )(place, *rim, current, first, hidden, last)
 
 
 def side_by_side(value):
@@ -634,7 +646,7 @@
 
 
 def rims(cells, depth):
-    agents, count = 4, lax.axis_size("tile")
+    count = lax.axis_size("tile")
     pairs = [(a * count + t, a * count + t + 1) for a in (1, 2) for t in range(count - 1)]
     both = ("agent", "tile")
     before = lax.ppermute(cells[:, cells.shape[1] - depth :], both, pairs)
@@ -673,19 +685,20 @@
     groups = stage_groups(tile_count)
     net = jnp.zeros_like(current)
     x_data = start
-    prepared, rim, k = None, None, 0
     for step in range(DATA_STEPS):
         for n, group in enumerate(groups):
             sums, net = lax.optimization_barrier((sums, net))
-            if n == 0 and step == 0:
+            if step == DATA_STEPS - 1:
+                if n == 0:
+                    prepared = prepare(place, rim, current, conv_first, conv_hidden, conv_last)
+                for k in PIECES[n]:
+                    net = piece(k, place, blocks_here, net, prepared)
+            if step == DATA_STEPS - 2 and n == len(groups) - 1:
                 around, sums = lax.optimization_barrier((current, sums))
                 rim = rims(around, conv_hidden.shape[1] + 2)
-            elif n > 0:
-                if prepared is None:
-                    prepared = prepare(place, rim, current, conv_first, conv_hidden, conv_last)
-                net = piece(k, place, blocks_here, net, prepared)
-                k += 1
-            sums = added_up(sums, group)
+                rim, sums = lax.optimization_barrier((rim, added_up(sums, group)))
+            else:
+                sums = added_up(sums, group)
         if step < DATA_STEPS - 1:
             x_data, sums = back_project(
                 place, ray_index, block_tile, sums, x_data, sinogram, blocks_here

time: 92.3 us -> 86.8 us (0.940)
  blocking collectives: 14.7 us -> 12 us
  starting transfers between devices: 34.5 us -> 32.9 us
    all_gather x1, blocking collectives: 14.7 us -> 12 us  [per_device(): everything = lax.all_gather(sent, 'agent')]
    ppermute x14, starting transfers between devices: 26.4 us -> 24.5 us  [added_up(): total = total + lax.ppermute(values, 'tile', swapped(groups, k)).astype(F32)]
  transfers between devices with their start and end apart: 19 -> 19, of which waited for: 10 -> 8; matrix products, arithmetic and copies ran while one was open for 0% -> 0% of each run, Pallas kernels for 13% -> 13%
where the time goes in v3:
time: 86.8 us; the launch traced here: 86.6 us
  starting transfers between devices  32.9 us (38%)
  Pallas kernels  26.1 us (30%)
  waiting for transfers between devices  14.1 us (16%)
  blocking collectives  12 us (14%)
  local copies, waits for them, and re-layouts  0.95 us (1%)
    ppermute x14, starting transfers between devices, added_up(): total = total + lax.ppermute(values, 'tile', swapped(groups, k)).astype(F32)  24.5 us
    all_gather x1, blocking collectives, per_device(): everything = lax.all_gather(sent, 'agent')  12 us
    pallas_call x4, Pallas kernels, piece(): pl.pallas_call(functools.partial(piece_kernel, k), out_shape=jax.ShapeDty...  10.5 us
    ppermute x14, waiting for transfers between devices, added_up(): total = total + lax.ppermute(values, 'tile', swapped(groups, k)).astype(F32)  8.31 us
    pallas_call x1, Pallas kernels, project(): pl.pallas_call(project_kernel, out_shape=(jax.ShapeDtypeStruct((ray_total...  5.5 us
    pallas_call x1, Pallas kernels, back_project(): pl.pallas_call(back_project_kernel, out_shape=(jax.ShapeDtypeStruct(x.sha...  5.3 us
    ppermute x3, waiting for transfers between devices, slices_sent(): lax.ppermute(current[k], 'agent', [(0, k)])  4.88 us
    ppermute x1, starting transfers between devices, rims(): before = lax.ppermute(cells[:, cells.shape[1] - depth:], both, pairs)  4.48 us
  transfers between devices with their start and end apart: 19, of which 8 were waited for; matrix products, arithmetic and copies ran while one was open for 0% of the time, Pallas kernels for 13%

profile of v3, /device:TPU:1, one launch (start us, length us, event | category | flops | bytes accessed | tf_op | source)
XLA Modules:
  0.0 86.6 jit_solution(3982844691872407571)
XLA Ops:
  0.0 0.0 copy-start
  0.0 0.0 copy-start.5
  0.0 0.0 copy-start.6
  0.0 0.0 copy-start.7
  0.0 0.0 copy-start.2
  0.0 0.9 %slice_bitcast_fusion = (f32[16,512]{1,0:T(8,128)S(1)}, f32[16,512]{1,0:T(8,128)S(1)}, f32[16,512]{1,0:T(8,128)S(1)}) fusion(f32[1,4,16,512]{3,2,1,0:T(8,128)} %states_in.1), kind=kLoop, calls=%fused_computation.6 | loop fusion | bytes 196608 | tf_op jit(solution)/shard_map/squeeze | solution.py:658
  0.9 0.7 collective-permute-start.2
  1.6 0.7 collective-permute-start.1
  2.3 1.3 %collective-permute-start = (f32[16,512]{1,0:T(8,128)S(1)}, f32[16,512]{1,0:T(8,128)S(1)}, u32[]{:S(2)}, u32[]{:S(2)}) collective-permute-start(f32[16,512]{1,0:T(8,128)S(1)} %get-tuple-element.71), channel_id=1, source_target_pairs={{0,32},{1,33},{2,34},{3,35},{4,36},{5,37},{6,38},{7,39},{8,40},{9,... | collective-permute-start | bytes 98312 | tf_op jit(solution)/shard_map/ppermute | solution.py:658
  3.6 0.1 pad_add_fusion.place_ref
  3.6 0.0 copy-start.1
  3.6 0.0 collective-permute-done.2.got_3
  3.6 0.0 collective-permute-done.1.got_2
  3.7 4.9 %collective-permute-done.got_1 = f32[16,512]{1,0:T(8,128)S(1)} collective-permute-done((f32[16,512]{1,0:T(8,128)S(1)}, f32[16,512]{1,0:T(8,128)S(1)}, u32[]{:S(2)}, u32[]{:S(2)}) %collective-permute-start) | collective-permute-done | bytes 32800 | tf_op jit(solution)/shard_map/ppermute | solution.py:658
  8.5 5.5 %project.1 = (bf16[256,128]{1,0:T(8,128)(2,1)S(1)}, f32[16,512]{1,0:T(8,128)S(1)}, bf16[256,128,128]{2,1,0:T(8,128)(2,1)S(1)}) custom-call(s32[3]{0:T(128)S(1)} %pad_add_fusion.place_ref, s32[256]{0:T(256)} %angle_in.1, s32[256]{0:T(256)} %detector_in.1, s32[256]{0:T(256)} %tile_ref.3, f32[1,4,16,512]{3,2,1,0:T(8,128)} %states_in.1, ...), custom_call_target="tpu_custom_call" | custom-call | tf_op jit(solution)/shard_map/project/pallas_call | solution.py:229
  14.0 2.5 %collective-permute-start.3 = (bf16[256,128]{1,0:T(8,128)(2,1)S(1)}, bf16[256,128]{1,0:T(8,128)(2,1)S(1)}, u32[]{:S(2)}, u32[]{:S(2)}) collective-permute-start(bf16[256,128]{1,0:T(8,128)(2,1)S(1)} %get-tuple-element.37), channel_id=1, source_target_pairs={{0,16},{16,0},{1,17},{17,1},{2,18},{18,2},{3,19},{19,3},{4,20},{20... | collective-permute-start | bytes 196616 | tf_op jit(solution)/shard_map/ppermute | solution.py:644
  16.6 2.6 %collective-permute-done.3 = bf16[256,128]{1,0:T(8,128)(2,1)S(1)} collective-permute-done((bf16[256,128]{1,0:T(8,128)(2,1)S(1)}, bf16[256,128]{1,0:T(8,128)(2,1)S(1)}, u32[]{:S(2)}, u32[]{:S(2)}) %collective-permute-start.3) | collective-permute-done | bytes 65568 | tf_op jit(solution)/shard_map/ppermute | solution.py:644
  19.2 2.8 %collective-permute-start.6 = (bf16[256,128]{1,0:T(8,128)(2,1)S(1)}, bf16[256,128]{1,0:T(8,128)(2,1)S(1)}, u32[]{:S(2)}, u32[]{:S(2)}) collective-permute-start(bf16[256,128]{1,0:T(8,128)(2,1)S(1)} %add_convert_fusion.5), channel_id=1, source_target_pairs={{0,12},{4,0},{8,4},{12,8},{1,13},{5,1},{9,5},{13,9},{2,14},{6,2},{... | collective-permute-start | bytes 196616 | tf_op jit(solution)/shard_map/ppermute | solution.py:644
  22.0 0.4 collective-permute-start.5
  22.3 0.7 collective-permute-start.4
  23.0 0.0 copy-done.6
  23.0 0.0 copy-done.7
  23.0 0.3 collective-permute-done.6
  23.3 3.4 %collective-permute-done.5 = bf16[256,128]{1,0:T(8,128)(2,1)S(1)} collective-permute-done((bf16[256,128]{1,0:T(8,128)(2,1)S(1)}, bf16[256,128]{1,0:T(8,128)(2,1)S(1)}, u32[]{:S(2)}, u32[]{:S(2)}) %collective-permute-start.5) | collective-permute-done | bytes 65568 | tf_op jit(solution)/shard_map/ppermute | solution.py:644
  26.7 0.6 collective-permute-done.4
  27.4 3.8 %collective-permute-start.11 = (bf16[256,128]{1,0:T(8,128)(2,1)S(1)}, bf16[256,128]{1,0:T(8,128)(2,1)S(1)}, u32[]{:S(2)}, u32[]{:S(2)}) collective-permute-start(bf16[256,128]{1,0:T(8,128)(2,1)S(1)} %add_convert_fusion.4), channel_id=1, source_target_pairs={{0,3},{1,0},{2,1},{3,2},{4,7},{5,4},{6,5},{7,6},{8,11},{9,8},{10,9... | collective-permute-start | bytes 196616 | tf_op jit(solution)/shard_map/ppermute | solution.py:644
  31.2 0.0 collective-permute-start.10
  31.2 0.7 collective-permute-start.9
  31.9 0.0 copy-done
  31.9 1.3 %collective-permute-start.8 = (f32[4,4,512]{2,1,0:T(4,128)S(1)}, f32[4,4,512]{2,1,0:T(4,128)S(1)}, u32[]{:S(2)}, u32[]{:S(2)}) collective-permute-start(f32[4,4,512]{2,1,0:T(4,128)S(1)} %get-tuple-element.67), channel_id=1, source_target_pairs={{33,32},{34,33},{35,34},{36,35},{37,36},{38,37},{39,38},{40,39},{4... | collective-permute-start | bytes 98312 | tf_op jit(solution)/shard_map/ppermute | solution.py:653
  33.2 4.5 %collective-permute-start.7 = (f32[4,4,512]{2,1,0:T(4,128)S(1)}, f32[4,4,512]{2,1,0:T(4,128)S(1)}, u32[]{:S(2)}, u32[]{:S(2)}) collective-permute-start(f32[4,4,512]{2,1,0:T(4,128)S(1)} %get-tuple-element.68), channel_id=1, source_target_pairs={{32,33},{33,34},{34,35},{35,36},{36,37},{37,38},{38,39},{39,40},{4... | collective-permute-start | bytes 98312 | tf_op jit(solution)/shard_map/ppermute | solution.py:652
  37.7 0.0 collective-permute-done.11
  37.7 0.0 collective-permute-done.10
  37.7 0.0 collective-permute-done.9
  37.8 0.0 collective-permute-done.8.after
  37.8 0.9 %collective-permute-done.7.before = f32[4,4,512]{2,1,0:T(4,128)S(1)} collective-permute-done((f32[4,4,512]{2,1,0:T(4,128)S(1)}, f32[4,4,512]{2,1,0:T(4,128)S(1)}, u32[]{:S(2)}, u32[]{:S(2)}) %collective-permute-start.7) | collective-permute-done | bytes 32800 | tf_op jit(solution)/shard_map/ppermute | solution.py:652
  38.7 0.0 copy-done.5
  38.7 0.0 copy-done.2
  38.7 5.3 %back_project.1 = (f32[16,512]{1,0:T(8,128)S(1)}, bf16[256,128]{1,0:T(8,128)(2,1)S(1)}) custom-call(s32[3]{0:T(128)S(1)} %pad_add_fusion.place_ref, s32[256]{0:T(256)S(1)} %multiply_add_fusion.ray_ref, s32[256]{0:T(256)S(1)} %copy-done.5, bf16[256,128]{1,0:T(8,128)(2,1)S(1)} %add_convert_fusion.3.r_ref, f32[16,512]{1,0:T(8,128)S(1)} %get-tuple-element.45.x_ref.start_ref, ...), custom_call_target="tpu_custom_call" | custom-call | tf_op jit(solution)/shard_map/back_project/pallas_call | solution.py:281
  44.0 10.5 %collective-permute-start.12 = (bf16[256,128]{1,0:T(8,128)(2,1)S(1)}, bf16[256,128]{1,0:T(8,128)(2,1)S(1)}, u32[]{:S(2)}, u32[]{:S(2)}) collective-permute-start(bf16[256,128]{1,0:T(8,128)(2,1)S(1)} %get-tuple-element.49), channel_id=1, source_target_pairs={{0,16},{16,0},{1,17},{17,1},{2,18},{18,2},{3,19},{19,3},{4,20},{20... | collective-permute-start | bytes 196616 | tf_op jit(solution)/shard_map/ppermute | solution.py:644
  54.6 0.0 copy-done.1
  54.6 0.0 copy-done.3
  54.6 0.0 copy-done.4
  54.6 1.1 %prepare.1 = (f32[4,24,512]{2,1,0:T(8,128)S(1)}, bf16[128,16]{1,0:T(8,128)(2,1)S(1)}, bf16[2,128,384]{2,1,0:T(8,128)(2,1)S(1)}, bf16[8,384]{1,0:T(8,128)(2,1)S(1...) custom-call(s32[3]{0:T(128)S(1)} %pad_add_fusion.place_ref, ...), custom_call_target="tpu_custom_call" | custom-call | tf_op jit(solution)/shard_map/prepare/pallas_call | solution.py:462
  55.7 2.6 %piece_0.1.net = f32[4,16,512]{2,1,0:T(8,128)S(1)} custom-call(s32[3]{0:T(128)S(1)} %pad_add_fusion.place_ref, bf16[256,128,128]{2,1,0:T(8,128)(2,1)S(1)} %get-tuple-element.46.blk, f32[4,16,512]{2,1,0:T(8,128)S(1)} %broadcast_in_dim.6.net, f32[4,24,512]{2,1,0:T(8,128)S(1)} %get-tuple-element.53.rim, bf16[128,16]{1,0:T(8,128)(2,1)S(1)} %get-tuple-element.54.zf, ...), custom_call_target="tpu_custom_call" | custom-call | tf_op jit(solution)/shard_map/piece_0/pallas_call | solution.py:612
  58.4 0.0 collective-permute-done.12
  58.4 0.1 collective-permute-start.15
  58.5 0.1 collective-permute-start.14
  58.6 1.4 %collective-permute-start.13 = (bf16[256,128]{1,0:T(8,128)(2,1)S(1)}, bf16[256,128]{1,0:T(8,128)(2,1)S(1)}, u32[]{:S(2)}, u32[]{:S(2)}) collective-permute-start(bf16[256,128]{1,0:T(8,128)(2,1)S(1)} %add_convert_fusion.2), channel_id=1, source_target_pairs={{0,4},{4,8},{8,12},{12,0},{1,5},{5,9},{9,13},{13,1},{2,6},{6,10},{... | collective-permute-start | bytes 196616 | tf_op jit(solution)/shard_map/ppermute | solution.py:644
  59.9 2.6 %piece_1.1.net = f32[4,16,512]{2,1,0:T(8,128)S(1)} custom-call(s32[3]{0:T(128)S(1)} %pad_add_fusion.place_ref, bf16[256,128,128]{2,1,0:T(8,128)(2,1)S(1)} %get-tuple-element.46.blk, f32[4,16,512]{2,1,0:T(8,128)S(1)} %piece_0.1.net, f32[4,24,512]{2,1,0:T(8,128)S(1)} %get-tuple-element.53.rim, bf16[128,16]{1,0:T(8,128)(2,1)S(1)} %get-tuple-element.54.zf, ...), custom_call_target="tpu_custom_call" | custom-call | tf_op jit(solution)/shard_map/piece_1/pallas_call | solution.py:612
  62.5 2.6 %piece_2.1.net = f32[4,16,512]{2,1,0:T(8,128)S(1)} custom-call(s32[3]{0:T(128)S(1)} %pad_add_fusion.place_ref, bf16[256,128,128]{2,1,0:T(8,128)(2,1)S(1)} %get-tuple-element.46.blk, f32[4,16,512]{2,1,0:T(8,128)S(1)} %piece_1.1.net, f32[4,24,512]{2,1,0:T(8,128)S(1)} %get-tuple-element.53.rim, bf16[128,16]{1,0:T(8,128)(2,1)S(1)} %get-tuple-element.54.zf, ...), custom_call_target="tpu_custom_call" | custom-call | tf_op jit(solution)/shard_map/piece_2/pallas_call | solution.py:612
  65.2 0.0 collective-permute-done.15
  65.2 0.0 collective-permute-done.14
  65.2 0.0 collective-permute-done.13
  65.2 0.1 collective-permute-start.18
  65.3 0.1 collective-permute-start.17
  65.4 1.4 %collective-permute-start.16 = (bf16[256,128]{1,0:T(8,128)(2,1)S(1)}, bf16[256,128]{1,0:T(8,128)(2,1)S(1)}, u32[]{:S(2)}, u32[]{:S(2)}) collective-permute-start(bf16[256,128]{1,0:T(8,128)(2,1)S(1)} %add_convert_fusion.1), channel_id=1, source_target_pairs={{0,1},{1,2},{2,3},{3,0},{4,5},{5,6},{6,7},{7,4},{8,9},{9,10},{10,1... | collective-permute-start | bytes 196616 | tf_op jit(solution)/shard_map/ppermute | solution.py:644
  66.8 2.6 %piece_3.1.net_ref = f32[4,16,512]{2,1,0:T(8,128)S(1)} custom-call(s32[3]{0:T(128)S(1)} %pad_add_fusion.place_ref, bf16[256,128,128]{2,1,0:T(8,128)(2,1)S(1)} %get-tuple-element.46.blk, f32[4,16,512]{2,1,0:T(8,128)S(1)} %piece_2.1.net, f32[4,24,512]{2,1,0:T(8,128)S(1)} %get-tuple-element.53.rim, bf16[128,16]{1,0:T(8,128)(2,1)S(1)} %get-tuple-element.54.zf, ...), custom_call_target="tpu_custom_call" | custom-call | tf_op jit(solution)/shard_map/piece_3/pallas_call | solution.py:612
  69.4 0.0 collective-permute-done.18
  69.4 0.6 collective-permute-done.17
  70.0 0.8 collective-permute-done.16
  70.9 2.4 %back_reflect.1 = bf16[5,16,512]{2,1,0:T(8,128)(2,1)S(1)} custom-call(s32[256]{0:T(256)S(1)} %multiply_add_fusion.ray_ref, s32[256]{0:T(256)S(1)} %copy-done.5, bf16[256,128]{1,0:T(8,128)(2,1)S(1)} %add_convert_fusion.r_ref, f32[16,512]{1,0:T(8,128)S(1)} %get-tuple-element.65.x_ref, f32[16,512]{1,0:T(8,128)S(1)} %get-tuple-element.45.x_ref.start_ref, ...), custom_call_target="tpu_custom_call" | custom-call | tf_op jit(solution)/shard_map/back_reflect/pallas_call | solution.py:312
  73.3 12.0 %all-gather = bf16[20,16,512]{2,1,0:T(8,128)(2,1)S(1)} all-gather(bf16[5,16,512]{2,1,0:T(8,128)(2,1)S(1)} %back_reflect.1), channel_id=2, replica_groups=mesh['agent'=4,'tile'=32] {'agent'}, dimensions={0}, use_global_device_ids=true | all-gather | bytes 409600 | tf_op jit(solution)/shard_map/all_gather | solution.py:707
  85.3 1.3 %finish.1 = f32[4,16,512]{2,1,0:T(8,128)} custom-call(s32[3]{0:T(128)S(1)} %pad_add_fusion.place_ref, bf16[4,5,16,512]{3,2,1,0:T(8,128)(2,1)S(1)} %bitcast.15, f32[4,16,512]{2,1,0:T(8,128)S(1)} %bitcast.14, f32[4,16,512]{2,1,0:T(8,128)S(1)} %piece_3.1.net_ref), custom_call_target="tpu_custom_call" | custom-call | tf_op jit(solution)/shard_map/finish/pallas_call | solution.py:343
  (11 shorter events, 0.2 us)
Async XLA Ops:
  0.0 31.9 %copy-start = (f32[1,4,16,512]{3,2,1,0:T(8,128)S(1)}, f32[1,4,16,512]{3,2,1,0:T(8,128)}, u32[]{:S(2)}) copy-start(f32[1,4,16,512]{3,2,1,0:T(8,128)} %states_in.1) | copy-start | bytes 393220
  0.0 38.7 %copy-start.5 = (s32[256]{0:T(256)S(1)}, s32[256]{0:T(256)}, u32[]{:S(2)}) copy-start(s32[256]{0:T(256)} %tile_ref.3) | copy-start | bytes 3076
  0.0 23.0 %copy-start.6 = (s32[256]{0:T(256)S(1)}, s32[256]{0:T(256)}, u32[]{:S(2)}) copy-start(s32[256]{0:T(256)} %detector_in.1) | copy-start | bytes 3076
  0.0 23.0 %copy-start.7 = (s32[256]{0:T(256)S(1)}, s32[256]{0:T(256)}, u32[]{:S(2)}) copy-start(s32[256]{0:T(256)} %angle_in.1) | copy-start | bytes 3076
  0.0 38.7 %copy-start.2 = (f32[8,4,128]{2,1,0:T(4,128)S(1)}, f32[8,4,128]{2,1,0:T(4,128)}, u32[]{:S(2)}) copy-start(f32[8,4,128]{2,1,0:T(4,128)} %sino_ref.1) | copy-start | bytes 49156
  0.9 2.7 %collective-permute-start.2 = (f32[16,512]{1,0:T(8,128)S(1)}, f32[16,512]{1,0:T(8,128)S(1)}, u32[]{:S(2)}, u32[]{:S(2)}) collective-permute-start(f32[16,512]{1,0:T(8,128)S(1)} %get-tuple-element.69), channel_id=1, source_target_pairs={{0,96},{1,97},{2,98},{3,99},{4,100},{5,101},{6,102},{7,103},{8,104... | collective-permute-start | bytes 98312 | tf_op jit(solution)/shard_map/ppermute | solution.py:658
  1.6 2.1 %collective-permute-start.1 = (f32[16,512]{1,0:T(8,128)S(1)}, f32[16,512]{1,0:T(8,128)S(1)}, u32[]{:S(2)}, u32[]{:S(2)}) collective-permute-start(f32[16,512]{1,0:T(8,128)S(1)} %get-tuple-element.70), channel_id=1, source_target_pairs={{0,64},{1,65},{2,66},{3,67},{4,68},{5,69},{6,70},{7,71},{8,72},{9,... | collective-permute-start | bytes 98312 | tf_op jit(solution)/shard_map/ppermute | solution.py:658
  2.3 6.3 %collective-permute-start = (f32[16,512]{1,0:T(8,128)S(1)}, f32[16,512]{1,0:T(8,128)S(1)}, u32[]{:S(2)}, u32[]{:S(2)}) collective-permute-start(f32[16,512]{1,0:T(8,128)S(1)} %get-tuple-element.71), channel_id=1, source_target_pairs={{0,32},{1,33},{2,34},{3,35},{4,36},{5,37},{6,38},{7,39},{8,40},{9,... | collective-permute-start | bytes 98312 | tf_op jit(solution)/shard_map/ppermute | solution.py:658
  3.6 50.9 %copy-start.1 = (bf16[3,2,3,3,32,32]{5,4,3,2,1,0:T(8,128)(2,1)S(1)}, bf16[3,2,3,3,32,32]{5,4,3,2,1,0:T(8,128)(2,1)}, u32[]{:S(2)}) copy-start(bf16[3,2,3,3,32,32]{5,4,3,2,1,0:T(8,128)(2,1)} %hidden.1) | copy-start | bytes 331780
  3.6 50.9 %copy-start.3 = (bf16[3,3,3,32]{3,2,1,0:T(4,128)(2,1)S(1)}, bf16[3,3,3,32]{3,2,1,0:T(4,128)(2,1)}, u32[]{:S(2)}) copy-start(bf16[3,3,3,32]{3,2,1,0:T(4,128)(2,1)} %first.1) | copy-start | bytes 5188
  3.6 50.9 %copy-start.4 = (bf16[3,3,3,32]{3,2,1,0:T(4,128)(2,1)S(1)}, bf16[3,3,3,32]{3,2,1,0:T(4,128)(2,1)}, u32[]{:S(2)}) copy-start(bf16[3,3,3,32]{3,2,1,0:T(4,128)(2,1)} %last.1) | copy-start | bytes 5188
  14.0 5.1 %collective-permute-start.3 = (bf16[256,128]{1,0:T(8,128)(2,1)S(1)}, bf16[256,128]{1,0:T(8,128)(2,1)S(1)}, u32[]{:S(2)}, u32[]{:S(2)}) collective-permute-start(bf16[256,128]{1,0:T(8,128)(2,1)S(1)} %get-tuple-element.37), channel_id=1, source_target_pairs={{0,16},{16,0},{1,17},{17,1},{2,18},{18,2},{3,19},{19,3},{4,20},{20... | collective-permute-start | bytes 196616 | tf_op jit(solution)/shard_map/ppermute | solution.py:644
  19.2 4.1 %collective-permute-start.6 = (bf16[256,128]{1,0:T(8,128)(2,1)S(1)}, bf16[256,128]{1,0:T(8,128)(2,1)S(1)}, u32[]{:S(2)}, u32[]{:S(2)}) collective-permute-start(bf16[256,128]{1,0:T(8,128)(2,1)S(1)} %add_convert_fusion.5), channel_id=1, source_target_pairs={{0,12},{4,0},{8,4},{12,8},{1,13},{5,1},{9,5},{13,9},{2,14},{6,2},{... | collective-permute-start | bytes 196616 | tf_op jit(solution)/shard_map/ppermute | solution.py:644
  22.0 4.7 %collective-permute-start.5 = (bf16[256,128]{1,0:T(8,128)(2,1)S(1)}, bf16[256,128]{1,0:T(8,128)(2,1)S(1)}, u32[]{:S(2)}, u32[]{:S(2)}) collective-permute-start(bf16[256,128]{1,0:T(8,128)(2,1)S(1)} %add_convert_fusion.5), channel_id=1, source_target_pairs={{0,8},{4,12},{8,0},{12,4},{1,9},{5,13},{9,1},{13,5},{2,10},{6,14},... | collective-permute-start | bytes 196616 | tf_op jit(solution)/shard_map/ppermute | solution.py:644
  22.3 5.0 %collective-permute-start.4 = (bf16[256,128]{1,0:T(8,128)(2,1)S(1)}, bf16[256,128]{1,0:T(8,128)(2,1)S(1)}, u32[]{:S(2)}, u32[]{:S(2)}) collective-permute-start(bf16[256,128]{1,0:T(8,128)(2,1)S(1)} %add_convert_fusion.5), channel_id=1, source_target_pairs={{0,4},{4,8},{8,12},{12,0},{1,5},{5,9},{9,13},{13,1},{2,6},{6,10},{... | collective-permute-start | bytes 196616 | tf_op jit(solution)/shard_map/ppermute | solution.py:644
  27.4 10.3 %collective-permute-start.11 = (bf16[256,128]{1,0:T(8,128)(2,1)S(1)}, bf16[256,128]{1,0:T(8,128)(2,1)S(1)}, u32[]{:S(2)}, u32[]{:S(2)}) collective-permute-start(bf16[256,128]{1,0:T(8,128)(2,1)S(1)} %add_convert_fusion.4), channel_id=1, source_target_pairs={{0,3},{1,0},{2,1},{3,2},{4,7},{5,4},{6,5},{7,6},{8,11},{9,8},{10,9... | collective-permute-start | bytes 196616 | tf_op jit(solution)/shard_map/ppermute | solution.py:644
  31.2 6.5 %collective-permute-start.10 = (bf16[256,128]{1,0:T(8,128)(2,1)S(1)}, bf16[256,128]{1,0:T(8,128)(2,1)S(1)}, u32[]{:S(2)}, u32[]{:S(2)}) collective-permute-start(bf16[256,128]{1,0:T(8,128)(2,1)S(1)} %add_convert_fusion.4), channel_id=1, source_target_pairs={{0,2},{1,3},{2,0},{3,1},{4,6},{5,7},{6,4},{7,5},{8,10},{9,11},{10,... | collective-permute-start | bytes 196616 | tf_op jit(solution)/shard_map/ppermute | solution.py:644
  31.2 6.5 %collective-permute-start.9 = (bf16[256,128]{1,0:T(8,128)(2,1)S(1)}, bf16[256,128]{1,0:T(8,128)(2,1)S(1)}, u32[]{:S(2)}, u32[]{:S(2)}) collective-permute-start(bf16[256,128]{1,0:T(8,128)(2,1)S(1)} %add_convert_fusion.4), channel_id=1, source_target_pairs={{0,1},{1,2},{2,3},{3,0},{4,5},{5,6},{6,7},{7,4},{8,9},{9,10},{10,1... | collective-permute-start | bytes 196616 | tf_op jit(solution)/shard_map/ppermute | solution.py:644
  31.9 5.9 %collective-permute-start.8 = (f32[4,4,512]{2,1,0:T(4,128)S(1)}, f32[4,4,512]{2,1,0:T(4,128)S(1)}, u32[]{:S(2)}, u32[]{:S(2)}) collective-permute-start(f32[4,4,512]{2,1,0:T(4,128)S(1)} %get-tuple-element.67), channel_id=1, source_target_pairs={{33,32},{34,33},{35,34},{36,35},{37,36},{38,37},{39,38},{40,39},{4... | collective-permute-start | bytes 98312 | tf_op jit(solution)/shard_map/ppermute | solution.py:653
  33.2 5.5 %collective-permute-start.7 = (f32[4,4,512]{2,1,0:T(4,128)S(1)}, f32[4,4,512]{2,1,0:T(4,128)S(1)}, u32[]{:S(2)}, u32[]{:S(2)}) collective-permute-start(f32[4,4,512]{2,1,0:T(4,128)S(1)} %get-tuple-element.68), channel_id=1, source_target_pairs={{32,33},{33,34},{34,35},{35,36},{36,37},{37,38},{38,39},{39,40},{4... | collective-permute-start | bytes 98312 | tf_op jit(solution)/shard_map/ppermute | solution.py:652
  44.0 14.3 %collective-permute-start.12 = (bf16[256,128]{1,0:T(8,128)(2,1)S(1)}, bf16[256,128]{1,0:T(8,128)(2,1)S(1)}, u32[]{:S(2)}, u32[]{:S(2)}) collective-permute-start(bf16[256,128]{1,0:T(8,128)(2,1)S(1)} %get-tuple-element.49), channel_id=1, source_target_pairs={{0,16},{16,0},{1,17},{17,1},{2,18},{18,2},{3,19},{19,3},{4,20},{20... | collective-permute-start | bytes 196616 | tf_op jit(solution)/shard_map/ppermute | solution.py:644
  58.4 6.8 %collective-permute-start.15 = (bf16[256,128]{1,0:T(8,128)(2,1)S(1)}, bf16[256,128]{1,0:T(8,128)(2,1)S(1)}, u32[]{:S(2)}, u32[]{:S(2)}) collective-permute-start(bf16[256,128]{1,0:T(8,128)(2,1)S(1)} %add_convert_fusion.2), channel_id=1, source_target_pairs={{0,12},{4,0},{8,4},{12,8},{1,13},{5,1},{9,5},{13,9},{2,14},{6,2},{... | collective-permute-start | bytes 196616 | tf_op jit(solution)/shard_map/ppermute | solution.py:644
  58.5 6.7 %collective-permute-start.14 = (bf16[256,128]{1,0:T(8,128)(2,1)S(1)}, bf16[256,128]{1,0:T(8,128)(2,1)S(1)}, u32[]{:S(2)}, u32[]{:S(2)}) collective-permute-start(bf16[256,128]{1,0:T(8,128)(2,1)S(1)} %add_convert_fusion.2), channel_id=1, source_target_pairs={{0,8},{4,12},{8,0},{12,4},{1,9},{5,13},{9,1},{13,5},{2,10},{6,14},... | collective-permute-start | bytes 196616 | tf_op jit(solution)/shard_map/ppermute | solution.py:644
  58.6 6.6 %collective-permute-start.13 = (bf16[256,128]{1,0:T(8,128)(2,1)S(1)}, bf16[256,128]{1,0:T(8,128)(2,1)S(1)}, u32[]{:S(2)}, u32[]{:S(2)}) collective-permute-start(bf16[256,128]{1,0:T(8,128)(2,1)S(1)} %add_convert_fusion.2), channel_id=1, source_target_pairs={{0,4},{4,8},{8,12},{12,0},{1,5},{5,9},{9,13},{13,1},{2,6},{6,10},{... | collective-permute-start | bytes 196616 | tf_op jit(solution)/shard_map/ppermute | solution.py:644
  65.2 4.2 %collective-permute-start.18 = (bf16[256,128]{1,0:T(8,128)(2,1)S(1)}, bf16[256,128]{1,0:T(8,128)(2,1)S(1)}, u32[]{:S(2)}, u32[]{:S(2)}) collective-permute-start(bf16[256,128]{1,0:T(8,128)(2,1)S(1)} %add_convert_fusion.1), channel_id=1, source_target_pairs={{0,3},{1,0},{2,1},{3,2},{4,7},{5,4},{6,5},{7,6},{8,11},{9,8},{10,9... | collective-permute-start | bytes 196616 | tf_op jit(solution)/shard_map/ppermute | solution.py:644
  65.3 4.7 %collective-permute-start.17 = (bf16[256,128]{1,0:T(8,128)(2,1)S(1)}, bf16[256,128]{1,0:T(8,128)(2,1)S(1)}, u32[]{:S(2)}, u32[]{:S(2)}) collective-permute-start(bf16[256,128]{1,0:T(8,128)(2,1)S(1)} %add_convert_fusion.1), channel_id=1, source_target_pairs={{0,2},{1,3},{2,0},{3,1},{4,6},{5,7},{6,4},{7,5},{8,10},{9,11},{10,... | collective-permute-start | bytes 196616 | tf_op jit(solution)/shard_map/ppermute | solution.py:644
  65.4 5.4 %collective-permute-start.16 = (bf16[256,128]{1,0:T(8,128)(2,1)S(1)}, bf16[256,128]{1,0:T(8,128)(2,1)S(1)}, u32[]{:S(2)}, u32[]{:S(2)}) collective-permute-start(bf16[256,128]{1,0:T(8,128)(2,1)S(1)} %add_convert_fusion.1), channel_id=1, source_target_pairs={{0,1},{1,2},{2,3},{3,0},{4,5},{5,6},{6,7},{7,4},{8,9},{9,10},{10,1... | collective-permute-start | bytes 196616 | tf_op jit(solution)/shard_map/ppermute | solution.py:644

commit v4 on v3

--- a/solution.py
+++ b/solution.py
@@ -13,6 +13,7 @@
 VMEM_LIMIT = 32 << 20
 TOGETHER = 4
 UNROLL = 16
+RIM = 4
 CHUNK = 64
 PIECES = ((0,), (1, 2), (3,))
 SPAN = 6
@@ -139,7 +140,15 @@
         def _():
             total[mine] = total[mine] - sino_ref[:, z, :]
 
-    o_ref[...] = total[0 : acc.shape[0]].astype(o_ref.dtype)
+    o_ref[0 : acc.shape[0]] = total[0 : acc.shape[0]].astype(o_ref.dtype)
+
+
+def in_pieces(cur, first):
+    pieces = []
+    for z in range(cur.shape[0]):
+        for c in range(cur.shape[2] // 128):
+            pieces.append(cur[z, first : first + RIM, c * 128 : c * 128 + 128])
+    return jnp.concatenate(pieces, axis=0)
 
 
 def project_kernel(
@@ -159,7 +168,7 @@
     angle,
     detector,
     tile,
-    first_slice,
+    cur,
     sino,
     pix,
     acc,
@@ -171,7 +180,7 @@
         pltpu.make_async_copy(source, target, small_sems.at[n])
         for n, (source, target) in enumerate(
             [
-                (states_in.at[0, 0], first_slice),
+                (states_in.at[0], cur),
                 (angle_in, angle),
                 (detector_in, detector),
                 (tile_in, tile),
@@ -202,14 +211,22 @@
     acc[...] = jnp.zeros_like(acc)
     for copy in small:
         copy.wait()
-    for k, value in enumerate((first_slice, got_1, got_2, got_3)):
-
-        @pl.when(place_ref[0] == k)
+    @pl.when(place_ref[0] == 0)
+    def _():
+        start_ref[...] = cur[0]
+
+    for k, value in enumerate((got_1, got_2, got_3)):
+
+        @pl.when(place_ref[0] == k + 1)
         def _():
             start_ref[...] = value[...]
 
+    rows = acc.shape[0]
+    edge = RIM * cur.shape[0] * cur.shape[2] // 128
+    o_ref[rows : rows + edge] = in_pieces(cur, cur.shape[1] - RIM).astype(BF16)
+    o_ref[rows + edge :] = in_pieces(cur, 0).astype(BF16)
     load_pixels(start_ref[...], pix)
-    wide = first_slice.shape[1] // 128
+    wide = cur.shape[2] // 128
     project_blocks(
         lambda b: angle[b] * wide + detector[b],
         tile,
@@ -224,12 +241,13 @@
 def project(place, angle, detector, tile, states, got, sinogram, blocks, ray_total):
     shape = got[0].shape
     count = blocks.shape[0]
+    edge = RIM * states.shape[1] * states.shape[3] // 128
     far = pl.BlockSpec(memory_space=pltpu.HBM)
     stay = lambda x: pltpu.with_memory_space_constraint(x, pltpu.HBM)
     return pl.pallas_call(
         project_kernel,
         out_shape=(
-            jax.ShapeDtypeStruct((ray_total, 128), BF16),
+            jax.ShapeDtypeStruct((ray_total + 2 * edge, 128), BF16),
             jax.ShapeDtypeStruct(shape, F32),
             pltpu.VMEM(blocks.shape, BF16),
         ),
@@ -239,7 +257,7 @@
             pltpu.SMEM((count,), jnp.int32),
             pltpu.SMEM((count,), jnp.int32),
             pltpu.SMEM((count,), jnp.int32),
-            pltpu.VMEM(shape, F32),
+            pltpu.VMEM(states.shape[1:], F32),
             pltpu.VMEM(sinogram.shape, F32),
             pltpu.VMEM((shape[0] * shape[1] // 128 + 8, 128), F32),
             pltpu.VMEM((ray_total, 8, 128), F32),
@@ -424,11 +442,16 @@
 def prepare_kernel(
     place_ref, before, after, cur, first, hidden, last, rim, zf, zh, zl, zw, zm, af, ah, al, turn
 ):
-    depth = before.shape[1]
     rows = cur.shape[1]
-    rim[:, 0:depth] = before[...].astype(BF16).astype(F32)
-    rim[:, depth : depth + rows] = cur[...].astype(BF16).astype(F32)
-    rim[:, depth + rows :] = after[...].astype(BF16).astype(F32)
+    wide = cur.shape[2] // 128
+    rim[:, RIM : RIM + rows] = cur[...].astype(BF16).astype(F32)
+    above = jnp.where(place_ref[1] > 0, before[...].astype(F32), 0.0)
+    below = jnp.where(place_ref[1] < place_ref[2] - 1, after[...].astype(F32), 0.0)
+    for z in range(cur.shape[0]):
+        for c in range(wide):
+            n = (z * wide + c) * RIM
+            rim[z, 0:RIM, c * 128 : c * 128 + 128] = above[n : n + RIM]
+            rim[z, RIM + rows :, c * 128 : c * 128 + 128] = below[n : n + RIM]
 
     @pl.when(place_ref[0] == 1)
     def _():
@@ -447,8 +470,7 @@
 def prepare(place, rim, current, first, hidden, last):
     layers = hidden.shape[1]
     slices, rows, columns = current.shape
-    depth = rim[0].shape[1]
-    whole = jax.ShapeDtypeStruct((slices, rows + 2 * depth, columns), F32)
+    whole = jax.ShapeDtypeStruct((slices, rows + 2 * RIM, columns), F32)
     shapes = [
         (128, 16),
         (layers, 128, 384),
@@ -645,13 +667,27 @@
     return total.astype(values.dtype)
 
 
-def rims(cells, depth):
-    count = lax.axis_size("tile")
-    pairs = [(a * count + t, a * count + t + 1) for a in (1, 2) for t in range(count - 1)]
-    both = ("agent", "tile")
-    before = lax.ppermute(cells[:, cells.shape[1] - depth :], both, pairs)
-    after = lax.ppermute(cells[:, 0:depth], both, [(b, a) for a, b in pairs])
-    return before, after
+def added_up_with_rims(sums, groups, ends):
+    far, strided, near = groups
+    rows = sums.shape[0] * 2 // 3
+    edge = (sums.shape[0] - rows) // 2
+    got = lax.ppermute(sums, "tile", swapped(far, 1))
+    tail, head = sums[rows : rows + edge], sums[rows + edge :]
+    onward, backward = got[rows : rows + edge], got[rows + edge :]
+    sums = (sums[0:rows].astype(F32) + got[0:rows].astype(F32)).astype(BF16)
+    for n, group in enumerate((strided, near)):
+        first, last = ends[n]
+        onward = jnp.where(last, onward, tail)
+        backward = jnp.where(first, backward, head)
+        sums, onward, backward = lax.optimization_barrier((sums, onward, backward))
+        up = lax.ppermute(jnp.concatenate([sums, onward]), "tile", swapped(group, 1))
+        across = lax.ppermute(sums, "tile", swapped(group, 2))
+        down = lax.ppermute(jnp.concatenate([sums, backward]), "tile", swapped(group, 3))
+        onward, backward = up[rows:], down[rows:]
+        total = sums.astype(F32) + up[0:rows].astype(F32)
+        total = total + across.astype(F32) + down[0:rows].astype(F32)
+        sums = total.astype(BF16)
+    return sums, (onward, backward)
 
 
 def slices_sent(current):
@@ -677,7 +713,9 @@
     ray_total = sinogram.shape[0] * tile_count
     ray_index = block_angle * (current.shape[2] // 128) + block_detector
 
-    got = slices_sent(current)
+    within = [lax.shift_right_logical(tile_place, 2) & 3, tile_place & 3]
+    ends = [(at == 0, at == 3) for at in within]
+    got, ends = lax.optimization_barrier((slices_sent(current), ends))
     sums, start, blocks_here = project(
         place, block_angle, block_detector, block_tile, states, got, sinogram, blocks, ray_total
     )
@@ -685,24 +723,21 @@
     groups = stage_groups(tile_count)
     net = jnp.zeros_like(current)
     x_data = start
-    for step in range(DATA_STEPS):
-        for n, group in enumerate(groups):
-            sums, net = lax.optimization_barrier((sums, net))
-            if step == DATA_STEPS - 1:
-                if n == 0:
-                    prepared = prepare(place, rim, current, conv_first, conv_hidden, conv_last)
-                for k in PIECES[n]:
-                    net = piece(k, place, blocks_here, net, prepared)
-            if step == DATA_STEPS - 2 and n == len(groups) - 1:
-                around, sums = lax.optimization_barrier((current, sums))
-                rim = rims(around, conv_hidden.shape[1] + 2)
-                rim, sums = lax.optimization_barrier((rim, added_up(sums, group)))
-            else:
-                sums = added_up(sums, group)
-        if step < DATA_STEPS - 1:
-            x_data, sums = back_project(
-                place, ray_index, block_tile, sums, x_data, sinogram, blocks_here
-            )
+    sums, rim = added_up_with_rims(sums, groups, ends)
+    for _ in range(DATA_STEPS - 2):
+        x_data, sums = back_project(
+            place, ray_index, block_tile, sums, x_data, sinogram, blocks_here
+        )
+        for group in groups:
+            sums = added_up(sums, group)
+    x_data, sums = back_project(place, ray_index, block_tile, sums, x_data, sinogram, blocks_here)
+    for n, group in enumerate(groups):
+        sums, net = lax.optimization_barrier((sums, net))
+        if n == 0:
+            prepared = prepare(place, rim, current, conv_first, conv_hidden, conv_last)
+        for k in PIECES[n]:
+            net = piece(k, place, blocks_here, net, prepared)
+        sums = added_up(sums, group)
     sent = back_reflect(ray_index, block_tile, sums, x_data, start, current, net, blocks_here)
     everything = lax.all_gather(sent, "agent")
     return finish(place, everything, current, net)[None]

time: 86.8 us -> 78.7 us (0.907)
  starting transfers between devices: 32.9 us -> 24.6 us
  waiting for transfers between devices: 14.1 us -> 15.7 us
  blocking collectives: 12 us -> 10.6 us
    ppermute x14 -> x7, starting transfers between devices: 24.5 us -> 8.58 us  [added_up(): total = total + lax.ppermute(values, 'tile', swapped(groups, k)).astype(F32)]
    ppermute x2 -> x7, waiting for transfers between devices: 0.92 us -> 9.03 us  [the longest x2 3.49 us: added_up_with_rims(): across = lax.ppermute(sums, 'tile', swapped(group, 2))]
    ppermute x2 -> x7, starting transfers between devices: 5.77 us -> 13.4 us  [the longest x2 5.24 us: added_up_with_rims(): across = lax.ppermute(sums, 'tile', swapped(group, 2))]
    ppermute x14 -> x7, waiting for transfers between devices: 8.31 us -> 1.76 us  [added_up(): total = total + lax.ppermute(values, 'tile', swapped(groups, k)).astype(F32)]
    all_gather x1, blocking collectives: 12 us -> 10.6 us  [per_device(): everything = lax.all_gather(sent, 'agent')]
  transfers between devices with their start and end apart: 19 -> 17, of which waited for: 8 -> 6; matrix products, arithmetic and copies ran while one was open for 0% -> 0% of each run, Pallas kernels for 13% -> 15%
where the time goes in v4:
time: 78.7 us; the launch traced here: 78.4 us
  Pallas kernels  26.1 us (33%)
  starting transfers between devices  24.6 us (31%)
  waiting for transfers between devices  15.7 us (20%)
  blocking collectives  10.6 us (13%)
  local copies, waits for them, and re-layouts  0.87 us (1%)
    all_gather x1, blocking collectives, per_device(): everything = lax.all_gather(sent, 'agent')  10.6 us
    pallas_call x4, Pallas kernels, piece(): pl.pallas_call(functools.partial(piece_kernel, k), out_shape=jax.ShapeDty...  10.5 us
    ppermute x7, starting transfers between devices, added_up(): total = total + lax.ppermute(values, 'tile', swapped(groups, k)).astype(F32)  8.58 us
    pallas_call x1, Pallas kernels, project(): pl.pallas_call(project_kernel, out_shape=(jax.ShapeDtypeStruct((ray_total...  5.55 us
    pallas_call x1, Pallas kernels, back_project(): pl.pallas_call(back_project_kernel, out_shape=(jax.ShapeDtypeStruct(x.sha...  5.29 us
    ppermute x2, starting transfers between devices, added_up_with_rims(): across = lax.ppermute(sums, 'tile', swapped(group, 2))  5.24 us
    ppermute x3, waiting for transfers between devices, slices_sent(): lax.ppermute(current[k], 'agent', [(0, k)])  4.87 us
    ppermute x2, waiting for transfers between devices, added_up_with_rims(): across = lax.ppermute(sums, 'tile', swapped(group, 2))  3.49 us
  transfers between devices with their start and end apart: 17, of which 6 were waited for; matrix products, arithmetic and copies ran while one was open for 0% of the time, Pallas kernels for 15%

profile of v4, /device:TPU:1, one launch (start us, length us, event | category | flops | bytes accessed | tf_op | source)
XLA Modules:
  0.0 78.4 jit_solution(9058192061702521166)
XLA Ops:
  0.0 0.0 copy-start.5
  0.0 0.0 copy-start.6
  0.0 0.0 copy-start.7
  0.0 0.0 copy-start.2
  0.0 0.8 %slice_bitcast_fusion = (f32[16,512]{1,0:T(8,128)S(1)}, f32[16,512]{1,0:T(8,128)S(1)}, f32[16,512]{1,0:T(8,128)S(1)}) fusion(f32[1,4,16,512]{3,2,1,0:T(8,128)} %states_in.1), kind=kLoop, calls=%fused_computation.10 | loop fusion | bytes 196608 | tf_op jit(solution)/shard_map/squeeze | solution.py:694
  0.8 0.7 collective-permute-start.2
  1.5 0.7 collective-permute-start.1
  2.2 1.3 %collective-permute-start = (f32[16,512]{1,0:T(8,128)S(1)}, f32[16,512]{1,0:T(8,128)S(1)}, u32[]{:S(2)}, u32[]{:S(2)}) collective-permute-start(f32[16,512]{1,0:T(8,128)S(1)} %get-tuple-element.75), channel_id=1, source_target_pairs={{0,32},{1,33},{2,34},{3,35},{4,36},{5,37},{6,38},{7,39},{8,40},{9,... | collective-permute-start | bytes 98312 | tf_op jit(solution)/shard_map/ppermute | solution.py:694
  3.5 0.1 pad_add_fusion.place_ref
  3.6 0.0 copy-start
  3.6 0.0 copy-start.1
  3.6 0.0 copy-start.3
  3.6 0.0 copy-start.4
  3.6 0.0 collective-permute-done.2.got_3
  3.6 0.0 collective-permute-done.1.got_2
  3.6 4.9 %collective-permute-done.got_1 = f32[16,512]{1,0:T(8,128)S(1)} collective-permute-done((f32[16,512]{1,0:T(8,128)S(1)}, f32[16,512]{1,0:T(8,128)S(1)}, u32[]{:S(2)}, u32[]{:S(2)}) %collective-permute-start) | collective-permute-done | bytes 32800 | tf_op jit(solution)/shard_map/ppermute | solution.py:694
  8.5 5.6 %project.1 = (bf16[384,128]{1,0:T(8,128)(2,1)S(1)}, f32[16,512]{1,0:T(8,128)S(1)}, bf16[256,128,128]{2,1,0:T(8,128)(2,1)S(1)}) custom-call(s32[3]{0:T(128)S(1)} %pad_add_fusion.place_ref, s32[256]{0:T(256)} %angle_in.1, s32[256]{0:T(256)} %detector_in.1, s32[256]{0:T(256)} %tile_ref.3, f32[1,4,16,512]{3,2,1,0:T(8,128)} %states_in.1, ...), custom_call_target="tpu_custom_call" | custom-call | tf_op jit(solution)/shard_map/project/pallas_call | solution.py:247
  14.0 2.5 %collective-permute-start.3 = (bf16[384,128]{1,0:T(8,128)(2,1)S(1)}, bf16[384,128]{1,0:T(8,128)(2,1)S(1)}, u32[]{:S(2)}, u32[]{:S(2)}) collective-permute-start(bf16[384,128]{1,0:T(8,128)(2,1)S(1)} %get-tuple-element.41), channel_id=1, source_target_pairs={{0,16},{16,0},{1,17},{17,1},{2,18},{18,2},{3,19},{19,3},{4,20},{20... | collective-permute-start | bytes 294920 | tf_op jit(solution)/shard_map/ppermute | solution.py:674
  16.5 3.3 %collective-permute-done.3 = bf16[384,128]{1,0:T(8,128)(2,1)S(1)} collective-permute-done((bf16[384,128]{1,0:T(8,128)(2,1)S(1)}, bf16[384,128]{1,0:T(8,128)(2,1)S(1)}, u32[]{:S(2)}, u32[]{:S(2)}) %collective-permute-start.3) | collective-permute-done | bytes 98336 | tf_op jit(solution)/shard_map/ppermute | solution.py:674
  19.9 1.4 %collective-permute-start.4 = (bf16[320,128]{1,0:T(8,128)(2,1)S(1)}, bf16[320,128]{1,0:T(8,128)(2,1)S(1)}, u32[]{:S(2)}, u32[]{:S(2)}) collective-permute-start(bf16[320,128]{1,0:T(8,128)(2,1)S(1)} %get-tuple-element.80), channel_id=1, source_target_pairs={{0,4},{4,8},{8,12},{12,0},{1,5},{5,9},{9,13},{13,1},{2,6},{6,10},{... | collective-permute-start | bytes 245768 | tf_op jit(solution)/shard_map/ppermute | solution.py:683
  21.3 1.5 %collective-permute-start.6 = (bf16[320,128]{1,0:T(8,128)(2,1)S(1)}, bf16[320,128]{1,0:T(8,128)(2,1)S(1)}, u32[]{:S(2)}, u32[]{:S(2)}) collective-permute-start(bf16[320,128]{1,0:T(8,128)(2,1)S(1)} %get-tuple-element.81), channel_id=1, source_target_pairs={{0,12},{4,0},{8,4},{12,8},{1,13},{5,1},{9,5},{13,9},{2,14},{6,2},{... | collective-permute-start | bytes 245768 | tf_op jit(solution)/shard_map/ppermute | solution.py:685
  22.8 1.6 %collective-permute-start.5 = (bf16[256,128]{1,0:T(8,128)(2,1)S(1)}, bf16[256,128]{1,0:T(8,128)(2,1)S(1)}, u32[]{:S(2)}, u32[]{:S(2)}) collective-permute-start(bf16[256,128]{1,0:T(8,128)(2,1)S(1)} %add_convert_fusion.5), channel_id=1, source_target_pairs={{0,8},{4,12},{8,0},{12,4},{1,9},{5,13},{9,1},{13,5},{2,10},{6,14},... | collective-permute-start | bytes 196616 | tf_op jit(solution)/shard_map/ppermute | solution.py:684
  24.4 3.5 %collective-permute-done.5 = bf16[256,128]{1,0:T(8,128)(2,1)S(1)} collective-permute-done((bf16[256,128]{1,0:T(8,128)(2,1)S(1)}, bf16[256,128]{1,0:T(8,128)(2,1)S(1)}, u32[]{:S(2)}, u32[]{:S(2)}) %collective-permute-start.5) | collective-permute-done | bytes 65568 | tf_op jit(solution)/shard_map/ppermute | solution.py:684
  27.9 0.0 collective-permute-done.4
  27.9 0.0 collective-permute-done.6
  27.9 3.7 %collective-permute-start.8 = (bf16[256,128]{1,0:T(8,128)(2,1)S(1)}, bf16[256,128]{1,0:T(8,128)(2,1)S(1)}, u32[]{:S(2)}, u32[]{:S(2)}) collective-permute-start(bf16[256,128]{1,0:T(8,128)(2,1)S(1)} %add_convert_fusion.4), channel_id=1, source_target_pairs={{0,2},{1,3},{2,0},{3,1},{4,6},{5,7},{6,4},{7,5},{8,10},{9,11},{10,... | collective-permute-start | bytes 196616 | tf_op jit(solution)/shard_map/ppermute | solution.py:684
  31.6 0.8 %collective-permute-start.7 = (bf16[320,128]{1,0:T(8,128)(2,1)S(1)}, bf16[320,128]{1,0:T(8,128)(2,1)S(1)}, u32[]{:S(2)}, u32[]{:S(2)}) collective-permute-start(bf16[320,128]{1,0:T(8,128)(2,1)S(1)} %get-tuple-element.78), channel_id=1, source_target_pairs={{0,1},{1,2},{2,3},{3,0},{4,5},{5,6},{6,7},{7,4},{8,9},{9,10},{10,1... | collective-permute-start | bytes 245768 | tf_op jit(solution)/shard_map/ppermute | solution.py:683
  32.4 1.9 %collective-permute-start.9 = (bf16[320,128]{1,0:T(8,128)(2,1)S(1)}, bf16[320,128]{1,0:T(8,128)(2,1)S(1)}, u32[]{:S(2)}, u32[]{:S(2)}) collective-permute-start(bf16[320,128]{1,0:T(8,128)(2,1)S(1)} %get-tuple-element.79), channel_id=1, source_target_pairs={{0,3},{1,0},{2,1},{3,2},{4,7},{5,4},{6,5},{7,6},{8,11},{9,8},{10,9... | collective-permute-start | bytes 245768 | tf_op jit(solution)/shard_map/ppermute | solution.py:685
  34.4 0.0 copy-done.6
  34.4 0.0 copy-done.7
  34.4 0.0 collective-permute-done.8
  34.4 2.2 %collective-permute-done.7 = bf16[320,128]{1,0:T(8,128)(2,1)S(1)} collective-permute-done((bf16[320,128]{1,0:T(8,128)(2,1)S(1)}, bf16[320,128]{1,0:T(8,128)(2,1)S(1)}, u32[]{:S(2)}, u32[]{:S(2)}) %collective-permute-start.7) | collective-permute-done | bytes 81952 | tf_op jit(solution)/shard_map/ppermute | solution.py:683
  36.6 0.0 collective-permute-done.9
  36.7 0.0 copy-done.5
  36.7 0.0 copy-done.2
  36.7 5.3 %back_project.1 = (f32[16,512]{1,0:T(8,128)S(1)}, bf16[256,128]{1,0:T(8,128)(2,1)S(1)}) custom-call(s32[3]{0:T(128)S(1)} %pad_add_fusion.place_ref, s32[256]{0:T(256)S(1)} %multiply_add_fusion.ray_ref, s32[256]{0:T(256)S(1)} %copy-done.5, bf16[256,128]{1,0:T(8,128)(2,1)S(1)} %add_convert_fusion.3.r_ref, f32[16,512]{1,0:T(8,128)S(1)} %get-tuple-element.52.x_ref.start_ref, ...), custom_call_target="tpu_custom_call" | custom-call | tf_op jit(solution)/shard_map/back_project/pallas_call | solution.py:299
  42.0 2.5 %collective-permute-start.10 = (bf16[256,128]{1,0:T(8,128)(2,1)S(1)}, bf16[256,128]{1,0:T(8,128)(2,1)S(1)}, u32[]{:S(2)}, u32[]{:S(2)}) collective-permute-start(bf16[256,128]{1,0:T(8,128)(2,1)S(1)} %get-tuple-element.55), channel_id=1, source_target_pairs={{0,16},{16,0},{1,17},{17,1},{2,18},{18,2},{3,19},{19,3},{4,20},{20... | collective-permute-start | bytes 196616 | tf_op jit(solution)/shard_map/ppermute | solution.py:666
  44.5 0.0 copy-done
  44.5 0.0 copy-done.1
  44.5 0.0 copy-done.3
  44.5 0.0 copy-done.4
  44.6 1.1 %prepare.1 = (f32[4,24,512]{2,1,0:T(8,128)S(1)}, bf16[128,16]{1,0:T(8,128)(2,1)S(1)}, bf16[2,128,384]{2,1,0:T(8,128)(2,1)S(1)}, bf16[8,384]{1,0:T(8,128)(2,1)S(1...) custom-call(s32[3]{0:T(128)S(1)} %pad_add_fusion.place_ref, ...), custom_call_target="tpu_custom_call" | custom-call | tf_op jit(solution)/shard_map/prepare/pallas_call | solution.py:484
  45.7 2.6 %piece_0.1.net = f32[4,16,512]{2,1,0:T(8,128)S(1)} custom-call(s32[3]{0:T(128)S(1)} %pad_add_fusion.place_ref, bf16[256,128,128]{2,1,0:T(8,128)(2,1)S(1)} %get-tuple-element.53.blk, f32[4,16,512]{2,1,0:T(8,128)S(1)} %broadcast_in_dim.6.net, f32[4,24,512]{2,1,0:T(8,128)S(1)} %get-tuple-element.57.rim, bf16[128,16]{1,0:T(8,128)(2,1)S(1)} %get-tuple-element.58.zf, ...), custom_call_target="tpu_custom_call" | custom-call | tf_op jit(solution)/shard_map/piece_0/pallas_call | solution.py:634
  48.3 0.0 collective-permute-done.10
  48.4 1.6 %collective-permute-start.13 = (bf16[256,128]{1,0:T(8,128)(2,1)S(1)}, bf16[256,128]{1,0:T(8,128)(2,1)S(1)}, u32[]{:S(2)}, u32[]{:S(2)}) collective-permute-start(bf16[256,128]{1,0:T(8,128)(2,1)S(1)} %add_convert_fusion.2), channel_id=1, source_target_pairs={{0,12},{4,0},{8,4},{12,8},{1,13},{5,1},{9,5},{13,9},{2,14},{6,2},{... | collective-permute-start | bytes 196616 | tf_op jit(solution)/shard_map/ppermute | solution.py:666
  50.0 0.1 collective-permute-start.12
  50.1 0.6 collective-permute-start.11
  50.7 2.6 %piece_1.1.net = f32[4,16,512]{2,1,0:T(8,128)S(1)} custom-call(s32[3]{0:T(128)S(1)} %pad_add_fusion.place_ref, bf16[256,128,128]{2,1,0:T(8,128)(2,1)S(1)} %get-tuple-element.53.blk, f32[4,16,512]{2,1,0:T(8,128)S(1)} %piece_0.1.net, f32[4,24,512]{2,1,0:T(8,128)S(1)} %get-tuple-element.57.rim, bf16[128,16]{1,0:T(8,128)(2,1)S(1)} %get-tuple-element.58.zf, ...), custom_call_target="tpu_custom_call" | custom-call | tf_op jit(solution)/shard_map/piece_1/pallas_call | solution.py:634
  53.3 2.6 %piece_2.1.net = f32[4,16,512]{2,1,0:T(8,128)S(1)} custom-call(s32[3]{0:T(128)S(1)} %pad_add_fusion.place_ref, bf16[256,128,128]{2,1,0:T(8,128)(2,1)S(1)} %get-tuple-element.53.blk, f32[4,16,512]{2,1,0:T(8,128)S(1)} %piece_1.1.net, f32[4,24,512]{2,1,0:T(8,128)S(1)} %get-tuple-element.57.rim, bf16[128,16]{1,0:T(8,128)(2,1)S(1)} %get-tuple-element.58.zf, ...), custom_call_target="tpu_custom_call" | custom-call | tf_op jit(solution)/shard_map/piece_2/pallas_call | solution.py:634
  56.0 0.0 collective-permute-done.13
  56.0 0.0 collective-permute-done.12
  56.0 0.0 collective-permute-done.11
  56.0 3.0 %collective-permute-start.16 = (bf16[256,128]{1,0:T(8,128)(2,1)S(1)}, bf16[256,128]{1,0:T(8,128)(2,1)S(1)}, u32[]{:S(2)}, u32[]{:S(2)}) collective-permute-start(bf16[256,128]{1,0:T(8,128)(2,1)S(1)} %add_convert_fusion.1), channel_id=1, source_target_pairs={{0,3},{1,0},{2,1},{3,2},{4,7},{5,4},{6,5},{7,6},{8,11},{9,8},{10,9... | collective-permute-start | bytes 196616 | tf_op jit(solution)/shard_map/ppermute | solution.py:666
  59.1 0.0 collective-permute-start.15
  59.1 0.7 collective-permute-start.14
  59.8 2.6 %piece_3.1.net_ref = f32[4,16,512]{2,1,0:T(8,128)S(1)} custom-call(s32[3]{0:T(128)S(1)} %pad_add_fusion.place_ref, bf16[256,128,128]{2,1,0:T(8,128)(2,1)S(1)} %get-tuple-element.53.blk, f32[4,16,512]{2,1,0:T(8,128)S(1)} %piece_2.1.net, f32[4,24,512]{2,1,0:T(8,128)S(1)} %get-tuple-element.57.rim, bf16[128,16]{1,0:T(8,128)(2,1)S(1)} %get-tuple-element.58.zf, ...), custom_call_target="tpu_custom_call" | custom-call | tf_op jit(solution)/shard_map/piece_3/pallas_call | solution.py:634
  62.4 0.0 collective-permute-done.16
  62.4 1.4 %collective-permute-done.15 = bf16[256,128]{1,0:T(8,128)(2,1)S(1)} collective-permute-done((bf16[256,128]{1,0:T(8,128)(2,1)S(1)}, bf16[256,128]{1,0:T(8,128)(2,1)S(1)}, u32[]{:S(2)}, u32[]{:S(2)}) %collective-permute-start.15) | collective-permute-done | bytes 65568 | tf_op jit(solution)/shard_map/ppermute | solution.py:666
  63.8 0.3 collective-permute-done.14
  64.2 2.4 %back_reflect.1 = bf16[5,16,512]{2,1,0:T(8,128)(2,1)S(1)} custom-call(s32[256]{0:T(256)S(1)} %multiply_add_fusion.ray_ref, s32[256]{0:T(256)S(1)} %copy-done.5, bf16[256,128]{1,0:T(8,128)(2,1)S(1)} %add_convert_fusion.r_ref, f32[16,512]{1,0:T(8,128)S(1)} %get-tuple-element.69.x_ref, f32[16,512]{1,0:T(8,128)S(1)} %get-tuple-element.52.x_ref.start_ref, ...), custom_call_target="tpu_custom_call" | custom-call | tf_op jit(solution)/shard_map/back_reflect/pallas_call | solution.py:330
  66.6 10.6 %all-gather = bf16[20,16,512]{2,1,0:T(8,128)(2,1)S(1)} all-gather(bf16[5,16,512]{2,1,0:T(8,128)(2,1)S(1)} %back_reflect.1), channel_id=2, replica_groups=mesh['agent'=4,'tile'=32] {'agent'}, dimensions={0}, use_global_device_ids=true | all-gather | bytes 409600 | tf_op jit(solution)/shard_map/all_gather | solution.py:742
  77.2 1.3 %finish.1 = f32[4,16,512]{2,1,0:T(8,128)} custom-call(s32[3]{0:T(128)S(1)} %pad_add_fusion.place_ref, bf16[4,5,16,512]{3,2,1,0:T(8,128)(2,1)S(1)} %bitcast.14, f32[4,16,512]{2,1,0:T(8,128)S(1)} %bitcast.13, f32[4,16,512]{2,1,0:T(8,128)S(1)} %piece_3.1.net_ref), custom_call_target="tpu_custom_call" | custom-call | tf_op jit(solution)/shard_map/finish/pallas_call | solution.py:361
  (14 shorter events, 0.3 us)
Async XLA Ops:
  0.0 36.7 %copy-start.5 = (s32[256]{0:T(256)S(1)}, s32[256]{0:T(256)}, u32[]{:S(2)}) copy-start(s32[256]{0:T(256)} %tile_ref.3) | copy-start | bytes 3076
  0.0 34.4 %copy-start.6 = (s32[256]{0:T(256)S(1)}, s32[256]{0:T(256)}, u32[]{:S(2)}) copy-start(s32[256]{0:T(256)} %detector_in.1) | copy-start | bytes 3076
  0.0 34.4 %copy-start.7 = (s32[256]{0:T(256)S(1)}, s32[256]{0:T(256)}, u32[]{:S(2)}) copy-start(s32[256]{0:T(256)} %angle_in.1) | copy-start | bytes 3076
  0.0 36.7 %copy-start.2 = (f32[8,4,128]{2,1,0:T(4,128)S(1)}, f32[8,4,128]{2,1,0:T(4,128)}, u32[]{:S(2)}) copy-start(f32[8,4,128]{2,1,0:T(4,128)} %sino_ref.1) | copy-start | bytes 49156
  0.8 2.7 %collective-permute-start.2 = (f32[16,512]{1,0:T(8,128)S(1)}, f32[16,512]{1,0:T(8,128)S(1)}, u32[]{:S(2)}, u32[]{:S(2)}) collective-permute-start(f32[16,512]{1,0:T(8,128)S(1)} %get-tuple-element.73), channel_id=1, source_target_pairs={{0,96},{1,97},{2,98},{3,99},{4,100},{5,101},{6,102},{7,103},{8,104... | collective-permute-start | bytes 98312 | tf_op jit(solution)/shard_map/ppermute | solution.py:694
  1.5 2.1 %collective-permute-start.1 = (f32[16,512]{1,0:T(8,128)S(1)}, f32[16,512]{1,0:T(8,128)S(1)}, u32[]{:S(2)}, u32[]{:S(2)}) collective-permute-start(f32[16,512]{1,0:T(8,128)S(1)} %get-tuple-element.74), channel_id=1, source_target_pairs={{0,64},{1,65},{2,66},{3,67},{4,68},{5,69},{6,70},{7,71},{8,72},{9,... | collective-permute-start | bytes 98312 | tf_op jit(solution)/shard_map/ppermute | solution.py:694
  2.2 6.3 %collective-permute-start = (f32[16,512]{1,0:T(8,128)S(1)}, f32[16,512]{1,0:T(8,128)S(1)}, u32[]{:S(2)}, u32[]{:S(2)}) collective-permute-start(f32[16,512]{1,0:T(8,128)S(1)} %get-tuple-element.75), channel_id=1, source_target_pairs={{0,32},{1,33},{2,34},{3,35},{4,36},{5,37},{6,38},{7,39},{8,40},{9,... | collective-permute-start | bytes 98312 | tf_op jit(solution)/shard_map/ppermute | solution.py:694
  3.6 41.0 %copy-start = (f32[1,4,16,512]{3,2,1,0:T(8,128)S(1)}, f32[1,4,16,512]{3,2,1,0:T(8,128)}, u32[]{:S(2)}) copy-start(f32[1,4,16,512]{3,2,1,0:T(8,128)} %states_in.1) | copy-start | bytes 393220
  3.6 41.0 %copy-start.1 = (bf16[3,2,3,3,32,32]{5,4,3,2,1,0:T(8,128)(2,1)S(1)}, bf16[3,2,3,3,32,32]{5,4,3,2,1,0:T(8,128)(2,1)}, u32[]{:S(2)}) copy-start(bf16[3,2,3,3,32,32]{5,4,3,2,1,0:T(8,128)(2,1)} %hidden.1) | copy-start | bytes 331780
  3.6 41.0 %copy-start.3 = (bf16[3,3,3,32]{3,2,1,0:T(4,128)(2,1)S(1)}, bf16[3,3,3,32]{3,2,1,0:T(4,128)(2,1)}, u32[]{:S(2)}) copy-start(bf16[3,3,3,32]{3,2,1,0:T(4,128)(2,1)} %first.1) | copy-start | bytes 5188
  3.6 41.0 %copy-start.4 = (bf16[3,3,3,32]{3,2,1,0:T(4,128)(2,1)S(1)}, bf16[3,3,3,32]{3,2,1,0:T(4,128)(2,1)}, u32[]{:S(2)}) copy-start(bf16[3,3,3,32]{3,2,1,0:T(4,128)(2,1)} %last.1) | copy-start | bytes 5188
  14.0 5.8 %collective-permute-start.3 = (bf16[384,128]{1,0:T(8,128)(2,1)S(1)}, bf16[384,128]{1,0:T(8,128)(2,1)S(1)}, u32[]{:S(2)}, u32[]{:S(2)}) collective-permute-start(bf16[384,128]{1,0:T(8,128)(2,1)S(1)} %get-tuple-element.41), channel_id=1, source_target_pairs={{0,16},{16,0},{1,17},{17,1},{2,18},{18,2},{3,19},{19,3},{4,20},{20... | collective-permute-start | bytes 294920 | tf_op jit(solution)/shard_map/ppermute | solution.py:674
  19.9 7.9 %collective-permute-start.4 = (bf16[320,128]{1,0:T(8,128)(2,1)S(1)}, bf16[320,128]{1,0:T(8,128)(2,1)S(1)}, u32[]{:S(2)}, u32[]{:S(2)}) collective-permute-start(bf16[320,128]{1,0:T(8,128)(2,1)S(1)} %get-tuple-element.80), channel_id=1, source_target_pairs={{0,4},{4,8},{8,12},{12,0},{1,5},{5,9},{9,13},{13,1},{2,6},{6,10},{... | collective-permute-start | bytes 245768 | tf_op jit(solution)/shard_map/ppermute | solution.py:683
  21.3 6.6 %collective-permute-start.6 = (bf16[320,128]{1,0:T(8,128)(2,1)S(1)}, bf16[320,128]{1,0:T(8,128)(2,1)S(1)}, u32[]{:S(2)}, u32[]{:S(2)}) collective-permute-start(bf16[320,128]{1,0:T(8,128)(2,1)S(1)} %get-tuple-element.81), channel_id=1, source_target_pairs={{0,12},{4,0},{8,4},{12,8},{1,13},{5,1},{9,5},{13,9},{2,14},{6,2},{... | collective-permute-start | bytes 245768 | tf_op jit(solution)/shard_map/ppermute | solution.py:685
  22.8 5.1 %collective-permute-start.5 = (bf16[256,128]{1,0:T(8,128)(2,1)S(1)}, bf16[256,128]{1,0:T(8,128)(2,1)S(1)}, u32[]{:S(2)}, u32[]{:S(2)}) collective-permute-start(bf16[256,128]{1,0:T(8,128)(2,1)S(1)} %add_convert_fusion.5), channel_id=1, source_target_pairs={{0,8},{4,12},{8,0},{12,4},{1,9},{5,13},{9,1},{13,5},{2,10},{6,14},... | collective-permute-start | bytes 196616 | tf_op jit(solution)/shard_map/ppermute | solution.py:684
  27.9 6.5 %collective-permute-start.8 = (bf16[256,128]{1,0:T(8,128)(2,1)S(1)}, bf16[256,128]{1,0:T(8,128)(2,1)S(1)}, u32[]{:S(2)}, u32[]{:S(2)}) collective-permute-start(bf16[256,128]{1,0:T(8,128)(2,1)S(1)} %add_convert_fusion.4), channel_id=1, source_target_pairs={{0,2},{1,3},{2,0},{3,1},{4,6},{5,7},{6,4},{7,5},{8,10},{9,11},{10,... | collective-permute-start | bytes 196616 | tf_op jit(solution)/shard_map/ppermute | solution.py:684
  31.6 5.0 %collective-permute-start.7 = (bf16[320,128]{1,0:T(8,128)(2,1)S(1)}, bf16[320,128]{1,0:T(8,128)(2,1)S(1)}, u32[]{:S(2)}, u32[]{:S(2)}) collective-permute-start(bf16[320,128]{1,0:T(8,128)(2,1)S(1)} %get-tuple-element.78), channel_id=1, source_target_pairs={{0,1},{1,2},{2,3},{3,0},{4,5},{5,6},{6,7},{7,4},{8,9},{9,10},{10,1... | collective-permute-start | bytes 245768 | tf_op jit(solution)/shard_map/ppermute | solution.py:683
  32.4 4.2 %collective-permute-start.9 = (bf16[320,128]{1,0:T(8,128)(2,1)S(1)}, bf16[320,128]{1,0:T(8,128)(2,1)S(1)}, u32[]{:S(2)}, u32[]{:S(2)}) collective-permute-start(bf16[320,128]{1,0:T(8,128)(2,1)S(1)} %get-tuple-element.79), channel_id=1, source_target_pairs={{0,3},{1,0},{2,1},{3,2},{4,7},{5,4},{6,5},{7,6},{8,11},{9,8},{10,9... | collective-permute-start | bytes 245768 | tf_op jit(solution)/shard_map/ppermute | solution.py:685
  42.0 6.4 %collective-permute-start.10 = (bf16[256,128]{1,0:T(8,128)(2,1)S(1)}, bf16[256,128]{1,0:T(8,128)(2,1)S(1)}, u32[]{:S(2)}, u32[]{:S(2)}) collective-permute-start(bf16[256,128]{1,0:T(8,128)(2,1)S(1)} %get-tuple-element.55), channel_id=1, source_target_pairs={{0,16},{16,0},{1,17},{17,1},{2,18},{18,2},{3,19},{19,3},{4,20},{20... | collective-permute-start | bytes 196616 | tf_op jit(solution)/shard_map/ppermute | solution.py:666
  48.4 7.6 %collective-permute-start.13 = (bf16[256,128]{1,0:T(8,128)(2,1)S(1)}, bf16[256,128]{1,0:T(8,128)(2,1)S(1)}, u32[]{:S(2)}, u32[]{:S(2)}) collective-permute-start(bf16[256,128]{1,0:T(8,128)(2,1)S(1)} %add_convert_fusion.2), channel_id=1, source_target_pairs={{0,12},{4,0},{8,4},{12,8},{1,13},{5,1},{9,5},{13,9},{2,14},{6,2},{... | collective-permute-start | bytes 196616 | tf_op jit(solution)/shard_map/ppermute | solution.py:666
  50.0 5.9 %collective-permute-start.12 = (bf16[256,128]{1,0:T(8,128)(2,1)S(1)}, bf16[256,128]{1,0:T(8,128)(2,1)S(1)}, u32[]{:S(2)}, u32[]{:S(2)}) collective-permute-start(bf16[256,128]{1,0:T(8,128)(2,1)S(1)} %add_convert_fusion.2), channel_id=1, source_target_pairs={{0,8},{4,12},{8,0},{12,4},{1,9},{5,13},{9,1},{13,5},{2,10},{6,14},... | collective-permute-start | bytes 196616 | tf_op jit(solution)/shard_map/ppermute | solution.py:666
  50.1 5.9 %collective-permute-start.11 = (bf16[256,128]{1,0:T(8,128)(2,1)S(1)}, bf16[256,128]{1,0:T(8,128)(2,1)S(1)}, u32[]{:S(2)}, u32[]{:S(2)}) collective-permute-start(bf16[256,128]{1,0:T(8,128)(2,1)S(1)} %add_convert_fusion.2), channel_id=1, source_target_pairs={{0,4},{4,8},{8,12},{12,0},{1,5},{5,9},{9,13},{13,1},{2,6},{6,10},{... | collective-permute-start | bytes 196616 | tf_op jit(solution)/shard_map/ppermute | solution.py:666
  56.0 6.3 %collective-permute-start.16 = (bf16[256,128]{1,0:T(8,128)(2,1)S(1)}, bf16[256,128]{1,0:T(8,128)(2,1)S(1)}, u32[]{:S(2)}, u32[]{:S(2)}) collective-permute-start(bf16[256,128]{1,0:T(8,128)(2,1)S(1)} %add_convert_fusion.1), channel_id=1, source_target_pairs={{0,3},{1,0},{2,1},{3,2},{4,7},{5,4},{6,5},{7,6},{8,11},{9,8},{10,9... | collective-permute-start | bytes 196616 | tf_op jit(solution)/shard_map/ppermute | solution.py:666
  59.1 4.7 %collective-permute-start.15 = (bf16[256,128]{1,0:T(8,128)(2,1)S(1)}, bf16[256,128]{1,0:T(8,128)(2,1)S(1)}, u32[]{:S(2)}, u32[]{:S(2)}) collective-permute-start(bf16[256,128]{1,0:T(8,128)(2,1)S(1)} %add_convert_fusion.1), channel_id=1, source_target_pairs={{0,2},{1,3},{2,0},{3,1},{4,6},{5,7},{6,4},{7,5},{8,10},{9,11},{10,... | collective-permute-start | bytes 196616 | tf_op jit(solution)/shard_map/ppermute | solution.py:666
  59.1 5.0 %collective-permute-start.14 = (bf16[256,128]{1,0:T(8,128)(2,1)S(1)}, bf16[256,128]{1,0:T(8,128)(2,1)S(1)}, u32[]{:S(2)}, u32[]{:S(2)}) collective-permute-start(bf16[256,128]{1,0:T(8,128)(2,1)S(1)} %add_convert_fusion.1), channel_id=1, source_target_pairs={{0,1},{1,2},{2,3},{3,0},{4,5},{5,6},{6,7},{7,4},{8,9},{9,10},{10,1... | collective-permute-start | bytes 196616 | tf_op jit(solution)/shard_map/ppermute | solution.py:666

commit v5 on v4

--- a/solution.py
+++ b/solution.py
@@ -13,6 +13,8 @@
 VMEM_LIMIT = 32 << 20
 TOGETHER = 4
 UNROLL = 16
+HOLDERS = (1, 3)
+HELD = 2
 RIM = 4
 CHUNK = 64
 PIECES = ((0,), (1, 2), (3,))
@@ -44,10 +46,6 @@
     left = blk[pl.ds(b, 2)].reshape(2 * size, size)
     right = blk[pl.ds(b + 2, 2)].reshape(2 * size, size)
     return jnp.concatenate([left, right], axis=1)
-
-
-def row(ref, index):
-    return ref[pl.ds(index, 8, stride=0), :]
 
 
 def add_rows(acc, index, value):
@@ -64,7 +62,7 @@
         outs = []
         for u in range(UNROLL):
             b = (i * UNROLL + u) * TOGETHER
-            t = [row(pix, tile_ref[b + k]) for k in range(TOGETHER)]
+            t = [pix[tile_ref[b + k]] for k in range(TOGETHER)]
             upper = jnp.concatenate([jnp.where(low, t[0], t[1]), zero], axis=0)
             lower = jnp.concatenate([zero, jnp.where(low, t[2], t[3])], axis=0)
             lhs = jnp.concatenate([upper.astype(BF16), lower.astype(BF16)], axis=1)
@@ -92,7 +90,7 @@
         outs = []
         for u in range(UNROLL):
             b = (i * UNROLL + u) * TOGETHER
-            t = [row(res, ray_ref[b + k]) for k in range(TOGETHER)]
+            t = [res[ray_ref[b + k]] for k in range(TOGETHER)]
             left = jnp.concatenate([jnp.where(low, t[0], 0.0), jnp.where(low, t[2], 0.0)], axis=0)
             right = jnp.concatenate([jnp.where(low, 0.0, t[1]), jnp.where(low, 0.0, t[3])], axis=0)
             lhs = jnp.concatenate([left.astype(BF16), right.astype(BF16)], axis=1)
@@ -109,38 +107,48 @@
     lax.fori_loop(0, blk.shape[0] // (TOGETHER * UNROLL), body, 0)
 
 
-def tiles_of(x_shape):
-    wide = x_shape[1] // 128
-    return [(r, c, slice(c * 128, c * 128 + 128)) for r in range(x_shape[0]) for c in range(wide)]
-
-
-def load_pixels(value, pix):
-    wide = value.shape[1] // 128
-    for r, c, columns in tiles_of(value.shape):
-        pix[r * wide + c : r * wide + c + 1] = value[r : r + 1, columns]
+def twice(ref, index, n, value):
+    ref[index, n, :] = value
+    ref[index, n + 4, :] = value
+
+
+def load_pixels(x, pix):
+    for n in range(HELD):
+        for c in range(x.shape[2] // 128):
+            own = pl.ds(c, x.shape[1], stride=x.shape[2] // 128)
+            twice(pix, own, n, x[n, :, c * 128 : c * 128 + 128])
+
+
+def load_residual(r_ref, res):
+    rays = res.shape[0]
+    for n in range(HELD):
+        twice(res, slice(None), n, r_ref[n * rays : (n + 1) * rays].astype(F32))
 
 
 def moved_by(x, back):
-    wide = x.shape[1] // 128
-    rows = back.shape[0]
-    columns = []
-    for c in range(wide):
-        own = pl.ds(c, rows // wide, stride=wide)
-        columns.append(back[own, 0, :] + back[own, 4, :])
-    return x - 0.8 * jnp.concatenate(columns, axis=1)
+    parts = []
+    for n in range(HELD):
+        columns = []
+        for c in range(x.shape[2] // 128):
+            own = pl.ds(c, x.shape[1], stride=x.shape[2] // 128)
+            columns.append(back[own, n, :] + back[own, n + 4, :])
+        parts.append(x[n] - 0.8 * jnp.concatenate(columns, axis=1))
+    return parts
 
 
 def store_rays(place_ref, sino_ref, acc, total, o_ref):
-    total[0 : acc.shape[0]] = acc[:, 0, :] + acc[:, 4, :]
+    rays = acc.shape[0]
     own = sino_ref.shape[0]
     mine = pl.ds(pl.multiple_of(place_ref[1] * own, own), own)
-    for z in range(sino_ref.shape[1]):
-
-        @pl.when(place_ref[0] == z)
-        def _():
-            total[mine] = total[mine] - sino_ref[:, z, :]
-
-    o_ref[0 : acc.shape[0]] = total[0 : acc.shape[0]].astype(o_ref.dtype)
+    for n in range(HELD):
+        total[...] = acc[:, n, :] + acc[:, n + 4, :]
+        for half in range(sino_ref.shape[1] // HELD):
+
+            @pl.when(place_ref[0] // 2 == half)
+            def _():
+                total[mine] = total[mine] - sino_ref[:, half * HELD + n, :]
+
+        o_ref[n * rays : (n + 1) * rays] = total[...].astype(o_ref.dtype)
 
 
 def in_pieces(cur, first):
@@ -158,11 +166,11 @@
     tile_in,
     states_in,
     got_1,
-    got_2,
     got_3,
     sino_in,
     blk_in,
     o_ref,
+    edge_ref,
     start_ref,
     blk,
     angle,
@@ -211,21 +219,24 @@
     acc[...] = jnp.zeros_like(acc)
     for copy in small:
         copy.wait()
-    @pl.when(place_ref[0] == 0)
+    start_ref[...] = got_1[...] + got_3[...]
+    tail = in_pieces(cur, cur.shape[1] - RIM).astype(BF16)
+    head = in_pieces(cur, 0).astype(BF16)
+    edge = tail.shape[0]
+    edge_ref[0:edge] = tail
+    edge_ref[edge:] = head
+    sums = o_ref.shape[0] - edge
+    at_end = (place_ref[1] // 4) % 4 == 3
+
+    @pl.when(at_end)
     def _():
-        start_ref[...] = cur[0]
-
-    for k, value in enumerate((got_1, got_2, got_3)):
-
-        @pl.when(place_ref[0] == k + 1)
-        def _():
-            start_ref[...] = value[...]
-
-    rows = acc.shape[0]
-    edge = RIM * cur.shape[0] * cur.shape[2] // 128
-    o_ref[rows : rows + edge] = in_pieces(cur, cur.shape[1] - RIM).astype(BF16)
-    o_ref[rows + edge :] = in_pieces(cur, 0).astype(BF16)
-    load_pixels(start_ref[...], pix)
+        o_ref[sums:] = tail
+
+    @pl.when(jnp.logical_not(at_end))
+    def _():
+        o_ref[sums:] = head
+
+    load_pixels(start_ref, pix)
     wide = cur.shape[2] // 128
     project_blocks(
         lambda b: angle[b] * wide + detector[b],
@@ -247,21 +258,22 @@
     return pl.pallas_call(
         project_kernel,
         out_shape=(
-            jax.ShapeDtypeStruct((ray_total + 2 * edge, 128), BF16),
+            jax.ShapeDtypeStruct((HELD * ray_total + edge, 128), BF16),
+            jax.ShapeDtypeStruct((2 * edge, 128), BF16),
             jax.ShapeDtypeStruct(shape, F32),
             pltpu.VMEM(blocks.shape, BF16),
         ),
-        in_specs=[in_smem()] + [far] * 4 + [in_vmem()] * 3 + [far] * 2,
-        out_specs=(in_vmem(),) * 3,
+        in_specs=[in_smem()] + [far] * 4 + [in_vmem()] * 2 + [far] * 2,
+        out_specs=(in_vmem(),) * 4,
         scratch_shapes=[
             pltpu.SMEM((count,), jnp.int32),
             pltpu.SMEM((count,), jnp.int32),
             pltpu.SMEM((count,), jnp.int32),
             pltpu.VMEM(states.shape[1:], F32),
             pltpu.VMEM(sinogram.shape, F32),
-            pltpu.VMEM((shape[0] * shape[1] // 128 + 8, 128), F32),
+            pltpu.VMEM((shape[1] * shape[2] // 128, 8, 128), F32),
             pltpu.VMEM((ray_total, 8, 128), F32),
-            pltpu.VMEM((ray_total + 8, 128), F32),
+            pltpu.VMEM((ray_total, 128), F32),
             pltpu.SemaphoreType.DMA((5,)),
             pltpu.SemaphoreType.DMA((count // CHUNK,)),
         ],
@@ -280,22 +292,22 @@
 
 
 def back_project_kernel(
-    place_ref, ray_ref, tile_ref, r_ref, x_ref, sino_ref, blk, x_out, o_ref, res, pix, back, acc
+    place_ref, ray_ref, tile_ref, r_ref, x_ref, sino_ref, blk, x_out, o_ref, res, pix, back, acc, total
 ):
-    res[0 : r_ref.shape[0]] = r_ref[...].astype(F32)
+    load_residual(r_ref, res)
     back[...] = jnp.zeros_like(back)
     back_blocks(ray_ref, tile_ref, res, blk, back)
-    moved = moved_by(x_ref[...], back)
-    x_out[...] = moved
-    load_pixels(moved, pix)
+    for n, moved in enumerate(moved_by(x_ref, back)):
+        x_out[n] = moved
+    load_pixels(x_out, pix)
     acc[...] = jnp.zeros_like(acc)
     project_blocks(lambda b: ray_ref[b], tile_ref, pix, blk, acc)
-    store_rays(place_ref, sino_ref, acc, res, o_ref)
+    store_rays(place_ref, sino_ref, acc, total, o_ref)
 
 
 def back_project(place, ray_index, tile_index, residual, x, sinogram, blocks):
-    ray_total = residual.shape[0]
-    tiles = x.size // 128
+    ray_total = residual.shape[0] // HELD
+    tiles = x.shape[1] * x.shape[2] // 128
     return pl.pallas_call(
         back_project_kernel,
         out_shape=(
@@ -305,10 +317,11 @@
         in_specs=[in_smem()] * 3 + [in_vmem()] * 4,
         out_specs=(in_vmem(), in_vmem()),
         scratch_shapes=[
-            pltpu.VMEM((ray_total + 8, 128), F32),
-            pltpu.VMEM((tiles + 8, 128), F32),
+            pltpu.VMEM((ray_total, 8, 128), F32),
+            pltpu.VMEM((tiles, 8, 128), F32),
             pltpu.VMEM((tiles, 8, 128), F32),
             pltpu.VMEM((ray_total, 8, 128), F32),
+            pltpu.VMEM((ray_total, 128), F32),
         ],
         compiler_params=params(),
         name="back_project",
@@ -316,24 +329,25 @@
 
 
 def back_kernel(ray_ref, tile_ref, r_ref, x_ref, start_ref, cur_ref, net_ref, blk, o_ref, res, back):
-    res[0 : r_ref.shape[0]] = r_ref[...].astype(F32)
+    load_residual(r_ref, res)
     back[...] = jnp.zeros_like(back)
     for z in range(net_ref.shape[0]):
-        o_ref[z + 1] = (cur_ref[z] - 2.0 * net_ref[z]).astype(o_ref.dtype)
+        o_ref[HELD + z] = (cur_ref[z] - 2.0 * net_ref[z]).astype(o_ref.dtype)
     back_blocks(ray_ref, tile_ref, res, blk, back)
-    o_ref[0] = (2.0 * moved_by(x_ref[...], back) - start_ref[...]).astype(o_ref.dtype)
+    for n, moved in enumerate(moved_by(x_ref, back)):
+        o_ref[n] = (2.0 * moved - start_ref[n]).astype(o_ref.dtype)
 
 
 def back_reflect(ray_index, tile_index, residual, x, start, current, net, blocks):
-    ray_total = residual.shape[0]
-    tiles = x.size // 128
+    ray_total = residual.shape[0] // HELD
+    tiles = x.shape[1] * x.shape[2] // 128
     return pl.pallas_call(
         back_kernel,
-        out_shape=jax.ShapeDtypeStruct((1 + net.shape[0], *x.shape), BF16),
+        out_shape=jax.ShapeDtypeStruct((HELD + net.shape[0], *x.shape[1:]), BF16),
         in_specs=[in_smem()] * 2 + [in_vmem()] * 6,
         out_specs=in_vmem(),
         scratch_shapes=[
-            pltpu.VMEM((ray_total + 8, 128), F32),
+            pltpu.VMEM((ray_total, 8, 128), F32),
             pltpu.VMEM((tiles, 8, 128), F32),
         ],
         compiler_params=params(),
@@ -343,10 +357,10 @@
 
 def finish_kernel(place_ref, all_ref, cur_ref, net_ref, o_ref):
     for z in range(o_ref.shape[0]):
-        data = all_ref[z, 0].astype(F32)
+        data = all_ref[HOLDERS[z // HELD], z % HELD].astype(F32)
         total = data
         for k in range(1, all_ref.shape[0]):
-            total = total + all_ref[k, 1 + z].astype(F32)
+            total = total + all_ref[k, HELD + z].astype(F32)
 
         @pl.when(place_ref[0] == 0)
         def _():
@@ -440,19 +454,8 @@
 
 
 def prepare_kernel(
-    place_ref, before, after, cur, first, hidden, last, rim, zf, zh, zl, zw, zm, af, ah, al, turn
+    place_ref, first, hidden, last, zf, zh, zl, zw, zm, af, ah, al, turn
 ):
-    rows = cur.shape[1]
-    wide = cur.shape[2] // 128
-    rim[:, RIM : RIM + rows] = cur[...].astype(BF16).astype(F32)
-    above = jnp.where(place_ref[1] > 0, before[...].astype(F32), 0.0)
-    below = jnp.where(place_ref[1] < place_ref[2] - 1, after[...].astype(F32), 0.0)
-    for z in range(cur.shape[0]):
-        for c in range(wide):
-            n = (z * wide + c) * RIM
-            rim[z, 0:RIM, c * 128 : c * 128 + 128] = above[n : n + RIM]
-            rim[z, RIM + rows :, c * 128 : c * 128 + 128] = below[n : n + RIM]
-
     @pl.when(place_ref[0] == 1)
     def _():
         row_band(first, hidden, last, af, ah, al, turn)
@@ -467,10 +470,8 @@
         slice_band(first, hidden, last, 2, zf, zh, zl, turn)
 
 
-def prepare(place, rim, current, first, hidden, last):
+def prepare(place, first, hidden, last):
     layers = hidden.shape[1]
-    slices, rows, columns = current.shape
-    whole = jax.ShapeDtypeStruct((slices, rows + 2 * RIM, columns), F32)
     shapes = [
         (128, 16),
         (layers, 128, 384),
@@ -483,13 +484,13 @@
     ]
     return pl.pallas_call(
         prepare_kernel,
-        out_shape=[whole] + [jax.ShapeDtypeStruct(s, BF16) for s in shapes],
-        in_specs=[in_smem()] + [in_vmem()] * 6,
-        out_specs=[in_vmem()] * 9,
+        out_shape=[jax.ShapeDtypeStruct(s, BF16) for s in shapes],
+        in_specs=[in_smem()] + [in_vmem()] * 3,
+        out_specs=[in_vmem()] * 8,
         scratch_shapes=[pltpu.VMEM((256, 256), F32)],
         compiler_params=params(),
         name="prepare",
-    )(place, *rim, current, first, hidden, last)
+    )(place, first, hidden, last)
 
 
 def side_by_side(value):
@@ -605,12 +606,45 @@
 
 
 def piece_kernel(
-    k, place_ref, blk, net, rim, zf, zh, zl, zw, zm, af, ah, al, o_ref, sa, sb, ca, xa, xb
+    k,
+    place_ref,
+    blk,
+    net,
+    before,
+    after,
+    cur,
+    zf,
+    zh,
+    zl,
+    zw,
+    zm,
+    af,
+    ah,
+    al,
+    o_ref,
+    rim,
+    sa,
+    sb,
+    ca,
+    xa,
+    xb,
 ):
     rows = o_ref.shape[1]
-    depth = (rim.shape[1] - rows) // 2
+    depth = RIM
     above, below = place_ref[1] > 0, place_ref[1] < place_ref[2] - 1
     o_ref[...] = net[...]
+
+    @pl.when(place_ref[0] > 0)
+    def _():
+        wide = cur.shape[2] // 128
+        rim[:, RIM : RIM + rows] = cur[...].astype(BF16).astype(F32)
+        over = jnp.where(above, before[...].astype(F32), 0.0)
+        under = jnp.where(below, after[...].astype(F32), 0.0)
+        for z in range(cur.shape[0]):
+            for c in range(wide):
+                n = (z * wide + c) * RIM
+                rim[z, 0:RIM, c * 128 : c * 128 + 128] = over[n : n + RIM]
+                rim[z, RIM + rows :, c * 128 : c * 128 + 128] = under[n : n + RIM]
 
     @pl.when(place_ref[0] == 1)
     def _():
@@ -628,24 +662,28 @@
         coronal_piece(k * (rows // 4), rows // 4, depth, rim, zf, zh, zl, o_ref, ca)
 
 
-def piece(k, place, blocks, net, prepared):
+def piece(k, place, blocks, net, rim, current, prepared):
     slices, rows, columns = net.shape
     reach = rows + 6
+    assert reach == rows + 2 * RIM - 2
     return pl.pallas_call(
         functools.partial(piece_kernel, k),
         out_shape=jax.ShapeDtypeStruct(net.shape, F32),
-        in_specs=[in_smem()] + [in_vmem()] * (2 + len(prepared)),
+        in_specs=[in_smem()] + [in_vmem()] * (5 + len(prepared)),
         out_specs=in_vmem(),
-        scratch_shapes=[pltpu.VMEM((reach * 128, columns // 2), BF16)] * 2
+        scratch_shapes=[pltpu.VMEM((slices, rows + 2 * RIM, columns), F32)]
+        + [pltpu.VMEM((reach * 128, columns // 2), BF16)] * 2
         + [pltpu.VMEM((rows // 4, 384, columns), BF16)]
         + [pltpu.VMEM((3, reach * 32, columns), BF16)] * 2,
         compiler_params=params(),
         name=f"piece_{k}",
-    )(place, near(blocks), net, *prepared)
-
-
-def swapped(groups, k):
-    return [(g[n], g[(n + k) % len(g)]) for g in groups for n in range(len(g))]
+    )(place, near(blocks), net, *rim, current, *prepared)
+
+
+def swapped(groups, k, agents):
+    count = sum(len(g) for g in groups)
+    pairs = [(g[n], g[(n + k) % len(g)]) for g in groups for n in range(len(g))]
+    return [(a * count + i, a * count + j) for a in agents for i, j in pairs]
 
 
 def stage_groups(count):
@@ -660,38 +698,50 @@
     ]
 
 
+BOTH = ("agent", "tile")
+
+
 def added_up(values, groups):
     total = values.astype(F32)
     for k in range(1, len(groups[0])):
-        total = total + lax.ppermute(values, "tile", swapped(groups, k)).astype(F32)
+        total = total + lax.ppermute(values, BOTH, swapped(groups, k, HOLDERS)).astype(F32)
     return total.astype(values.dtype)
 
 
-def added_up_with_rims(sums, groups, ends):
-    far, strided, near = groups
-    rows = sums.shape[0] * 2 // 3
-    edge = (sums.shape[0] - rows) // 2
-    got = lax.ppermute(sums, "tile", swapped(far, 1))
-    tail, head = sums[rows : rows + edge], sums[rows + edge :]
-    onward, backward = got[rows : rows + edge], got[rows + edge :]
-    sums = (sums[0:rows].astype(F32) + got[0:rows].astype(F32)).astype(BF16)
-    for n, group in enumerate((strided, near)):
-        first, last = ends[n]
-        onward = jnp.where(last, onward, tail)
-        backward = jnp.where(first, backward, head)
+def added_up_with_rims(first, own, groups, ends, between):
+    agents = (1, 2, 3)
+    far, strided, near_by = groups
+    edge = own.shape[0] // 2
+    rows = first.shape[0] - edge
+    got = lax.ppermute(first, BOTH, swapped(far, 1, agents))
+    tail, head = own[0:edge], own[edge:]
+    onward = backward = got[rows:]
+    sums = (first[0:rows].astype(F32) + got[0:rows].astype(F32)).astype(BF16)
+    made = None
+    for n, group in enumerate((strided, near_by)):
+        at_first, at_last = ends[n]
+        onward = jnp.where(at_last, onward, tail)
+        backward = jnp.where(at_first, backward, head)
         sums, onward, backward = lax.optimization_barrier((sums, onward, backward))
-        up = lax.ppermute(jnp.concatenate([sums, onward]), "tile", swapped(group, 1))
-        across = lax.ppermute(sums, "tile", swapped(group, 2))
-        down = lax.ppermute(jnp.concatenate([sums, backward]), "tile", swapped(group, 3))
+        if n == 0:
+            made = between(sums)
+        up = lax.ppermute(jnp.concatenate([sums, onward]), BOTH, swapped(group, 1, agents))
+        across = lax.ppermute(sums, BOTH, swapped(group, 2, agents))
+        down = lax.ppermute(jnp.concatenate([sums, backward]), BOTH, swapped(group, 3, agents))
         onward, backward = up[rows:], down[rows:]
         total = sums.astype(F32) + up[0:rows].astype(F32)
         total = total + across.astype(F32) + down[0:rows].astype(F32)
         sums = total.astype(BF16)
-    return sums, (onward, backward)
+        if n == 0:
+            sums, made = lax.optimization_barrier((sums, made))
+    return sums, (onward, backward), made
 
 
 def slices_sent(current):
-    return [lax.ppermute(current[k], "agent", [(0, k)]) for k in range(1, current.shape[0])]
+    return [
+        lax.ppermute(current[n * HELD : (n + 1) * HELD], "agent", [(0, holder)])
+        for n, holder in enumerate(HOLDERS)
+    ]
 
 
 def per_device(
@@ -716,14 +766,19 @@
     within = [lax.shift_right_logical(tile_place, 2) & 3, tile_place & 3]
     ends = [(at == 0, at == 3) for at in within]
     got, ends = lax.optimization_barrier((slices_sent(current), ends))
-    sums, start, blocks_here = project(
+    first, own, start, blocks_here = project(
         place, block_angle, block_detector, block_tile, states, got, sinogram, blocks, ray_total
     )
 
     groups = stage_groups(tile_count)
     net = jnp.zeros_like(current)
     x_data = start
-    sums, rim = added_up_with_rims(sums, groups, ends)
+
+    def weights(sums):
+        tied, _ = lax.optimization_barrier((place, sums))
+        return prepare(tied, conv_first, conv_hidden, conv_last)
+
+    sums, rim, prepared = added_up_with_rims(first, own, groups, ends, weights)
     for _ in range(DATA_STEPS - 2):
         x_data, sums = back_project(
             place, ray_index, block_tile, sums, x_data, sinogram, blocks_here
@@ -733,10 +788,8 @@
     x_data, sums = back_project(place, ray_index, block_tile, sums, x_data, sinogram, blocks_here)
     for n, group in enumerate(groups):
         sums, net = lax.optimization_barrier((sums, net))
-        if n == 0:
-            prepared = prepare(place, rim, current, conv_first, conv_hidden, conv_last)
         for k in PIECES[n]:
-            net = piece(k, place, blocks_here, net, prepared)
+            net = piece(k, place, blocks_here, net, rim, current, prepared)
         sums = added_up(sums, group)
     sent = back_reflect(ray_index, block_tile, sums, x_data, start, current, net, blocks_here)
     everything = lax.all_gather(sent, "agent")

time: 78.7 us -> 101 us (1.28)
  starting transfers between devices: 24.6 us -> 50.4 us
  blocking collectives: 10.6 us -> 6.88 us
  waiting for transfers between devices: 15.7 us -> 13.9 us
  Pallas kernels: 26.1 us -> 27.4 us
    ppermute x17 -> x16, starting transfers between devices: 24.6 us -> 50.4 us  [the longest x7 22 us: added_up(): lax.ppermute(values, BOTH, swapped(groups, k, HOLDERS)).astype(F32)]
    all_gather x1, blocking collectives: 10.6 us -> 6.88 us  [per_device(): everything = lax.all_gather(sent, 'agent')]
    ppermute x17 -> x16, waiting for transfers between devices: 15.7 us -> 13.9 us  [the longest x2 4.31 us: slices_sent(): lax.ppermute(current[n * HELD:(n + 1) * HELD], 'agent', [(0, holder)])]
  transfers between devices with their start and end apart: 17 -> 16, of which waited for: 6 -> 8; matrix products, arithmetic and copies ran while one was open for 0% -> 0% of each run, Pallas kernels for 15% -> 12%
where the time goes in v5:
time: 101 us; the launch traced here: 100 us
  starting transfers between devices  50.4 us (50%)
  Pallas kernels  27.4 us (27%)
  waiting for transfers between devices  13.9 us (14%)
  blocking collectives  6.88 us (7%)
    ppermute x7, starting transfers between devices, added_up(): lax.ppermute(values, BOTH, swapped(groups, k, HOLDERS)).astype(F32)  22 us
    pallas_call x4, Pallas kernels, piece(): pl.pallas_call(functools.partial(piece_kernel, k), out_shape=jax.ShapeDty...  10.8 us
    ppermute x2, starting transfers between devices, added_up_with_rims(): across = lax.ppermute(sums, BOTH, swapped(group, 2, agents))  9.05 us
    ppermute x2, starting transfers between devices, added_up_with_rims(): lax.ppermute(jnp.concatenate([sums, backward]), BOTH, swapped(group, 3, a...  7.21 us
    all_gather x1, blocking collectives, per_device(): everything = lax.all_gather(sent, 'agent')  6.88 us
    ppermute x2, starting transfers between devices, added_up_with_rims(): lax.ppermute(jnp.concatenate([sums, onward]), BOTH, swapped(group, 1, age...  5.85 us
    pallas_call x1, Pallas kernels, back_project(): pl.pallas_call(back_project_kernel, out_shape=(jax.ShapeDtypeStruct(x.sha...  5.81 us
    pallas_call x1, Pallas kernels, project(): pl.pallas_call(project_kernel, out_shape=(jax.ShapeDtypeStruct((HELD * ra...  5.69 us
  transfers between devices with their start and end apart: 16, of which 8 were waited for; matrix products, arithmetic and copies ran while one was open for 0% of the time, Pallas kernels for 12%

profile of v5, /device:TPU:1, one launch (start us, length us, event | category | flops | bytes accessed | tf_op | source)
XLA Modules:
  0.0 100.4 jit_solution(8105019314742287624)
XLA Ops:
  0.0 0.0 copy-start.5
  0.0 0.0 copy-start.6
  0.0 0.0 copy-start.7
  0.0 0.0 copy-start.2
  0.0 0.0 copy-start.4
  0.0 0.0 copy-start.1
  0.0 0.0 copy-start.3
  0.1 0.9 slice_bitcast_fusion
  1.0 0.7 collective-permute-start.1
  1.7 1.3 %collective-permute-start = (f32[2,16,512]{2,1,0:T(8,128)S(1)}, f32[2,16,512]{2,1,0:T(8,128)S(1)}, u32[]{:S(2)}, u32[]{:S(2)}) collective-permute-start(f32[2,16,512]{2,1,0:T(8,128)S(1)} %get-tuple-element.96), channel_id=1, source_target_pairs={{0,32},{1,33},{2,34},{3,35},{4,36},{5,37},{6,38},{7,39},{8,40},{9,... | collective-permute-start | bytes 196616 | tf_op jit(solution)/shard_map/ppermute | solution.py:742
  3.0 0.1 pad_add_fusion.place_ref
  3.1 0.0 copy-start
  3.1 0.0 collective-permute-done.1.got_3
  3.1 4.3 %collective-permute-done.got_1 = f32[2,16,512]{2,1,0:T(8,128)S(1)} collective-permute-done((f32[2,16,512]{2,1,0:T(8,128)S(1)}, f32[2,16,512]{2,1,0:T(8,128)S(1)}, u32[]{:S(2)}, u32[]{:S(2)}) %collective-permute-start) | collective-permute-done | bytes 65568 | tf_op jit(solution)/shard_map/ppermute | solution.py:742
  7.4 5.7 %project.1 = (bf16[576,128]{1,0:T(8,128)(2,1)S(1)}, bf16[128,128]{1,0:T(8,128)(2,1)S(1)}, f32[2,16,512]{2,1,0:T(8,128)S(1)}, bf16[256,128,128]{2,1,0:T(8,128)(2,1)S(1)}) custom-call(s32[3]{0:T(128)S(1)} %pad_add_fusion.place_ref, s32[256]{0:T(256)} %angle_in.1, s32[256]{0:T(256)} %detector_in.1, s32[256]{0:T(256)} %tile_ref.3, f32[1,4,16,512]{3,2,1,0:T(8,128)} %states_in.1, ...), custom_call_target="tpu_custom_call" | custom-call | tf_op jit(solution)/shard_map/project/pallas_call | solution.py:258
  13.1 4.4 %collective-permute-start.2 = (bf16[576,128]{1,0:T(8,128)(2,1)S(1)}, bf16[576,128]{1,0:T(8,128)(2,1)S(1)}, u32[]{:S(2)}, u32[]{:S(2)}) collective-permute-start(bf16[576,128]{1,0:T(8,128)(2,1)S(1)} %get-tuple-element.49), channel_id=1, source_target_pairs={{32,48},{48,32},{33,49},{49,33},{34,50},{50,34},{35,51},{51,35},{3... | collective-permute-start | bytes 442376 | tf_op jit(solution)/shard_map/ppermute | solution.py:716
  17.4 3.0 %collective-permute-done.2 = bf16[576,128]{1,0:T(8,128)(2,1)S(1)} collective-permute-done((bf16[576,128]{1,0:T(8,128)(2,1)S(1)}, bf16[576,128]{1,0:T(8,128)(2,1)S(1)}, u32[]{:S(2)}, u32[]{:S(2)}) %collective-permute-start.2) | collective-permute-done | bytes 147488 | tf_op jit(solution)/shard_map/ppermute | solution.py:716
  20.5 3.2 %collective-permute-start.3 = (bf16[576,128]{1,0:T(8,128)(2,1)S(1)}, bf16[576,128]{1,0:T(8,128)(2,1)S(1)}, u32[]{:S(2)}, u32[]{:S(2)}) collective-permute-start(bf16[576,128]{1,0:T(8,128)(2,1)S(1)} %get-tuple-element.93), channel_id=1, source_target_pairs={{32,36},{36,40},{40,44},{44,32},{33,37},{37,41},{41,45},{45,33},{3... | collective-permute-start | bytes 442376 | tf_op jit(solution)/shard_map/ppermute | solution.py:728
  23.8 3.4 %collective-permute-start.5 = (bf16[576,128]{1,0:T(8,128)(2,1)S(1)}, bf16[576,128]{1,0:T(8,128)(2,1)S(1)}, u32[]{:S(2)}, u32[]{:S(2)}) collective-permute-start(bf16[576,128]{1,0:T(8,128)(2,1)S(1)} %get-tuple-element.94), channel_id=1, source_target_pairs={{32,44},{36,32},{40,36},{44,40},{33,45},{37,33},{41,37},{45,41},{3... | collective-permute-start | bytes 442376 | tf_op jit(solution)/shard_map/ppermute | solution.py:730
  27.1 3.5 %collective-permute-start.4 = (bf16[512,128]{1,0:T(8,128)(2,1)S(1)}, bf16[512,128]{1,0:T(8,128)(2,1)S(1)}, u32[]{:S(2)}, u32[]{:S(2)}) collective-permute-start(bf16[512,128]{1,0:T(8,128)(2,1)S(1)} %add_convert_fusion.5), channel_id=1, source_target_pairs={{32,40},{36,44},{40,32},{44,36},{33,41},{37,45},{41,33},{45,37},{3... | collective-permute-start | bytes 393224 | tf_op jit(solution)/shard_map/ppermute | solution.py:729
  30.7 0.0 copy-done.4
  30.7 0.0 copy-done.1
  30.7 0.0 copy-done.3
  30.7 1.1 %prepare.1 = (bf16[128,16]{1,0:T(8,128)(2,1)S(1)}, bf16[2,128,384]{2,1,0:T(8,128)(2,1)S(1)}, bf16[8,384]{1,0:T(8,128)(2,1)S(1)}, bf16[2,256,512]{2,1,0:T(8,128)(...) custom-call(s32[3]{0:T(128)S(1)} %pad_add_fusion.place_ref, ...), custom_call_target="tpu_custom_call" | custom-call | tf_op jit(solution)/shard_map/prepare/pallas_call | solution.py:485
  31.8 2.5 %collective-permute-done.4 = bf16[512,128]{1,0:T(8,128)(2,1)S(1)} collective-permute-done((bf16[512,128]{1,0:T(8,128)(2,1)S(1)}, bf16[512,128]{1,0:T(8,128)(2,1)S(1)}, u32[]{:S(2)}, u32[]{:S(2)}) %collective-permute-start.4) | collective-permute-done | bytes 131104 | tf_op jit(solution)/shard_map/ppermute | solution.py:729
  34.3 0.0 collective-permute-done.3
  34.3 0.0 collective-permute-done.5
  34.3 0.1 add_convert_fusion.4
  34.4 5.5 %collective-permute-start.7 = (bf16[512,128]{1,0:T(8,128)(2,1)S(1)}, bf16[512,128]{1,0:T(8,128)(2,1)S(1)}, u32[]{:S(2)}, u32[]{:S(2)}) collective-permute-start(bf16[512,128]{1,0:T(8,128)(2,1)S(1)} %add_convert_fusion.4), channel_id=1, source_target_pairs={{32,34},{33,35},{34,32},{35,33},{36,38},{37,39},{38,36},{39,37},{4... | collective-permute-start | bytes 393224 | tf_op jit(solution)/shard_map/ppermute | solution.py:729
  40.0 2.6 %collective-permute-start.6 = (bf16[576,128]{1,0:T(8,128)(2,1)S(1)}, bf16[576,128]{1,0:T(8,128)(2,1)S(1)}, u32[]{:S(2)}, u32[]{:S(2)}) collective-permute-start(bf16[576,128]{1,0:T(8,128)(2,1)S(1)} %get-tuple-element.91), channel_id=1, source_target_pairs={{32,33},{33,34},{34,35},{35,32},{36,37},{37,38},{38,39},{39,36},{4... | collective-permute-start | bytes 442376 | tf_op jit(solution)/shard_map/ppermute | solution.py:728
  42.6 3.8 %collective-permute-start.8 = (bf16[576,128]{1,0:T(8,128)(2,1)S(1)}, bf16[576,128]{1,0:T(8,128)(2,1)S(1)}, u32[]{:S(2)}, u32[]{:S(2)}) collective-permute-start(bf16[576,128]{1,0:T(8,128)(2,1)S(1)} %get-tuple-element.92), channel_id=1, source_target_pairs={{32,35},{33,32},{34,33},{35,34},{36,39},{37,36},{38,37},{39,38},{4... | collective-permute-start | bytes 442376 | tf_op jit(solution)/shard_map/ppermute | solution.py:730
  46.5 0.0 copy-done.6
  46.5 0.0 copy-done.7
  46.5 0.0 collective-permute-done.7
  46.5 0.5 collective-permute-done.6
  47.1 1.5 %collective-permute-done.8 = bf16[576,128]{1,0:T(8,128)(2,1)S(1)} collective-permute-done((bf16[576,128]{1,0:T(8,128)(2,1)S(1)}, bf16[576,128]{1,0:T(8,128)(2,1)S(1)}, u32[]{:S(2)}, u32[]{:S(2)}) %collective-permute-start.8) | collective-permute-done | bytes 147488 | tf_op jit(solution)/shard_map/ppermute | solution.py:730
  48.6 0.1 add_convert_fusion.3.r_ref
  48.7 0.0 copy-done.5
  48.7 0.0 copy-done.2
  48.7 5.8 %back_project.1 = (f32[2,16,512]{2,1,0:T(8,128)S(1)}, bf16[512,128]{1,0:T(8,128)(2,1)S(1)}) custom-call(s32[3]{0:T(128)S(1)} %pad_add_fusion.place_ref, s32[256]{0:T(256)S(1)} %multiply_add_fusion.ray_ref, s32[256]{0:T(256)S(1)} %copy-done.5, bf16[512,128]{1,0:T(8,128)(2,1)S(1)} %add_convert_fusion.3.r_ref, ...), custom_call_target="tpu_custom_call" | custom-call | tf_op jit(solution)/shard_map/back_project/pallas_call | solution.py:311
  54.5 4.4 %collective-permute-start.9 = (bf16[512,128]{1,0:T(8,128)(2,1)S(1)}, bf16[512,128]{1,0:T(8,128)(2,1)S(1)}, u32[]{:S(2)}, u32[]{:S(2)}) collective-permute-start(bf16[512,128]{1,0:T(8,128)(2,1)S(1)} %get-tuple-element.74), channel_id=1, source_target_pairs={{32,48},{48,32},{33,49},{49,33},{34,50},{50,34},{35,51},{51,35},{3... | collective-permute-start | bytes 393224 | tf_op jit(solution)/shard_map/ppermute | solution.py:707
  58.9 0.0 copy-done
  58.9 2.6 %piece_0.1.net = f32[4,16,512]{2,1,0:T(8,128)S(1)} custom-call(s32[3]{0:T(128)S(1)} %pad_add_fusion.place_ref, bf16[256,128,128]{2,1,0:T(8,128)(2,1)S(1)} %get-tuple-element.72.blk, f32[4,16,512]{2,1,0:T(8,128)S(1)} %broadcast_in_dim.6.net, bf16[64,128]{1,0:T(8,128)(2,1)S(1)} %slice.76.before, bf16[64,128]{1,0:T(8,128)(2,1)S(1)} %slice.77.after, ...), custom_call_target="tpu_custom_call" | custom-call | tf_op jit(solution)/shard_map/piece_0/pallas_call | solution.py:669
  61.6 0.2 collective-permute-done.9
  61.8 3.3 %collective-permute-start.12 = (bf16[512,128]{1,0:T(8,128)(2,1)S(1)}, bf16[512,128]{1,0:T(8,128)(2,1)S(1)}, u32[]{:S(2)}, u32[]{:S(2)}) collective-permute-start(bf16[512,128]{1,0:T(8,128)(2,1)S(1)} %add_convert_fusion.2), channel_id=1, source_target_pairs={{32,44},{36,32},{40,36},{44,40},{33,45},{37,33},{41,37},{45,41},{3... | collective-permute-start | bytes 393224 | tf_op jit(solution)/shard_map/ppermute | solution.py:707
  65.1 2.3 %collective-permute-start.11 = (bf16[512,128]{1,0:T(8,128)(2,1)S(1)}, bf16[512,128]{1,0:T(8,128)(2,1)S(1)}, u32[]{:S(2)}, u32[]{:S(2)}) collective-permute-start(bf16[512,128]{1,0:T(8,128)(2,1)S(1)} %add_convert_fusion.2), channel_id=1, source_target_pairs={{32,40},{36,44},{40,32},{44,36},{33,41},{37,45},{41,33},{45,37},{3... | collective-permute-start | bytes 393224 | tf_op jit(solution)/shard_map/ppermute | solution.py:707
  67.4 2.6 %collective-permute-start.10 = (bf16[512,128]{1,0:T(8,128)(2,1)S(1)}, bf16[512,128]{1,0:T(8,128)(2,1)S(1)}, u32[]{:S(2)}, u32[]{:S(2)}) collective-permute-start(bf16[512,128]{1,0:T(8,128)(2,1)S(1)} %add_convert_fusion.2), channel_id=1, source_target_pairs={{32,36},{36,40},{40,44},{44,32},{33,37},{37,41},{41,45},{45,33},{3... | collective-permute-start | bytes 393224 | tf_op jit(solution)/shard_map/ppermute | solution.py:707
  70.0 2.8 %piece_1.1.net = f32[4,16,512]{2,1,0:T(8,128)S(1)} custom-call(s32[3]{0:T(128)S(1)} %pad_add_fusion.place_ref, bf16[256,128,128]{2,1,0:T(8,128)(2,1)S(1)} %get-tuple-element.72.blk, f32[4,16,512]{2,1,0:T(8,128)S(1)} %piece_0.1.net, bf16[64,128]{1,0:T(8,128)(2,1)S(1)} %slice.76.before, bf16[64,128]{1,0:T(8,128)(2,1)S(1)} %slice.77.after, ...), custom_call_target="tpu_custom_call" | custom-call | tf_op jit(solution)/shard_map/piece_1/pallas_call | solution.py:669
  72.8 2.6 %piece_2.1.net = f32[4,16,512]{2,1,0:T(8,128)S(1)} custom-call(s32[3]{0:T(128)S(1)} %pad_add_fusion.place_ref, bf16[256,128,128]{2,1,0:T(8,128)(2,1)S(1)} %get-tuple-element.72.blk, f32[4,16,512]{2,1,0:T(8,128)S(1)} %piece_1.1.net, bf16[64,128]{1,0:T(8,128)(2,1)S(1)} %slice.76.before, bf16[64,128]{1,0:T(8,128)(2,1)S(1)} %slice.77.after, ...), custom_call_target="tpu_custom_call" | custom-call | tf_op jit(solution)/shard_map/piece_2/pallas_call | solution.py:669
  75.5 0.0 collective-permute-done.12
  75.5 0.0 collective-permute-done.11
  75.5 0.0 collective-permute-done.10
  75.5 0.1 add_convert_fusion.1
  75.6 5.0 %collective-permute-start.15 = (bf16[512,128]{1,0:T(8,128)(2,1)S(1)}, bf16[512,128]{1,0:T(8,128)(2,1)S(1)}, u32[]{:S(2)}, u32[]{:S(2)}) collective-permute-start(bf16[512,128]{1,0:T(8,128)(2,1)S(1)} %add_convert_fusion.1), channel_id=1, source_target_pairs={{32,35},{33,32},{34,33},{35,34},{36,39},{37,36},{38,37},{39,38},{4... | collective-permute-start | bytes 393224 | tf_op jit(solution)/shard_map/ppermute | solution.py:707
  80.6 1.9 %collective-permute-start.14 = (bf16[512,128]{1,0:T(8,128)(2,1)S(1)}, bf16[512,128]{1,0:T(8,128)(2,1)S(1)}, u32[]{:S(2)}, u32[]{:S(2)}) collective-permute-start(bf16[512,128]{1,0:T(8,128)(2,1)S(1)} %add_convert_fusion.1), channel_id=1, source_target_pairs={{32,34},{33,35},{34,32},{35,33},{36,38},{37,39},{38,36},{39,37},{4... | collective-permute-start | bytes 393224 | tf_op jit(solution)/shard_map/ppermute | solution.py:707
  82.5 2.5 %collective-permute-start.13 = (bf16[512,128]{1,0:T(8,128)(2,1)S(1)}, bf16[512,128]{1,0:T(8,128)(2,1)S(1)}, u32[]{:S(2)}, u32[]{:S(2)}) collective-permute-start(bf16[512,128]{1,0:T(8,128)(2,1)S(1)} %add_convert_fusion.1), channel_id=1, source_target_pairs={{32,33},{33,34},{34,35},{35,32},{36,37},{37,38},{38,39},{39,36},{4... | collective-permute-start | bytes 393224 | tf_op jit(solution)/shard_map/ppermute | solution.py:707
  85.0 2.6 %piece_3.1.net_ref = f32[4,16,512]{2,1,0:T(8,128)S(1)} custom-call(s32[3]{0:T(128)S(1)} %pad_add_fusion.place_ref, bf16[256,128,128]{2,1,0:T(8,128)(2,1)S(1)} %get-tuple-element.72.blk, f32[4,16,512]{2,1,0:T(8,128)S(1)} %piece_2.1.net, bf16[64,128]{1,0:T(8,128)(2,1)S(1)} %slice.76.before, bf16[64,128]{1,0:T(8,128)(2,1)S(1)} %slice.77.after, ...), custom_call_target="tpu_custom_call" | custom-call | tf_op jit(solution)/shard_map/piece_3/pallas_call | solution.py:669
  87.7 0.0 collective-permute-done.15
  87.7 0.1 collective-permute-done.14
  87.8 1.6 %collective-permute-done.13 = bf16[512,128]{1,0:T(8,128)(2,1)S(1)} collective-permute-done((bf16[512,128]{1,0:T(8,128)(2,1)S(1)}, bf16[512,128]{1,0:T(8,128)(2,1)S(1)}, u32[]{:S(2)}, u32[]{:S(2)}) %collective-permute-start.13) | collective-permute-done | bytes 131104 | tf_op jit(solution)/shard_map/ppermute | solution.py:707
  89.4 0.1 add_convert_fusion.r_ref
  89.5 2.7 %back_reflect.1 = bf16[6,16,512]{2,1,0:T(8,128)(2,1)S(1)} custom-call(s32[256]{0:T(256)S(1)} %multiply_add_fusion.ray_ref, s32[256]{0:T(256)S(1)} %copy-done.5, bf16[512,128]{1,0:T(8,128)(2,1)S(1)} %add_convert_fusion.r_ref, f32[2,16,512]{2,1,0:T(8,128)S(1)} %get-tuple-element.87.x_ref, f32[2,16,512]{2,1,0:T(8,128)S(1)} %get-tuple-element.71.x_ref.start_ref, ...), custom_call_target="tpu_custom_call" | custom-call | tf_op jit(solution)/shard_map/back_reflect/pallas_call | solution.py:344
  92.3 6.9 %all-gather = bf16[24,16,512]{2,1,0:T(8,128)(2,1)S(1)} all-gather(bf16[6,16,512]{2,1,0:T(8,128)(2,1)S(1)} %back_reflect.1), channel_id=2, replica_groups=mesh['agent'=4,'tile'=32] {'agent'}, dimensions={0}, use_global_device_ids=true | all-gather | bytes 491520 | tf_op jit(solution)/shard_map/all_gather | solution.py:795
  99.2 1.3 %finish.1 = f32[4,16,512]{2,1,0:T(8,128)} custom-call(s32[3]{0:T(128)S(1)} %pad_add_fusion.place_ref, bf16[4,6,16,512]{3,2,1,0:T(8,128)(2,1)S(1)} %bitcast.15, f32[4,16,512]{2,1,0:T(8,128)S(1)} %bitcast.14, f32[4,16,512]{2,1,0:T(8,128)S(1)} %piece_3.1.net_ref), custom_call_target="tpu_custom_call" | custom-call | tf_op jit(solution)/shard_map/finish/pallas_call | solution.py:375
  (10 shorter events, 0.2 us)
Async XLA Ops:
  0.0 48.7 %copy-start.5 = (s32[256]{0:T(256)S(1)}, s32[256]{0:T(256)}, u32[]{:S(2)}) copy-start(s32[256]{0:T(256)} %tile_ref.3) | copy-start | bytes 3076
  0.0 46.5 %copy-start.6 = (s32[256]{0:T(256)S(1)}, s32[256]{0:T(256)}, u32[]{:S(2)}) copy-start(s32[256]{0:T(256)} %detector_in.1) | copy-start | bytes 3076
  0.0 46.5 %copy-start.7 = (s32[256]{0:T(256)S(1)}, s32[256]{0:T(256)}, u32[]{:S(2)}) copy-start(s32[256]{0:T(256)} %angle_in.1) | copy-start | bytes 3076
  0.0 48.7 %copy-start.2 = (f32[8,4,128]{2,1,0:T(4,128)S(1)}, f32[8,4,128]{2,1,0:T(4,128)}, u32[]{:S(2)}) copy-start(f32[8,4,128]{2,1,0:T(4,128)} %sino_ref.1) | copy-start | bytes 49156
  0.0 30.7 %copy-start.4 = (bf16[3,3,3,32]{3,2,1,0:T(4,128)(2,1)S(1)}, bf16[3,3,3,32]{3,2,1,0:T(4,128)(2,1)}, u32[]{:S(2)}) copy-start(bf16[3,3,3,32]{3,2,1,0:T(4,128)(2,1)} %last.1) | copy-start | bytes 5188
  0.0 30.7 %copy-start.1 = (bf16[3,2,3,3,32,32]{5,4,3,2,1,0:T(8,128)(2,1)S(1)}, bf16[3,2,3,3,32,32]{5,4,3,2,1,0:T(8,128)(2,1)}, u32[]{:S(2)}) copy-start(bf16[3,2,3,3,32,32]{5,4,3,2,1,0:T(8,128)(2,1)} %hidden.1) | copy-start | bytes 331780
  0.0 30.7 %copy-start.3 = (bf16[3,3,3,32]{3,2,1,0:T(4,128)(2,1)S(1)}, bf16[3,3,3,32]{3,2,1,0:T(4,128)(2,1)}, u32[]{:S(2)}) copy-start(bf16[3,3,3,32]{3,2,1,0:T(4,128)(2,1)} %first.1) | copy-start | bytes 5188
  1.0 2.1 %collective-permute-start.1 = (f32[2,16,512]{2,1,0:T(8,128)S(1)}, f32[2,16,512]{2,1,0:T(8,128)S(1)}, u32[]{:S(2)}, u32[]{:S(2)}) collective-permute-start(f32[2,16,512]{2,1,0:T(8,128)S(1)} %get-tuple-element.95), channel_id=1, source_target_pairs={{0,96},{1,97},{2,98},{3,99},{4,100},{5,101},{6,102},{7,103},{8,104... | collective-permute-start | bytes 196616 | tf_op jit(solution)/shard_map/ppermute | solution.py:742
  1.7 5.7 %collective-permute-start = (f32[2,16,512]{2,1,0:T(8,128)S(1)}, f32[2,16,512]{2,1,0:T(8,128)S(1)}, u32[]{:S(2)}, u32[]{:S(2)}) collective-permute-start(f32[2,16,512]{2,1,0:T(8,128)S(1)} %get-tuple-element.96), channel_id=1, source_target_pairs={{0,32},{1,33},{2,34},{3,35},{4,36},{5,37},{6,38},{7,39},{8,40},{9,... | collective-permute-start | bytes 196616 | tf_op jit(solution)/shard_map/ppermute | solution.py:742
  3.1 55.8 %copy-start = (f32[1,4,16,512]{3,2,1,0:T(8,128)S(1)}, f32[1,4,16,512]{3,2,1,0:T(8,128)}, u32[]{:S(2)}) copy-start(f32[1,4,16,512]{3,2,1,0:T(8,128)} %states_in.1) | copy-start | bytes 393220
  13.1 7.4 %collective-permute-start.2 = (bf16[576,128]{1,0:T(8,128)(2,1)S(1)}, bf16[576,128]{1,0:T(8,128)(2,1)S(1)}, u32[]{:S(2)}, u32[]{:S(2)}) collective-permute-start(bf16[576,128]{1,0:T(8,128)(2,1)S(1)} %get-tuple-element.49), channel_id=1, source_target_pairs={{32,48},{48,32},{33,49},{49,33},{34,50},{50,34},{35,51},{51,35},{3... | collective-permute-start | bytes 442376 | tf_op jit(solution)/shard_map/ppermute | solution.py:716
  20.5 13.8 %collective-permute-start.3 = (bf16[576,128]{1,0:T(8,128)(2,1)S(1)}, bf16[576,128]{1,0:T(8,128)(2,1)S(1)}, u32[]{:S(2)}, u32[]{:S(2)}) collective-permute-start(bf16[576,128]{1,0:T(8,128)(2,1)S(1)} %get-tuple-element.93), channel_id=1, source_target_pairs={{32,36},{36,40},{40,44},{44,32},{33,37},{37,41},{41,45},{45,33},{3... | collective-permute-start | bytes 442376 | tf_op jit(solution)/shard_map/ppermute | solution.py:728
  23.8 10.6 %collective-permute-start.5 = (bf16[576,128]{1,0:T(8,128)(2,1)S(1)}, bf16[576,128]{1,0:T(8,128)(2,1)S(1)}, u32[]{:S(2)}, u32[]{:S(2)}) collective-permute-start(bf16[576,128]{1,0:T(8,128)(2,1)S(1)} %get-tuple-element.94), channel_id=1, source_target_pairs={{32,44},{36,32},{40,36},{44,40},{33,45},{37,33},{41,37},{45,41},{3... | collective-permute-start | bytes 442376 | tf_op jit(solution)/shard_map/ppermute | solution.py:730
  27.1 7.2 %collective-permute-start.4 = (bf16[512,128]{1,0:T(8,128)(2,1)S(1)}, bf16[512,128]{1,0:T(8,128)(2,1)S(1)}, u32[]{:S(2)}, u32[]{:S(2)}) collective-permute-start(bf16[512,128]{1,0:T(8,128)(2,1)S(1)} %add_convert_fusion.5), channel_id=1, source_target_pairs={{32,40},{36,44},{40,32},{44,36},{33,41},{37,45},{41,33},{45,37},{3... | collective-permute-start | bytes 393224 | tf_op jit(solution)/shard_map/ppermute | solution.py:729
  34.4 12.1 %collective-permute-start.7 = (bf16[512,128]{1,0:T(8,128)(2,1)S(1)}, bf16[512,128]{1,0:T(8,128)(2,1)S(1)}, u32[]{:S(2)}, u32[]{:S(2)}) collective-permute-start(bf16[512,128]{1,0:T(8,128)(2,1)S(1)} %add_convert_fusion.4), channel_id=1, source_target_pairs={{32,34},{33,35},{34,32},{35,33},{36,38},{37,39},{38,36},{39,37},{4... | collective-permute-start | bytes 393224 | tf_op jit(solution)/shard_map/ppermute | solution.py:729
  40.0 7.1 %collective-permute-start.6 = (bf16[576,128]{1,0:T(8,128)(2,1)S(1)}, bf16[576,128]{1,0:T(8,128)(2,1)S(1)}, u32[]{:S(2)}, u32[]{:S(2)}) collective-permute-start(bf16[576,128]{1,0:T(8,128)(2,1)S(1)} %get-tuple-element.91), channel_id=1, source_target_pairs={{32,33},{33,34},{34,35},{35,32},{36,37},{37,38},{38,39},{39,36},{4... | collective-permute-start | bytes 442376 | tf_op jit(solution)/shard_map/ppermute | solution.py:728
  42.6 5.9 %collective-permute-start.8 = (bf16[576,128]{1,0:T(8,128)(2,1)S(1)}, bf16[576,128]{1,0:T(8,128)(2,1)S(1)}, u32[]{:S(2)}, u32[]{:S(2)}) collective-permute-start(bf16[576,128]{1,0:T(8,128)(2,1)S(1)} %get-tuple-element.92), channel_id=1, source_target_pairs={{32,35},{33,32},{34,33},{35,34},{36,39},{37,36},{38,37},{39,38},{4... | collective-permute-start | bytes 442376 | tf_op jit(solution)/shard_map/ppermute | solution.py:730
  54.5 7.2 %collective-permute-start.9 = (bf16[512,128]{1,0:T(8,128)(2,1)S(1)}, bf16[512,128]{1,0:T(8,128)(2,1)S(1)}, u32[]{:S(2)}, u32[]{:S(2)}) collective-permute-start(bf16[512,128]{1,0:T(8,128)(2,1)S(1)} %get-tuple-element.74), channel_id=1, source_target_pairs={{32,48},{48,32},{33,49},{49,33},{34,50},{50,34},{35,51},{51,35},{3... | collective-permute-start | bytes 393224 | tf_op jit(solution)/shard_map/ppermute | solution.py:707
  61.8 13.7 %collective-permute-start.12 = (bf16[512,128]{1,0:T(8,128)(2,1)S(1)}, bf16[512,128]{1,0:T(8,128)(2,1)S(1)}, u32[]{:S(2)}, u32[]{:S(2)}) collective-permute-start(bf16[512,128]{1,0:T(8,128)(2,1)S(1)} %add_convert_fusion.2), channel_id=1, source_target_pairs={{32,44},{36,32},{40,36},{44,40},{33,45},{37,33},{41,37},{45,41},{3... | collective-permute-start | bytes 393224 | tf_op jit(solution)/shard_map/ppermute | solution.py:707
  65.1 10.4 %collective-permute-start.11 = (bf16[512,128]{1,0:T(8,128)(2,1)S(1)}, bf16[512,128]{1,0:T(8,128)(2,1)S(1)}, u32[]{:S(2)}, u32[]{:S(2)}) collective-permute-start(bf16[512,128]{1,0:T(8,128)(2,1)S(1)} %add_convert_fusion.2), channel_id=1, source_target_pairs={{32,40},{36,44},{40,32},{44,36},{33,41},{37,45},{41,33},{45,37},{3... | collective-permute-start | bytes 393224 | tf_op jit(solution)/shard_map/ppermute | solution.py:707
  67.4 8.1 %collective-permute-start.10 = (bf16[512,128]{1,0:T(8,128)(2,1)S(1)}, bf16[512,128]{1,0:T(8,128)(2,1)S(1)}, u32[]{:S(2)}, u32[]{:S(2)}) collective-permute-start(bf16[512,128]{1,0:T(8,128)(2,1)S(1)} %add_convert_fusion.2), channel_id=1, source_target_pairs={{32,36},{36,40},{40,44},{44,32},{33,37},{37,41},{41,45},{45,33},{3... | collective-permute-start | bytes 393224 | tf_op jit(solution)/shard_map/ppermute | solution.py:707
  75.6 12.1 %collective-permute-start.15 = (bf16[512,128]{1,0:T(8,128)(2,1)S(1)}, bf16[512,128]{1,0:T(8,128)(2,1)S(1)}, u32[]{:S(2)}, u32[]{:S(2)}) collective-permute-start(bf16[512,128]{1,0:T(8,128)(2,1)S(1)} %add_convert_fusion.1), channel_id=1, source_target_pairs={{32,35},{33,32},{34,33},{35,34},{36,39},{37,36},{38,37},{39,38},{4... | collective-permute-start | bytes 393224 | tf_op jit(solution)/shard_map/ppermute | solution.py:707
  80.6 7.2 %collective-permute-start.14 = (bf16[512,128]{1,0:T(8,128)(2,1)S(1)}, bf16[512,128]{1,0:T(8,128)(2,1)S(1)}, u32[]{:S(2)}, u32[]{:S(2)}) collective-permute-start(bf16[512,128]{1,0:T(8,128)(2,1)S(1)} %add_convert_fusion.1), channel_id=1, source_target_pairs={{32,34},{33,35},{34,32},{35,33},{36,38},{37,39},{38,36},{39,37},{4... | collective-permute-start | bytes 393224 | tf_op jit(solution)/shard_map/ppermute | solution.py:707
  82.5 6.9 %collective-permute-start.13 = (bf16[512,128]{1,0:T(8,128)(2,1)S(1)}, bf16[512,128]{1,0:T(8,128)(2,1)S(1)}, u32[]{:S(2)}, u32[]{:S(2)}) collective-permute-start(bf16[512,128]{1,0:T(8,128)(2,1)S(1)} %add_convert_fusion.1), channel_id=1, source_target_pairs={{32,33},{33,34},{34,35},{35,32},{36,37},{37,38},{38,39},{39,36},{4... | collective-permute-start | bytes 393224 | tf_op jit(solution)/shard_map/ppermute | solution.py:707

commit v6 on v4

--- a/solution.py
+++ b/solution.py
@@ -12,7 +12,7 @@
 F32, BF16 = jnp.float32, jnp.bfloat16
 VMEM_LIMIT = 32 << 20
 TOGETHER = 4
-UNROLL = 16
+UNROLL = 64
 RIM = 4
 CHUNK = 64
 PIECES = ((0,), (1, 2), (3,))
@@ -54,7 +54,7 @@
     acc[index] = acc[index] + value
 
 
-def project_blocks(ray_of, tile_ref, pix, blk, acc, ready=None):
+def project_blocks(ray_of, tile_ref, pix, blk, acc, ready=None, unroll=UNROLL):
     low = low_rows()
     zero = jnp.zeros((8, 128), F32)
 
@@ -62,8 +62,8 @@
         if ready is not None:
             ready(i)
         outs = []
-        for u in range(UNROLL):
-            b = (i * UNROLL + u) * TOGETHER
+        for u in range(unroll):
+            b = (i * unroll + u) * TOGETHER
             t = [row(pix, tile_ref[b + k]) for k in range(TOGETHER)]
             upper = jnp.concatenate([jnp.where(low, t[0], t[1]), zero], axis=0)
             lower = jnp.concatenate([zero, jnp.where(low, t[2], t[3])], axis=0)
@@ -73,8 +73,8 @@
                     lhs, four_blocks(blk, b), (((1,), (1,)), ((), ())), preferred_element_type=F32
                 )
             )
-        for u in range(UNROLL):
-            b = (i * UNROLL + u) * TOGETHER
+        for u in range(unroll):
+            b = (i * unroll + u) * TOGETHER
             out = outs[u]
             add_rows(acc, ray_of(b), jnp.where(low, out[0:8, 0:128], 0.0))
             add_rows(acc, ray_of(b + 1), jnp.where(low, 0.0, out[0:8, 128:256]))
@@ -82,7 +82,7 @@
             add_rows(acc, ray_of(b + 3), jnp.where(low, 0.0, out[8:16, 128:256]))
         return carry
 
-    lax.fori_loop(0, blk.shape[0] // (TOGETHER * UNROLL), body, 0)
+    lax.fori_loop(0, blk.shape[0] // (TOGETHER * unroll), body, 0)
 
 
 def back_blocks(ray_ref, tile_ref, res, blk, acc):
@@ -163,6 +163,7 @@
     sino_in,
     blk_in,
     o_ref,
+    edge_ref,
     start_ref,
     blk,
     angle,
@@ -221,10 +222,22 @@
         def _():
             start_ref[...] = value[...]
 
+    tail = in_pieces(cur, cur.shape[1] - RIM).astype(BF16)
+    head = in_pieces(cur, 0).astype(BF16)
+    edge = tail.shape[0]
+    edge_ref[0:edge] = tail
+    edge_ref[edge:] = head
     rows = acc.shape[0]
-    edge = RIM * cur.shape[0] * cur.shape[2] // 128
-    o_ref[rows : rows + edge] = in_pieces(cur, cur.shape[1] - RIM).astype(BF16)
-    o_ref[rows + edge :] = in_pieces(cur, 0).astype(BF16)
+    at_end = (place_ref[1] // 4) % 4 == 3
+
+    @pl.when(at_end)
+    def _():
+        o_ref[rows:] = tail
+
+    @pl.when(jnp.logical_not(at_end))
+    def _():
+        o_ref[rows:] = head
+
     load_pixels(start_ref[...], pix)
     wide = cur.shape[2] // 128
     project_blocks(
@@ -234,6 +247,7 @@
         blk,
         acc,
         ready,
+        CHUNK // TOGETHER,
     )
     store_rays(place_ref, sino, acc, total, o_ref)
 
@@ -247,12 +261,13 @@
     return pl.pallas_call(
         project_kernel,
         out_shape=(
-            jax.ShapeDtypeStruct((ray_total + 2 * edge, 128), BF16),
+            jax.ShapeDtypeStruct((ray_total + edge, 128), BF16),
+            jax.ShapeDtypeStruct((2 * edge, 128), BF16),
             jax.ShapeDtypeStruct(shape, F32),
             pltpu.VMEM(blocks.shape, BF16),
         ),
         in_specs=[in_smem()] + [far] * 4 + [in_vmem()] * 3 + [far] * 2,
-        out_specs=(in_vmem(),) * 3,
+        out_specs=(in_vmem(),) * 4,
         scratch_shapes=[
             pltpu.SMEM((count,), jnp.int32),
             pltpu.SMEM((count,), jnp.int32),
@@ -662,23 +677,23 @@
 
 def added_up(values, groups):
     total = values.astype(F32)
-    for k in range(1, len(groups[0])):
+    for k in [k for k in (1, 3, 2) if k < len(groups[0])]:
         total = total + lax.ppermute(values, "tile", swapped(groups, k)).astype(F32)
     return total.astype(values.dtype)
 
 
-def added_up_with_rims(sums, groups, ends):
+def added_up_with_rims(first, own, groups, ends):
     far, strided, near = groups
-    rows = sums.shape[0] * 2 // 3
-    edge = (sums.shape[0] - rows) // 2
-    got = lax.ppermute(sums, "tile", swapped(far, 1))
-    tail, head = sums[rows : rows + edge], sums[rows + edge :]
-    onward, backward = got[rows : rows + edge], got[rows + edge :]
-    sums = (sums[0:rows].astype(F32) + got[0:rows].astype(F32)).astype(BF16)
+    edge = own.shape[0] // 2
+    rows = first.shape[0] - edge
+    got = lax.ppermute(first, "tile", swapped(far, 1))
+    tail, head = own[0:edge], own[edge:]
+    onward = backward = got[rows:]
+    sums = (first[0:rows].astype(F32) + got[0:rows].astype(F32)).astype(BF16)
     for n, group in enumerate((strided, near)):
-        first, last = ends[n]
-        onward = jnp.where(last, onward, tail)
-        backward = jnp.where(first, backward, head)
+        at_first, at_last = ends[n]
+        onward = jnp.where(at_last, onward, tail)
+        backward = jnp.where(at_first, backward, head)
         sums, onward, backward = lax.optimization_barrier((sums, onward, backward))
         up = lax.ppermute(jnp.concatenate([sums, onward]), "tile", swapped(group, 1))
         across = lax.ppermute(sums, "tile", swapped(group, 2))
@@ -716,14 +731,14 @@
     within = [lax.shift_right_logical(tile_place, 2) & 3, tile_place & 3]
     ends = [(at == 0, at == 3) for at in within]
     got, ends = lax.optimization_barrier((slices_sent(current), ends))
-    sums, start, blocks_here = project(
+    first, own, start, blocks_here = project(
         place, block_angle, block_detector, block_tile, states, got, sinogram, blocks, ray_total
     )
 
     groups = stage_groups(tile_count)
     net = jnp.zeros_like(current)
     x_data = start
-    sums, rim = added_up_with_rims(sums, groups, ends)
+    sums, rim = added_up_with_rims(first, own, groups, ends)
     for _ in range(DATA_STEPS - 2):
         x_data, sums = back_project(
             place, ray_index, block_tile, sums, x_data, sinogram, blocks_here

time: 78.7 us -> 77.3 us (0.982)
  waiting for transfers between devices: 15.7 us -> 14.8 us
  transfers between devices with their start and end apart: 17 -> 17, of which waited for: 6 -> 5; matrix products, arithmetic and copies ran while one was open for 0% -> 0% of each run, Pallas kernels for 15% -> 15%
where the time goes in v6:
time: 77.3 us; the launch traced here: 77.1 us
  Pallas kernels  25.4 us (33%)
  starting transfers between devices  24.4 us (32%)
  waiting for transfers between devices  14.8 us (19%)
  blocking collectives  11 us (14%)
  local copies, waits for them, and re-layouts  0.87 us (1%)
    all_gather x1, blocking collectives, per_device(): everything = lax.all_gather(sent, 'agent')  11 us
    pallas_call x4, Pallas kernels, piece(): pl.pallas_call(functools.partial(piece_kernel, k), out_shape=jax.ShapeDty...  10.7 us
    ppermute x7, starting transfers between devices, added_up(): total = total + lax.ppermute(values, 'tile', swapped(groups, k)).astype(F32)  8.41 us
    pallas_call x1, Pallas kernels, project(): pl.pallas_call(project_kernel, out_shape=(jax.ShapeDtypeStruct((ray_total...  5.56 us
    ppermute x2, starting transfers between devices, added_up_with_rims(): across = lax.ppermute(sums, 'tile', swapped(group, 2))  5.24 us
    ppermute x3, waiting for transfers between devices, slices_sent(): lax.ppermute(current[k], 'agent', [(0, k)])  4.87 us
    pallas_call x1, Pallas kernels, back_project(): pl.pallas_call(back_project_kernel, out_shape=(jax.ShapeDtypeStruct(x.sha...  4.6 us
    ppermute x2, waiting for transfers between devices, added_up_with_rims(): across = lax.ppermute(sums, 'tile', swapped(group, 2))  3.49 us
  transfers between devices with their start and end apart: 17, of which 5 were waited for; matrix products, arithmetic and copies ran while one was open for 0% of the time, Pallas kernels for 15%

profile of v6, /device:TPU:1, one launch (start us, length us, event | category | flops | bytes accessed | tf_op | source)
XLA Modules:
  0.0 77.1 jit_solution(139952753139563469)
XLA Ops:
  0.0 0.0 copy-start.5
  0.0 0.0 copy-start.6
  0.0 0.0 copy-start.7
  0.0 0.0 copy-start.2
  0.0 0.8 %slice_bitcast_fusion = (f32[16,512]{1,0:T(8,128)S(1)}, f32[16,512]{1,0:T(8,128)S(1)}, f32[16,512]{1,0:T(8,128)S(1)}) fusion(f32[1,4,16,512]{3,2,1,0:T(8,128)} %states_in.1), kind=kLoop, calls=%fused_computation.10 | loop fusion | bytes 196608 | tf_op jit(solution)/shard_map/squeeze | solution.py:709
  0.8 0.7 collective-permute-start.2
  1.5 0.7 collective-permute-start.1
  2.2 1.3 %collective-permute-start = (f32[16,512]{1,0:T(8,128)S(1)}, f32[16,512]{1,0:T(8,128)S(1)}, u32[]{:S(2)}, u32[]{:S(2)}) collective-permute-start(f32[16,512]{1,0:T(8,128)S(1)} %get-tuple-element.75), channel_id=1, source_target_pairs={{0,32},{1,33},{2,34},{3,35},{4,36},{5,37},{6,38},{7,39},{8,40},{9,... | collective-permute-start | bytes 98312 | tf_op jit(solution)/shard_map/ppermute | solution.py:709
  3.5 0.1 pad_add_fusion.place_ref
  3.6 0.0 copy-start
  3.6 0.0 copy-start.1
  3.6 0.0 copy-start.3
  3.6 0.0 copy-start.4
  3.6 0.0 collective-permute-done.2.got_3
  3.6 0.0 collective-permute-done.1.got_2
  3.6 4.9 %collective-permute-done.got_1 = f32[16,512]{1,0:T(8,128)S(1)} collective-permute-done((f32[16,512]{1,0:T(8,128)S(1)}, f32[16,512]{1,0:T(8,128)S(1)}, u32[]{:S(2)}, u32[]{:S(2)}) %collective-permute-start) | collective-permute-done | bytes 32800 | tf_op jit(solution)/shard_map/ppermute | solution.py:709
  8.5 5.6 %project.1 = (bf16[320,128]{1,0:T(8,128)(2,1)S(1)}, bf16[128,128]{1,0:T(8,128)(2,1)S(1)}, f32[16,512]{1,0:T(8,128)S(1)}, bf16[256,128,128]{2,1,0:T(8,128)(2,1)S(1)}) custom-call(s32[3]{0:T(128)S(1)} %pad_add_fusion.place_ref, s32[256]{0:T(256)} %angle_in.1, s32[256]{0:T(256)} %detector_in.1, s32[256]{0:T(256)} %tile_ref.3, f32[1,4,16,512]{3,2,1,0:T(8,128)} %states_in.1, ...), custom_call_target="tpu_custom_call" | custom-call | tf_op jit(solution)/shard_map/project/pallas_call | solution.py:261
  14.0 2.5 %collective-permute-start.3 = (bf16[320,128]{1,0:T(8,128)(2,1)S(1)}, bf16[320,128]{1,0:T(8,128)(2,1)S(1)}, u32[]{:S(2)}, u32[]{:S(2)}) collective-permute-start(bf16[320,128]{1,0:T(8,128)(2,1)S(1)} %get-tuple-element.42), channel_id=1, source_target_pairs={{0,16},{16,0},{1,17},{17,1},{2,18},{18,2},{3,19},{19,3},{4,20},{20... | collective-permute-start | bytes 245768 | tf_op jit(solution)/shard_map/ppermute | solution.py:689
  16.6 2.9 %collective-permute-done.3 = bf16[320,128]{1,0:T(8,128)(2,1)S(1)} collective-permute-done((bf16[320,128]{1,0:T(8,128)(2,1)S(1)}, bf16[320,128]{1,0:T(8,128)(2,1)S(1)}, u32[]{:S(2)}, u32[]{:S(2)}) %collective-permute-start.3) | collective-permute-done | bytes 81952 | tf_op jit(solution)/shard_map/ppermute | solution.py:689
  19.6 1.4 %collective-permute-start.4 = (bf16[320,128]{1,0:T(8,128)(2,1)S(1)}, bf16[320,128]{1,0:T(8,128)(2,1)S(1)}, u32[]{:S(2)}, u32[]{:S(2)}) collective-permute-start(bf16[320,128]{1,0:T(8,128)(2,1)S(1)} %get-tuple-element.80), channel_id=1, source_target_pairs={{0,4},{4,8},{8,12},{12,0},{1,5},{5,9},{9,13},{13,1},{2,6},{6,10},{... | collective-permute-start | bytes 245768 | tf_op jit(solution)/shard_map/ppermute | solution.py:698
  20.9 1.5 %collective-permute-start.6 = (bf16[320,128]{1,0:T(8,128)(2,1)S(1)}, bf16[320,128]{1,0:T(8,128)(2,1)S(1)}, u32[]{:S(2)}, u32[]{:S(2)}) collective-permute-start(bf16[320,128]{1,0:T(8,128)(2,1)S(1)} %get-tuple-element.81), channel_id=1, source_target_pairs={{0,12},{4,0},{8,4},{12,8},{1,13},{5,1},{9,5},{13,9},{2,14},{6,2},{... | collective-permute-start | bytes 245768 | tf_op jit(solution)/shard_map/ppermute | solution.py:700
  22.4 1.6 %collective-permute-start.5 = (bf16[256,128]{1,0:T(8,128)(2,1)S(1)}, bf16[256,128]{1,0:T(8,128)(2,1)S(1)}, u32[]{:S(2)}, u32[]{:S(2)}) collective-permute-start(bf16[256,128]{1,0:T(8,128)(2,1)S(1)} %add_convert_fusion.5), channel_id=1, source_target_pairs={{0,8},{4,12},{8,0},{12,4},{1,9},{5,13},{9,1},{13,5},{2,10},{6,14},... | collective-permute-start | bytes 196616 | tf_op jit(solution)/shard_map/ppermute | solution.py:699
  24.0 3.5 %collective-permute-done.5 = bf16[256,128]{1,0:T(8,128)(2,1)S(1)} collective-permute-done((bf16[256,128]{1,0:T(8,128)(2,1)S(1)}, bf16[256,128]{1,0:T(8,128)(2,1)S(1)}, u32[]{:S(2)}, u32[]{:S(2)}) %collective-permute-start.5) | collective-permute-done | bytes 65568 | tf_op jit(solution)/shard_map/ppermute | solution.py:699
  27.5 0.0 collective-permute-done.4
  27.5 0.0 collective-permute-done.6
  27.6 3.7 %collective-permute-start.8 = (bf16[256,128]{1,0:T(8,128)(2,1)S(1)}, bf16[256,128]{1,0:T(8,128)(2,1)S(1)}, u32[]{:S(2)}, u32[]{:S(2)}) collective-permute-start(bf16[256,128]{1,0:T(8,128)(2,1)S(1)} %add_convert_fusion.4), channel_id=1, source_target_pairs={{0,2},{1,3},{2,0},{3,1},{4,6},{5,7},{6,4},{7,5},{8,10},{9,11},{10,... | collective-permute-start | bytes 196616 | tf_op jit(solution)/shard_map/ppermute | solution.py:699
  31.3 0.8 %collective-permute-start.7 = (bf16[320,128]{1,0:T(8,128)(2,1)S(1)}, bf16[320,128]{1,0:T(8,128)(2,1)S(1)}, u32[]{:S(2)}, u32[]{:S(2)}) collective-permute-start(bf16[320,128]{1,0:T(8,128)(2,1)S(1)} %get-tuple-element.78), channel_id=1, source_target_pairs={{0,1},{1,2},{2,3},{3,0},{4,5},{5,6},{6,7},{7,4},{8,9},{9,10},{10,1... | collective-permute-start | bytes 245768 | tf_op jit(solution)/shard_map/ppermute | solution.py:698
  32.1 1.9 %collective-permute-start.9 = (bf16[320,128]{1,0:T(8,128)(2,1)S(1)}, bf16[320,128]{1,0:T(8,128)(2,1)S(1)}, u32[]{:S(2)}, u32[]{:S(2)}) collective-permute-start(bf16[320,128]{1,0:T(8,128)(2,1)S(1)} %get-tuple-element.79), channel_id=1, source_target_pairs={{0,3},{1,0},{2,1},{3,2},{4,7},{5,4},{6,5},{7,6},{8,11},{9,8},{10,9... | collective-permute-start | bytes 245768 | tf_op jit(solution)/shard_map/ppermute | solution.py:700
  34.0 0.0 copy-done.6
  34.0 0.0 copy-done.7
  34.0 0.0 collective-permute-done.8
  34.0 2.2 %collective-permute-done.7 = bf16[320,128]{1,0:T(8,128)(2,1)S(1)} collective-permute-done((bf16[320,128]{1,0:T(8,128)(2,1)S(1)}, bf16[320,128]{1,0:T(8,128)(2,1)S(1)}, u32[]{:S(2)}, u32[]{:S(2)}) %collective-permute-start.7) | collective-permute-done | bytes 81952 | tf_op jit(solution)/shard_map/ppermute | solution.py:698
  36.3 0.0 collective-permute-done.9
  36.3 0.0 copy-done.5
  36.3 0.0 copy-done.2
  36.3 4.6 %back_project.1 = (f32[16,512]{1,0:T(8,128)S(1)}, bf16[256,128]{1,0:T(8,128)(2,1)S(1)}) custom-call(s32[3]{0:T(128)S(1)} %pad_add_fusion.place_ref, s32[256]{0:T(256)S(1)} %multiply_add_fusion.ray_ref, s32[256]{0:T(256)S(1)} %copy-done.5, bf16[256,128]{1,0:T(8,128)(2,1)S(1)} %add_convert_fusion.3.r_ref, f32[16,512]{1,0:T(8,128)S(1)} %get-tuple-element.54.x_ref.start_ref, ...), custom_call_target="tpu_custom_call" | custom-call | tf_op jit(solution)/shard_map/back_project/pallas_call | solution.py:314
  40.9 2.5 %collective-permute-start.10 = (bf16[256,128]{1,0:T(8,128)(2,1)S(1)}, bf16[256,128]{1,0:T(8,128)(2,1)S(1)}, u32[]{:S(2)}, u32[]{:S(2)}) collective-permute-start(bf16[256,128]{1,0:T(8,128)(2,1)S(1)} %get-tuple-element.57), channel_id=1, source_target_pairs={{0,16},{16,0},{1,17},{17,1},{2,18},{18,2},{3,19},{19,3},{4,20},{20... | collective-permute-start | bytes 196616 | tf_op jit(solution)/shard_map/ppermute | solution.py:681
  43.5 0.0 copy-done
  43.5 0.0 copy-done.1
  43.5 0.0 copy-done.3
  43.5 0.0 copy-done.4
  43.5 1.1 %prepare.1 = (f32[4,24,512]{2,1,0:T(8,128)S(1)}, bf16[128,16]{1,0:T(8,128)(2,1)S(1)}, bf16[2,128,384]{2,1,0:T(8,128)(2,1)S(1)}, bf16[8,384]{1,0:T(8,128)(2,1)S(1...) custom-call(s32[3]{0:T(128)S(1)} %pad_add_fusion.place_ref, ...), custom_call_target="tpu_custom_call" | custom-call | tf_op jit(solution)/shard_map/prepare/pallas_call | solution.py:499
  44.7 2.7 %piece_0.1.net = f32[4,16,512]{2,1,0:T(8,128)S(1)} custom-call(s32[3]{0:T(128)S(1)} %pad_add_fusion.place_ref, bf16[256,128,128]{2,1,0:T(8,128)(2,1)S(1)} %get-tuple-element.55.blk, f32[4,16,512]{2,1,0:T(8,128)S(1)} %broadcast_in_dim.6.net, f32[4,24,512]{2,1,0:T(8,128)S(1)} %get-tuple-element.59.rim, bf16[128,16]{1,0:T(8,128)(2,1)S(1)} %get-tuple-element.60.zf, ...), custom_call_target="tpu_custom_call" | custom-call | tf_op jit(solution)/shard_map/piece_0/pallas_call | solution.py:649
  47.4 0.0 collective-permute-done.10
  47.5 1.5 %collective-permute-start.13 = (bf16[256,128]{1,0:T(8,128)(2,1)S(1)}, bf16[256,128]{1,0:T(8,128)(2,1)S(1)}, u32[]{:S(2)}, u32[]{:S(2)}) collective-permute-start(bf16[256,128]{1,0:T(8,128)(2,1)S(1)} %add_convert_fusion.2), channel_id=1, source_target_pairs={{0,8},{4,12},{8,0},{12,4},{1,9},{5,13},{9,1},{13,5},{2,10},{6,14},... | collective-permute-start | bytes 196616 | tf_op jit(solution)/shard_map/ppermute | solution.py:681
  48.9 0.9 %collective-permute-start.12 = (bf16[256,128]{1,0:T(8,128)(2,1)S(1)}, bf16[256,128]{1,0:T(8,128)(2,1)S(1)}, u32[]{:S(2)}, u32[]{:S(2)}) collective-permute-start(bf16[256,128]{1,0:T(8,128)(2,1)S(1)} %add_convert_fusion.2), channel_id=1, source_target_pairs={{0,12},{4,0},{8,4},{12,8},{1,13},{5,1},{9,5},{13,9},{2,14},{6,2},{... | collective-permute-start | bytes 196616 | tf_op jit(solution)/shard_map/ppermute | solution.py:681
  49.8 0.6 collective-permute-start.11
  50.4 2.6 %piece_1.1.net = f32[4,16,512]{2,1,0:T(8,128)S(1)} custom-call(s32[3]{0:T(128)S(1)} %pad_add_fusion.place_ref, bf16[256,128,128]{2,1,0:T(8,128)(2,1)S(1)} %get-tuple-element.55.blk, f32[4,16,512]{2,1,0:T(8,128)S(1)} %piece_0.1.net, f32[4,24,512]{2,1,0:T(8,128)S(1)} %get-tuple-element.59.rim, bf16[128,16]{1,0:T(8,128)(2,1)S(1)} %get-tuple-element.60.zf, ...), custom_call_target="tpu_custom_call" | custom-call | tf_op jit(solution)/shard_map/piece_1/pallas_call | solution.py:649
  53.0 2.8 %piece_2.1.net = f32[4,16,512]{2,1,0:T(8,128)S(1)} custom-call(s32[3]{0:T(128)S(1)} %pad_add_fusion.place_ref, bf16[256,128,128]{2,1,0:T(8,128)(2,1)S(1)} %get-tuple-element.55.blk, f32[4,16,512]{2,1,0:T(8,128)S(1)} %piece_1.1.net, f32[4,24,512]{2,1,0:T(8,128)S(1)} %get-tuple-element.59.rim, bf16[128,16]{1,0:T(8,128)(2,1)S(1)} %get-tuple-element.60.zf, ...), custom_call_target="tpu_custom_call" | custom-call | tf_op jit(solution)/shard_map/piece_2/pallas_call | solution.py:649
  55.8 0.0 collective-permute-done.13
  55.8 0.0 collective-permute-done.12
  55.8 0.0 collective-permute-done.11
  55.8 1.2 %collective-permute-start.16 = (bf16[256,128]{1,0:T(8,128)(2,1)S(1)}, bf16[256,128]{1,0:T(8,128)(2,1)S(1)}, u32[]{:S(2)}, u32[]{:S(2)}) collective-permute-start(bf16[256,128]{1,0:T(8,128)(2,1)S(1)} %add_convert_fusion.1), channel_id=1, source_target_pairs={{0,2},{1,3},{2,0},{3,1},{4,6},{5,7},{6,4},{7,5},{8,10},{9,11},{10,... | collective-permute-start | bytes 196616 | tf_op jit(solution)/shard_map/ppermute | solution.py:681
  57.0 1.3 %collective-permute-start.15 = (bf16[256,128]{1,0:T(8,128)(2,1)S(1)}, bf16[256,128]{1,0:T(8,128)(2,1)S(1)}, u32[]{:S(2)}, u32[]{:S(2)}) collective-permute-start(bf16[256,128]{1,0:T(8,128)(2,1)S(1)} %add_convert_fusion.1), channel_id=1, source_target_pairs={{0,3},{1,0},{2,1},{3,2},{4,7},{5,4},{6,5},{7,6},{8,11},{9,8},{10,9... | collective-permute-start | bytes 196616 | tf_op jit(solution)/shard_map/ppermute | solution.py:681
  58.3 0.5 collective-permute-start.14
  58.8 2.6 %piece_3.1.net_ref = f32[4,16,512]{2,1,0:T(8,128)S(1)} custom-call(s32[3]{0:T(128)S(1)} %pad_add_fusion.place_ref, bf16[256,128,128]{2,1,0:T(8,128)(2,1)S(1)} %get-tuple-element.55.blk, f32[4,16,512]{2,1,0:T(8,128)S(1)} %piece_2.1.net, f32[4,24,512]{2,1,0:T(8,128)S(1)} %get-tuple-element.59.rim, bf16[128,16]{1,0:T(8,128)(2,1)S(1)} %get-tuple-element.60.zf, ...), custom_call_target="tpu_custom_call" | custom-call | tf_op jit(solution)/shard_map/piece_3/pallas_call | solution.py:649
  61.4 0.0 collective-permute-done.16
  61.4 0.0 collective-permute-done.15
  61.4 1.2 %collective-permute-done.14 = bf16[256,128]{1,0:T(8,128)(2,1)S(1)} collective-permute-done((bf16[256,128]{1,0:T(8,128)(2,1)S(1)}, bf16[256,128]{1,0:T(8,128)(2,1)S(1)}, u32[]{:S(2)}, u32[]{:S(2)}) %collective-permute-start.14) | collective-permute-done | bytes 65568 | tf_op jit(solution)/shard_map/ppermute | solution.py:681
  62.6 2.1 %back_reflect.1 = bf16[5,16,512]{2,1,0:T(8,128)(2,1)S(1)} custom-call(s32[256]{0:T(256)S(1)} %multiply_add_fusion.ray_ref, s32[256]{0:T(256)S(1)} %copy-done.5, bf16[256,128]{1,0:T(8,128)(2,1)S(1)} %add_convert_fusion.r_ref, f32[16,512]{1,0:T(8,128)S(1)} %get-tuple-element.71.x_ref, f32[16,512]{1,0:T(8,128)S(1)} %get-tuple-element.54.x_ref.start_ref, ...), custom_call_target="tpu_custom_call" | custom-call | tf_op jit(solution)/shard_map/back_reflect/pallas_call | solution.py:345
  64.8 11.0 %all-gather = bf16[20,16,512]{2,1,0:T(8,128)(2,1)S(1)} all-gather(bf16[5,16,512]{2,1,0:T(8,128)(2,1)S(1)} %back_reflect.1), channel_id=2, replica_groups=mesh['agent'=4,'tile'=32] {'agent'}, dimensions={0}, use_global_device_ids=true | all-gather | bytes 409600 | tf_op jit(solution)/shard_map/all_gather | solution.py:757
  75.8 1.3 %finish.1 = f32[4,16,512]{2,1,0:T(8,128)} custom-call(s32[3]{0:T(128)S(1)} %pad_add_fusion.place_ref, bf16[4,5,16,512]{3,2,1,0:T(8,128)(2,1)S(1)} %bitcast.14, f32[4,16,512]{2,1,0:T(8,128)S(1)} %bitcast.13, f32[4,16,512]{2,1,0:T(8,128)S(1)} %piece_3.1.net_ref), custom_call_target="tpu_custom_call" | custom-call | tf_op jit(solution)/shard_map/finish/pallas_call | solution.py:376
  (14 shorter events, 0.3 us)
Async XLA Ops:
  0.0 36.3 %copy-start.5 = (s32[256]{0:T(256)S(1)}, s32[256]{0:T(256)}, u32[]{:S(2)}) copy-start(s32[256]{0:T(256)} %tile_ref.3) | copy-start | bytes 3076
  0.0 34.0 %copy-start.6 = (s32[256]{0:T(256)S(1)}, s32[256]{0:T(256)}, u32[]{:S(2)}) copy-start(s32[256]{0:T(256)} %detector_in.1) | copy-start | bytes 3076
  0.0 34.0 %copy-start.7 = (s32[256]{0:T(256)S(1)}, s32[256]{0:T(256)}, u32[]{:S(2)}) copy-start(s32[256]{0:T(256)} %angle_in.1) | copy-start | bytes 3076
  0.0 36.3 %copy-start.2 = (f32[8,4,128]{2,1,0:T(4,128)S(1)}, f32[8,4,128]{2,1,0:T(4,128)}, u32[]{:S(2)}) copy-start(f32[8,4,128]{2,1,0:T(4,128)} %sino_ref.1) | copy-start | bytes 49156
  0.8 2.7 %collective-permute-start.2 = (f32[16,512]{1,0:T(8,128)S(1)}, f32[16,512]{1,0:T(8,128)S(1)}, u32[]{:S(2)}, u32[]{:S(2)}) collective-permute-start(f32[16,512]{1,0:T(8,128)S(1)} %get-tuple-element.73), channel_id=1, source_target_pairs={{0,96},{1,97},{2,98},{3,99},{4,100},{5,101},{6,102},{7,103},{8,104... | collective-permute-start | bytes 98312 | tf_op jit(solution)/shard_map/ppermute | solution.py:709
  1.5 2.1 %collective-permute-start.1 = (f32[16,512]{1,0:T(8,128)S(1)}, f32[16,512]{1,0:T(8,128)S(1)}, u32[]{:S(2)}, u32[]{:S(2)}) collective-permute-start(f32[16,512]{1,0:T(8,128)S(1)} %get-tuple-element.74), channel_id=1, source_target_pairs={{0,64},{1,65},{2,66},{3,67},{4,68},{5,69},{6,70},{7,71},{8,72},{9,... | collective-permute-start | bytes 98312 | tf_op jit(solution)/shard_map/ppermute | solution.py:709
  2.2 6.3 %collective-permute-start = (f32[16,512]{1,0:T(8,128)S(1)}, f32[16,512]{1,0:T(8,128)S(1)}, u32[]{:S(2)}, u32[]{:S(2)}) collective-permute-start(f32[16,512]{1,0:T(8,128)S(1)} %get-tuple-element.75), channel_id=1, source_target_pairs={{0,32},{1,33},{2,34},{3,35},{4,36},{5,37},{6,38},{7,39},{8,40},{9,... | collective-permute-start | bytes 98312 | tf_op jit(solution)/shard_map/ppermute | solution.py:709
  3.6 39.9 %copy-start = (f32[1,4,16,512]{3,2,1,0:T(8,128)S(1)}, f32[1,4,16,512]{3,2,1,0:T(8,128)}, u32[]{:S(2)}) copy-start(f32[1,4,16,512]{3,2,1,0:T(8,128)} %states_in.1) | copy-start | bytes 393220
  3.6 39.9 %copy-start.1 = (bf16[3,2,3,3,32,32]{5,4,3,2,1,0:T(8,128)(2,1)S(1)}, bf16[3,2,3,3,32,32]{5,4,3,2,1,0:T(8,128)(2,1)}, u32[]{:S(2)}) copy-start(bf16[3,2,3,3,32,32]{5,4,3,2,1,0:T(8,128)(2,1)} %hidden.1) | copy-start | bytes 331780
  3.6 39.9 %copy-start.3 = (bf16[3,3,3,32]{3,2,1,0:T(4,128)(2,1)S(1)}, bf16[3,3,3,32]{3,2,1,0:T(4,128)(2,1)}, u32[]{:S(2)}) copy-start(bf16[3,3,3,32]{3,2,1,0:T(4,128)(2,1)} %first.1) | copy-start | bytes 5188
  3.6 40.0 %copy-start.4 = (bf16[3,3,3,32]{3,2,1,0:T(4,128)(2,1)S(1)}, bf16[3,3,3,32]{3,2,1,0:T(4,128)(2,1)}, u32[]{:S(2)}) copy-start(bf16[3,3,3,32]{3,2,1,0:T(4,128)(2,1)} %last.1) | copy-start | bytes 5188
  14.0 5.5 %collective-permute-start.3 = (bf16[320,128]{1,0:T(8,128)(2,1)S(1)}, bf16[320,128]{1,0:T(8,128)(2,1)S(1)}, u32[]{:S(2)}, u32[]{:S(2)}) collective-permute-start(bf16[320,128]{1,0:T(8,128)(2,1)S(1)} %get-tuple-element.42), channel_id=1, source_target_pairs={{0,16},{16,0},{1,17},{17,1},{2,18},{18,2},{3,19},{19,3},{4,20},{20... | collective-permute-start | bytes 245768 | tf_op jit(solution)/shard_map/ppermute | solution.py:689
  19.6 7.9 %collective-permute-start.4 = (bf16[320,128]{1,0:T(8,128)(2,1)S(1)}, bf16[320,128]{1,0:T(8,128)(2,1)S(1)}, u32[]{:S(2)}, u32[]{:S(2)}) collective-permute-start(bf16[320,128]{1,0:T(8,128)(2,1)S(1)} %get-tuple-element.80), channel_id=1, source_target_pairs={{0,4},{4,8},{8,12},{12,0},{1,5},{5,9},{9,13},{13,1},{2,6},{6,10},{... | collective-permute-start | bytes 245768 | tf_op jit(solution)/shard_map/ppermute | solution.py:698
  20.9 6.6 %collective-permute-start.6 = (bf16[320,128]{1,0:T(8,128)(2,1)S(1)}, bf16[320,128]{1,0:T(8,128)(2,1)S(1)}, u32[]{:S(2)}, u32[]{:S(2)}) collective-permute-start(bf16[320,128]{1,0:T(8,128)(2,1)S(1)} %get-tuple-element.81), channel_id=1, source_target_pairs={{0,12},{4,0},{8,4},{12,8},{1,13},{5,1},{9,5},{13,9},{2,14},{6,2},{... | collective-permute-start | bytes 245768 | tf_op jit(solution)/shard_map/ppermute | solution.py:700
  22.4 5.1 %collective-permute-start.5 = (bf16[256,128]{1,0:T(8,128)(2,1)S(1)}, bf16[256,128]{1,0:T(8,128)(2,1)S(1)}, u32[]{:S(2)}, u32[]{:S(2)}) collective-permute-start(bf16[256,128]{1,0:T(8,128)(2,1)S(1)} %add_convert_fusion.5), channel_id=1, source_target_pairs={{0,8},{4,12},{8,0},{12,4},{1,9},{5,13},{9,1},{13,5},{2,10},{6,14},... | collective-permute-start | bytes 196616 | tf_op jit(solution)/shard_map/ppermute | solution.py:699
  27.6 6.5 %collective-permute-start.8 = (bf16[256,128]{1,0:T(8,128)(2,1)S(1)}, bf16[256,128]{1,0:T(8,128)(2,1)S(1)}, u32[]{:S(2)}, u32[]{:S(2)}) collective-permute-start(bf16[256,128]{1,0:T(8,128)(2,1)S(1)} %add_convert_fusion.4), channel_id=1, source_target_pairs={{0,2},{1,3},{2,0},{3,1},{4,6},{5,7},{6,4},{7,5},{8,10},{9,11},{10,... | collective-permute-start | bytes 196616 | tf_op jit(solution)/shard_map/ppermute | solution.py:699
  31.3 5.0 %collective-permute-start.7 = (bf16[320,128]{1,0:T(8,128)(2,1)S(1)}, bf16[320,128]{1,0:T(8,128)(2,1)S(1)}, u32[]{:S(2)}, u32[]{:S(2)}) collective-permute-start(bf16[320,128]{1,0:T(8,128)(2,1)S(1)} %get-tuple-element.78), channel_id=1, source_target_pairs={{0,1},{1,2},{2,3},{3,0},{4,5},{5,6},{6,7},{7,4},{8,9},{9,10},{10,1... | collective-permute-start | bytes 245768 | tf_op jit(solution)/shard_map/ppermute | solution.py:698
  32.1 4.2 %collective-permute-start.9 = (bf16[320,128]{1,0:T(8,128)(2,1)S(1)}, bf16[320,128]{1,0:T(8,128)(2,1)S(1)}, u32[]{:S(2)}, u32[]{:S(2)}) collective-permute-start(bf16[320,128]{1,0:T(8,128)(2,1)S(1)} %get-tuple-element.79), channel_id=1, source_target_pairs={{0,3},{1,0},{2,1},{3,2},{4,7},{5,4},{6,5},{7,6},{8,11},{9,8},{10,9... | collective-permute-start | bytes 245768 | tf_op jit(solution)/shard_map/ppermute | solution.py:700
  40.9 6.5 %collective-permute-start.10 = (bf16[256,128]{1,0:T(8,128)(2,1)S(1)}, bf16[256,128]{1,0:T(8,128)(2,1)S(1)}, u32[]{:S(2)}, u32[]{:S(2)}) collective-permute-start(bf16[256,128]{1,0:T(8,128)(2,1)S(1)} %get-tuple-element.57), channel_id=1, source_target_pairs={{0,16},{16,0},{1,17},{17,1},{2,18},{18,2},{3,19},{19,3},{4,20},{20... | collective-permute-start | bytes 196616 | tf_op jit(solution)/shard_map/ppermute | solution.py:681
  47.5 8.3 %collective-permute-start.13 = (bf16[256,128]{1,0:T(8,128)(2,1)S(1)}, bf16[256,128]{1,0:T(8,128)(2,1)S(1)}, u32[]{:S(2)}, u32[]{:S(2)}) collective-permute-start(bf16[256,128]{1,0:T(8,128)(2,1)S(1)} %add_convert_fusion.2), channel_id=1, source_target_pairs={{0,8},{4,12},{8,0},{12,4},{1,9},{5,13},{9,1},{13,5},{2,10},{6,14},... | collective-permute-start | bytes 196616 | tf_op jit(solution)/shard_map/ppermute | solution.py:681
  48.9 6.9 %collective-permute-start.12 = (bf16[256,128]{1,0:T(8,128)(2,1)S(1)}, bf16[256,128]{1,0:T(8,128)(2,1)S(1)}, u32[]{:S(2)}, u32[]{:S(2)}) collective-permute-start(bf16[256,128]{1,0:T(8,128)(2,1)S(1)} %add_convert_fusion.2), channel_id=1, source_target_pairs={{0,12},{4,0},{8,4},{12,8},{1,13},{5,1},{9,5},{13,9},{2,14},{6,2},{... | collective-permute-start | bytes 196616 | tf_op jit(solution)/shard_map/ppermute | solution.py:681
  49.8 6.0 %collective-permute-start.11 = (bf16[256,128]{1,0:T(8,128)(2,1)S(1)}, bf16[256,128]{1,0:T(8,128)(2,1)S(1)}, u32[]{:S(2)}, u32[]{:S(2)}) collective-permute-start(bf16[256,128]{1,0:T(8,128)(2,1)S(1)} %add_convert_fusion.2), channel_id=1, source_target_pairs={{0,4},{4,8},{8,12},{12,0},{1,5},{5,9},{9,13},{13,1},{2,6},{6,10},{... | collective-permute-start | bytes 196616 | tf_op jit(solution)/shard_map/ppermute | solution.py:681
  55.8 5.6 %collective-permute-start.16 = (bf16[256,128]{1,0:T(8,128)(2,1)S(1)}, bf16[256,128]{1,0:T(8,128)(2,1)S(1)}, u32[]{:S(2)}, u32[]{:S(2)}) collective-permute-start(bf16[256,128]{1,0:T(8,128)(2,1)S(1)} %add_convert_fusion.1), channel_id=1, source_target_pairs={{0,2},{1,3},{2,0},{3,1},{4,6},{5,7},{6,4},{7,5},{8,10},{9,11},{10,... | collective-permute-start | bytes 196616 | tf_op jit(solution)/shard_map/ppermute | solution.py:681
  57.0 4.4 %collective-permute-start.15 = (bf16[256,128]{1,0:T(8,128)(2,1)S(1)}, bf16[256,128]{1,0:T(8,128)(2,1)S(1)}, u32[]{:S(2)}, u32[]{:S(2)}) collective-permute-start(bf16[256,128]{1,0:T(8,128)(2,1)S(1)} %add_convert_fusion.1), channel_id=1, source_target_pairs={{0,3},{1,0},{2,1},{3,2},{4,7},{5,4},{6,5},{7,6},{8,11},{9,8},{10,9... | collective-permute-start | bytes 196616 | tf_op jit(solution)/shard_map/ppermute | solution.py:681
  58.3 4.3 %collective-permute-start.14 = (bf16[256,128]{1,0:T(8,128)(2,1)S(1)}, bf16[256,128]{1,0:T(8,128)(2,1)S(1)}, u32[]{:S(2)}, u32[]{:S(2)}) collective-permute-start(bf16[256,128]{1,0:T(8,128)(2,1)S(1)} %add_convert_fusion.1), channel_id=1, source_target_pairs={{0,1},{1,2},{2,3},{3,0},{4,5},{5,6},{6,7},{7,4},{8,9},{9,10},{10,1... | collective-permute-start | bytes 196616 | tf_op jit(solution)/shard_map/ppermute | solution.py:681

commit v7 on v6

--- a/solution.py
+++ b/solution.py
@@ -15,7 +15,7 @@
 UNROLL = 64
 RIM = 4
 CHUNK = 64
-PIECES = ((0,), (1, 2), (3,))
+PIECES = ((0,), (1,), (2, 3))
 SPAN = 6
 
 
@@ -692,9 +692,9 @@
     sums = (first[0:rows].astype(F32) + got[0:rows].astype(F32)).astype(BF16)
     for n, group in enumerate((strided, near)):
         at_first, at_last = ends[n]
+        sums, onward, backward = lax.optimization_barrier((sums, onward, backward))
         onward = jnp.where(at_last, onward, tail)
         backward = jnp.where(at_first, backward, head)
-        sums, onward, backward = lax.optimization_barrier((sums, onward, backward))
         up = lax.ppermute(jnp.concatenate([sums, onward]), "tile", swapped(group, 1))
         across = lax.ppermute(sums, "tile", swapped(group, 2))
         down = lax.ppermute(jnp.concatenate([sums, backward]), "tile", swapped(group, 3))

time: 77.3 us -> 77.3 us (level)
  transfers between devices with their start and end apart: 17 -> 17, of which waited for: 5 -> 6; matrix products, arithmetic and copies ran while one was open for 0% -> 0% of each run, Pallas kernels for 15% -> 15%
where the time goes in v7:
time: 77.3 us; the launch traced here: 77 us
  Pallas kernels  25.3 us (33%)
  starting transfers between devices  25 us (32%)
  waiting for transfers between devices  14.6 us (19%)
  blocking collectives  10.6 us (14%)
  local copies, waits for them, and re-layouts  0.88 us (1%)
    pallas_call x4, Pallas kernels, piece(): pl.pallas_call(functools.partial(piece_kernel, k), out_shape=jax.ShapeDty...  10.7 us
    all_gather x1, blocking collectives, per_device(): everything = lax.all_gather(sent, 'agent')  10.6 us
    ppermute x7, starting transfers between devices, added_up(): total = total + lax.ppermute(values, 'tile', swapped(groups, k)).astype(F32)  8.99 us
    pallas_call x1, Pallas kernels, project(): pl.pallas_call(project_kernel, out_shape=(jax.ShapeDtypeStruct((ray_total...  5.55 us
    ppermute x2, starting transfers between devices, added_up_with_rims(): across = lax.ppermute(sums, 'tile', swapped(group, 2))  5.24 us
    ppermute x3, waiting for transfers between devices, slices_sent(): lax.ppermute(current[k], 'agent', [(0, k)])  4.87 us
    pallas_call x1, Pallas kernels, back_project(): pl.pallas_call(back_project_kernel, out_shape=(jax.ShapeDtypeStruct(x.sha...  4.6 us
    ppermute x2, starting transfers between devices, added_up_with_rims(): lax.ppermute(jnp.concatenate([sums, backward]), 'tile', swapped(group, 3))  3.46 us
  transfers between devices with their start and end apart: 17, of which 6 were waited for; matrix products, arithmetic and copies ran while one was open for 0% of the time, Pallas kernels for 15%

profile of v7, /device:TPU:1, one launch (start us, length us, event | category | flops | bytes accessed | tf_op | source)
XLA Modules:
  0.0 77.0 jit_solution(9681944843647880207)
XLA Ops:
  0.0 0.0 copy-start.5
  0.0 0.0 copy-start.6
  0.0 0.0 copy-start.7
  0.0 0.0 copy-start.2
  0.0 0.8 %slice_bitcast_fusion = (f32[16,512]{1,0:T(8,128)S(1)}, f32[16,512]{1,0:T(8,128)S(1)}, f32[16,512]{1,0:T(8,128)S(1)}) fusion(f32[1,4,16,512]{3,2,1,0:T(8,128)} %states_in.1), kind=kLoop, calls=%fused_computation.10 | loop fusion | bytes 196608 | tf_op jit(solution)/shard_map/squeeze | solution.py:709
  0.8 0.7 collective-permute-start.2
  1.5 0.7 collective-permute-start.1
  2.2 1.3 %collective-permute-start = (f32[16,512]{1,0:T(8,128)S(1)}, f32[16,512]{1,0:T(8,128)S(1)}, u32[]{:S(2)}, u32[]{:S(2)}) collective-permute-start(f32[16,512]{1,0:T(8,128)S(1)} %get-tuple-element.75), channel_id=1, source_target_pairs={{0,32},{1,33},{2,34},{3,35},{4,36},{5,37},{6,38},{7,39},{8,40},{9,... | collective-permute-start | bytes 98312 | tf_op jit(solution)/shard_map/ppermute | solution.py:709
  3.5 0.1 pad_add_fusion.place_ref
  3.6 0.0 copy-start
  3.6 0.0 copy-start.1
  3.6 0.0 copy-start.3
  3.6 0.0 copy-start.4
  3.6 0.0 collective-permute-done.2.got_3
  3.6 0.0 collective-permute-done.1.got_2
  3.6 4.9 %collective-permute-done.got_1 = f32[16,512]{1,0:T(8,128)S(1)} collective-permute-done((f32[16,512]{1,0:T(8,128)S(1)}, f32[16,512]{1,0:T(8,128)S(1)}, u32[]{:S(2)}, u32[]{:S(2)}) %collective-permute-start) | collective-permute-done | bytes 32800 | tf_op jit(solution)/shard_map/ppermute | solution.py:709
  8.5 5.5 %project.1 = (bf16[320,128]{1,0:T(8,128)(2,1)S(1)}, bf16[128,128]{1,0:T(8,128)(2,1)S(1)}, f32[16,512]{1,0:T(8,128)S(1)}, bf16[256,128,128]{2,1,0:T(8,128)(2,1)S(1)}) custom-call(s32[3]{0:T(128)S(1)} %pad_add_fusion.place_ref, s32[256]{0:T(256)} %angle_in.1, s32[256]{0:T(256)} %detector_in.1, s32[256]{0:T(256)} %tile_ref.3, f32[1,4,16,512]{3,2,1,0:T(8,128)} %states_in.1, ...), custom_call_target="tpu_custom_call" | custom-call | tf_op jit(solution)/shard_map/project/pallas_call | solution.py:261
  14.0 2.5 %collective-permute-start.3 = (bf16[320,128]{1,0:T(8,128)(2,1)S(1)}, bf16[320,128]{1,0:T(8,128)(2,1)S(1)}, u32[]{:S(2)}, u32[]{:S(2)}) collective-permute-start(bf16[320,128]{1,0:T(8,128)(2,1)S(1)} %get-tuple-element.42), channel_id=1, source_target_pairs={{0,16},{16,0},{1,17},{17,1},{2,18},{18,2},{3,19},{19,3},{4,20},{20... | collective-permute-start | bytes 245768 | tf_op jit(solution)/shard_map/ppermute | solution.py:689
  16.6 2.9 %collective-permute-done.3 = bf16[320,128]{1,0:T(8,128)(2,1)S(1)} collective-permute-done((bf16[320,128]{1,0:T(8,128)(2,1)S(1)}, bf16[320,128]{1,0:T(8,128)(2,1)S(1)}, u32[]{:S(2)}, u32[]{:S(2)}) %collective-permute-start.3) | collective-permute-done | bytes 81952 | tf_op jit(solution)/shard_map/ppermute | solution.py:689
  19.6 1.4 %collective-permute-start.4 = (bf16[320,128]{1,0:T(8,128)(2,1)S(1)}, bf16[320,128]{1,0:T(8,128)(2,1)S(1)}, u32[]{:S(2)}, u32[]{:S(2)}) collective-permute-start(bf16[320,128]{1,0:T(8,128)(2,1)S(1)} %get-tuple-element.78), channel_id=1, source_target_pairs={{0,4},{4,8},{8,12},{12,0},{1,5},{5,9},{9,13},{13,1},{2,6},{6,10},{... | collective-permute-start | bytes 245768 | tf_op jit(solution)/shard_map/ppermute | solution.py:698
  20.9 1.5 %collective-permute-start.6 = (bf16[320,128]{1,0:T(8,128)(2,1)S(1)}, bf16[320,128]{1,0:T(8,128)(2,1)S(1)}, u32[]{:S(2)}, u32[]{:S(2)}) collective-permute-start(bf16[320,128]{1,0:T(8,128)(2,1)S(1)} %get-tuple-element.79), channel_id=1, source_target_pairs={{0,12},{4,0},{8,4},{12,8},{1,13},{5,1},{9,5},{13,9},{2,14},{6,2},{... | collective-permute-start | bytes 245768 | tf_op jit(solution)/shard_map/ppermute | solution.py:700
  22.5 1.6 %collective-permute-start.5 = (bf16[256,128]{1,0:T(8,128)(2,1)S(1)}, bf16[256,128]{1,0:T(8,128)(2,1)S(1)}, u32[]{:S(2)}, u32[]{:S(2)}) collective-permute-start(bf16[256,128]{1,0:T(8,128)(2,1)S(1)} %add_convert_fusion.5), channel_id=1, source_target_pairs={{0,8},{4,12},{8,0},{12,4},{1,9},{5,13},{9,1},{13,5},{2,10},{6,14},... | collective-permute-start | bytes 196616 | tf_op jit(solution)/shard_map/ppermute | solution.py:699
  24.0 0.2 collective-permute-done.4
  24.2 0.0 collective-permute-done.6
  24.2 3.3 %collective-permute-done.5 = bf16[256,128]{1,0:T(8,128)(2,1)S(1)} collective-permute-done((bf16[256,128]{1,0:T(8,128)(2,1)S(1)}, bf16[256,128]{1,0:T(8,128)(2,1)S(1)}, u32[]{:S(2)}, u32[]{:S(2)}) %collective-permute-start.5) | collective-permute-done | bytes 65568 | tf_op jit(solution)/shard_map/ppermute | solution.py:699
  27.6 3.7 %collective-permute-start.8 = (bf16[256,128]{1,0:T(8,128)(2,1)S(1)}, bf16[256,128]{1,0:T(8,128)(2,1)S(1)}, u32[]{:S(2)}, u32[]{:S(2)}) collective-permute-start(bf16[256,128]{1,0:T(8,128)(2,1)S(1)} %add_convert_fusion.4), channel_id=1, source_target_pairs={{0,2},{1,3},{2,0},{3,1},{4,6},{5,7},{6,4},{7,5},{8,10},{9,11},{10,... | collective-permute-start | bytes 196616 | tf_op jit(solution)/shard_map/ppermute | solution.py:699
  31.3 0.8 %collective-permute-start.7 = (bf16[320,128]{1,0:T(8,128)(2,1)S(1)}, bf16[320,128]{1,0:T(8,128)(2,1)S(1)}, u32[]{:S(2)}, u32[]{:S(2)}) collective-permute-start(bf16[320,128]{1,0:T(8,128)(2,1)S(1)} %get-tuple-element.76), channel_id=1, source_target_pairs={{0,1},{1,2},{2,3},{3,0},{4,5},{5,6},{6,7},{7,4},{8,9},{9,10},{10,1... | collective-permute-start | bytes 245768 | tf_op jit(solution)/shard_map/ppermute | solution.py:698
  32.1 1.9 %collective-permute-start.9 = (bf16[320,128]{1,0:T(8,128)(2,1)S(1)}, bf16[320,128]{1,0:T(8,128)(2,1)S(1)}, u32[]{:S(2)}, u32[]{:S(2)}) collective-permute-start(bf16[320,128]{1,0:T(8,128)(2,1)S(1)} %get-tuple-element.77), channel_id=1, source_target_pairs={{0,3},{1,0},{2,1},{3,2},{4,7},{5,4},{6,5},{7,6},{8,11},{9,8},{10,9... | collective-permute-start | bytes 245768 | tf_op jit(solution)/shard_map/ppermute | solution.py:700
  34.0 0.0 copy-done.6
  34.0 0.0 copy-done.7
  34.0 0.0 collective-permute-done.8
  34.0 2.2 %collective-permute-done.7 = bf16[320,128]{1,0:T(8,128)(2,1)S(1)} collective-permute-done((bf16[320,128]{1,0:T(8,128)(2,1)S(1)}, bf16[320,128]{1,0:T(8,128)(2,1)S(1)}, u32[]{:S(2)}, u32[]{:S(2)}) %collective-permute-start.7) | collective-permute-done | bytes 81952 | tf_op jit(solution)/shard_map/ppermute | solution.py:698
  36.3 0.0 collective-permute-done.9
  36.3 0.0 copy-done.5
  36.3 0.0 copy-done.2
  36.3 4.6 %back_project.1 = (f32[16,512]{1,0:T(8,128)S(1)}, bf16[256,128]{1,0:T(8,128)(2,1)S(1)}) custom-call(s32[3]{0:T(128)S(1)} %pad_add_fusion.place_ref, s32[256]{0:T(256)S(1)} %multiply_add_fusion.ray_ref, s32[256]{0:T(256)S(1)} %copy-done.5, bf16[256,128]{1,0:T(8,128)(2,1)S(1)} %add_convert_fusion.3.r_ref, f32[16,512]{1,0:T(8,128)S(1)} %get-tuple-element.54.x_ref.start_ref, ...), custom_call_target="tpu_custom_call" | custom-call | tf_op jit(solution)/shard_map/back_project/pallas_call | solution.py:314
  40.9 2.5 %collective-permute-start.10 = (bf16[256,128]{1,0:T(8,128)(2,1)S(1)}, bf16[256,128]{1,0:T(8,128)(2,1)S(1)}, u32[]{:S(2)}, u32[]{:S(2)}) collective-permute-start(bf16[256,128]{1,0:T(8,128)(2,1)S(1)} %get-tuple-element.57), channel_id=1, source_target_pairs={{0,16},{16,0},{1,17},{17,1},{2,18},{18,2},{3,19},{19,3},{4,20},{20... | collective-permute-start | bytes 196616 | tf_op jit(solution)/shard_map/ppermute | solution.py:681
  43.5 0.0 copy-done
  43.5 0.0 copy-done.1
  43.5 0.0 copy-done.3
  43.5 0.0 copy-done.4
  43.5 1.1 %prepare.1 = (f32[4,24,512]{2,1,0:T(8,128)S(1)}, bf16[128,16]{1,0:T(8,128)(2,1)S(1)}, bf16[2,128,384]{2,1,0:T(8,128)(2,1)S(1)}, bf16[8,384]{1,0:T(8,128)(2,1)S(1...) custom-call(s32[3]{0:T(128)S(1)} %pad_add_fusion.place_ref, ...), custom_call_target="tpu_custom_call" | custom-call | tf_op jit(solution)/shard_map/prepare/pallas_call | solution.py:499
  44.7 2.7 %piece_0.1.net = f32[4,16,512]{2,1,0:T(8,128)S(1)} custom-call(s32[3]{0:T(128)S(1)} %pad_add_fusion.place_ref, bf16[256,128,128]{2,1,0:T(8,128)(2,1)S(1)} %get-tuple-element.55.blk, f32[4,16,512]{2,1,0:T(8,128)S(1)} %broadcast_in_dim.6.net, f32[4,24,512]{2,1,0:T(8,128)S(1)} %get-tuple-element.59.rim, bf16[128,16]{1,0:T(8,128)(2,1)S(1)} %get-tuple-element.60.zf, ...), custom_call_target="tpu_custom_call" | custom-call | tf_op jit(solution)/shard_map/piece_0/pallas_call | solution.py:649
  47.4 0.0 collective-permute-done.10
  47.4 1.5 %collective-permute-start.13 = (bf16[256,128]{1,0:T(8,128)(2,1)S(1)}, bf16[256,128]{1,0:T(8,128)(2,1)S(1)}, u32[]{:S(2)}, u32[]{:S(2)}) collective-permute-start(bf16[256,128]{1,0:T(8,128)(2,1)S(1)} %add_convert_fusion.2), channel_id=1, source_target_pairs={{0,8},{4,12},{8,0},{12,4},{1,9},{5,13},{9,1},{13,5},{2,10},{6,14},... | collective-permute-start | bytes 196616 | tf_op jit(solution)/shard_map/ppermute | solution.py:681
  48.9 0.8 %collective-permute-start.12 = (bf16[256,128]{1,0:T(8,128)(2,1)S(1)}, bf16[256,128]{1,0:T(8,128)(2,1)S(1)}, u32[]{:S(2)}, u32[]{:S(2)}) collective-permute-start(bf16[256,128]{1,0:T(8,128)(2,1)S(1)} %add_convert_fusion.2), channel_id=1, source_target_pairs={{0,12},{4,0},{8,4},{12,8},{1,13},{5,1},{9,5},{13,9},{2,14},{6,2},{... | collective-permute-start | bytes 196616 | tf_op jit(solution)/shard_map/ppermute | solution.py:681
  49.7 0.6 collective-permute-start.11
  50.4 2.6 %piece_1.1.net = f32[4,16,512]{2,1,0:T(8,128)S(1)} custom-call(s32[3]{0:T(128)S(1)} %pad_add_fusion.place_ref, bf16[256,128,128]{2,1,0:T(8,128)(2,1)S(1)} %get-tuple-element.55.blk, f32[4,16,512]{2,1,0:T(8,128)S(1)} %piece_0.1.net, f32[4,24,512]{2,1,0:T(8,128)S(1)} %get-tuple-element.59.rim, bf16[128,16]{1,0:T(8,128)(2,1)S(1)} %get-tuple-element.60.zf, ...), custom_call_target="tpu_custom_call" | custom-call | tf_op jit(solution)/shard_map/piece_1/pallas_call | solution.py:649
  53.0 0.0 collective-permute-done.13
  53.0 0.0 collective-permute-done.12
  53.0 1.1 %collective-permute-done.11 = bf16[256,128]{1,0:T(8,128)(2,1)S(1)} collective-permute-done((bf16[256,128]{1,0:T(8,128)(2,1)S(1)}, bf16[256,128]{1,0:T(8,128)(2,1)S(1)}, u32[]{:S(2)}, u32[]{:S(2)}) %collective-permute-start.11) | collective-permute-done | bytes 65568 | tf_op jit(solution)/shard_map/ppermute | solution.py:681
  54.1 1.3 %collective-permute-start.16 = (bf16[256,128]{1,0:T(8,128)(2,1)S(1)}, bf16[256,128]{1,0:T(8,128)(2,1)S(1)}, u32[]{:S(2)}, u32[]{:S(2)}) collective-permute-start(bf16[256,128]{1,0:T(8,128)(2,1)S(1)} %add_convert_fusion.1), channel_id=1, source_target_pairs={{0,2},{1,3},{2,0},{3,1},{4,6},{5,7},{6,4},{7,5},{8,10},{9,11},{10,... | collective-permute-start | bytes 196616 | tf_op jit(solution)/shard_map/ppermute | solution.py:681
  55.4 1.7 %collective-permute-start.15 = (bf16[256,128]{1,0:T(8,128)(2,1)S(1)}, bf16[256,128]{1,0:T(8,128)(2,1)S(1)}, u32[]{:S(2)}, u32[]{:S(2)}) collective-permute-start(bf16[256,128]{1,0:T(8,128)(2,1)S(1)} %add_convert_fusion.1), channel_id=1, source_target_pairs={{0,3},{1,0},{2,1},{3,2},{4,7},{5,4},{6,5},{7,6},{8,11},{9,8},{10,9... | collective-permute-start | bytes 196616 | tf_op jit(solution)/shard_map/ppermute | solution.py:681
  57.1 0.5 collective-permute-start.14
  57.6 2.7 %piece_2.1.net = f32[4,16,512]{2,1,0:T(8,128)S(1)} custom-call(s32[3]{0:T(128)S(1)} %pad_add_fusion.place_ref, bf16[256,128,128]{2,1,0:T(8,128)(2,1)S(1)} %get-tuple-element.55.blk, f32[4,16,512]{2,1,0:T(8,128)S(1)} %piece_1.1.net, f32[4,24,512]{2,1,0:T(8,128)S(1)} %get-tuple-element.59.rim, bf16[128,16]{1,0:T(8,128)(2,1)S(1)} %get-tuple-element.60.zf, ...), custom_call_target="tpu_custom_call" | custom-call | tf_op jit(solution)/shard_map/piece_2/pallas_call | solution.py:649
  60.4 2.6 %piece_3.1.net_ref = f32[4,16,512]{2,1,0:T(8,128)S(1)} custom-call(s32[3]{0:T(128)S(1)} %pad_add_fusion.place_ref, bf16[256,128,128]{2,1,0:T(8,128)(2,1)S(1)} %get-tuple-element.55.blk, f32[4,16,512]{2,1,0:T(8,128)S(1)} %piece_2.1.net, f32[4,24,512]{2,1,0:T(8,128)S(1)} %get-tuple-element.59.rim, bf16[128,16]{1,0:T(8,128)(2,1)S(1)} %get-tuple-element.60.zf, ...), custom_call_target="tpu_custom_call" | custom-call | tf_op jit(solution)/shard_map/piece_3/pallas_call | solution.py:649
  63.0 0.0 collective-permute-done.16
  63.0 0.0 collective-permute-done.15
  63.0 0.0 collective-permute-done.14
  63.1 2.1 %back_reflect.1 = bf16[5,16,512]{2,1,0:T(8,128)(2,1)S(1)} custom-call(s32[256]{0:T(256)S(1)} %multiply_add_fusion.ray_ref, s32[256]{0:T(256)S(1)} %copy-done.5, bf16[256,128]{1,0:T(8,128)(2,1)S(1)} %add_convert_fusion.r_ref, f32[16,512]{1,0:T(8,128)S(1)} %get-tuple-element.71.x_ref, f32[16,512]{1,0:T(8,128)S(1)} %get-tuple-element.54.x_ref.start_ref, ...), custom_call_target="tpu_custom_call" | custom-call | tf_op jit(solution)/shard_map/back_reflect/pallas_call | solution.py:345
  65.2 10.6 %all-gather = bf16[20,16,512]{2,1,0:T(8,128)(2,1)S(1)} all-gather(bf16[5,16,512]{2,1,0:T(8,128)(2,1)S(1)} %back_reflect.1), channel_id=2, replica_groups=mesh['agent'=4,'tile'=32] {'agent'}, dimensions={0}, use_global_device_ids=true | all-gather | bytes 409600 | tf_op jit(solution)/shard_map/all_gather | solution.py:757
  75.8 1.3 %finish.1 = f32[4,16,512]{2,1,0:T(8,128)} custom-call(s32[3]{0:T(128)S(1)} %pad_add_fusion.place_ref, bf16[4,5,16,512]{3,2,1,0:T(8,128)(2,1)S(1)} %bitcast.14, f32[4,16,512]{2,1,0:T(8,128)S(1)} %bitcast.13, f32[4,16,512]{2,1,0:T(8,128)S(1)} %piece_3.1.net_ref), custom_call_target="tpu_custom_call" | custom-call | tf_op jit(solution)/shard_map/finish/pallas_call | solution.py:376
  (17 shorter events, 0.3 us)
Async XLA Ops:
  0.0 36.3 %copy-start.5 = (s32[256]{0:T(256)S(1)}, s32[256]{0:T(256)}, u32[]{:S(2)}) copy-start(s32[256]{0:T(256)} %tile_ref.3) | copy-start | bytes 3076
  0.0 34.0 %copy-start.6 = (s32[256]{0:T(256)S(1)}, s32[256]{0:T(256)}, u32[]{:S(2)}) copy-start(s32[256]{0:T(256)} %detector_in.1) | copy-start | bytes 3076
  0.0 34.0 %copy-start.7 = (s32[256]{0:T(256)S(1)}, s32[256]{0:T(256)}, u32[]{:S(2)}) copy-start(s32[256]{0:T(256)} %angle_in.1) | copy-start | bytes 3076
  0.0 36.3 %copy-start.2 = (f32[8,4,128]{2,1,0:T(4,128)S(1)}, f32[8,4,128]{2,1,0:T(4,128)}, u32[]{:S(2)}) copy-start(f32[8,4,128]{2,1,0:T(4,128)} %sino_ref.1) | copy-start | bytes 49156
  0.8 2.7 %collective-permute-start.2 = (f32[16,512]{1,0:T(8,128)S(1)}, f32[16,512]{1,0:T(8,128)S(1)}, u32[]{:S(2)}, u32[]{:S(2)}) collective-permute-start(f32[16,512]{1,0:T(8,128)S(1)} %get-tuple-element.73), channel_id=1, source_target_pairs={{0,96},{1,97},{2,98},{3,99},{4,100},{5,101},{6,102},{7,103},{8,104... | collective-permute-start | bytes 98312 | tf_op jit(solution)/shard_map/ppermute | solution.py:709
  1.5 2.1 %collective-permute-start.1 = (f32[16,512]{1,0:T(8,128)S(1)}, f32[16,512]{1,0:T(8,128)S(1)}, u32[]{:S(2)}, u32[]{:S(2)}) collective-permute-start(f32[16,512]{1,0:T(8,128)S(1)} %get-tuple-element.74), channel_id=1, source_target_pairs={{0,64},{1,65},{2,66},{3,67},{4,68},{5,69},{6,70},{7,71},{8,72},{9,... | collective-permute-start | bytes 98312 | tf_op jit(solution)/shard_map/ppermute | solution.py:709
  2.2 6.3 %collective-permute-start = (f32[16,512]{1,0:T(8,128)S(1)}, f32[16,512]{1,0:T(8,128)S(1)}, u32[]{:S(2)}, u32[]{:S(2)}) collective-permute-start(f32[16,512]{1,0:T(8,128)S(1)} %get-tuple-element.75), channel_id=1, source_target_pairs={{0,32},{1,33},{2,34},{3,35},{4,36},{5,37},{6,38},{7,39},{8,40},{9,... | collective-permute-start | bytes 98312 | tf_op jit(solution)/shard_map/ppermute | solution.py:709
  3.6 39.9 %copy-start = (f32[1,4,16,512]{3,2,1,0:T(8,128)S(1)}, f32[1,4,16,512]{3,2,1,0:T(8,128)}, u32[]{:S(2)}) copy-start(f32[1,4,16,512]{3,2,1,0:T(8,128)} %states_in.1) | copy-start | bytes 393220
  3.6 39.9 %copy-start.1 = (bf16[3,2,3,3,32,32]{5,4,3,2,1,0:T(8,128)(2,1)S(1)}, bf16[3,2,3,3,32,32]{5,4,3,2,1,0:T(8,128)(2,1)}, u32[]{:S(2)}) copy-start(bf16[3,2,3,3,32,32]{5,4,3,2,1,0:T(8,128)(2,1)} %hidden.1) | copy-start | bytes 331780
  3.6 39.9 %copy-start.3 = (bf16[3,3,3,32]{3,2,1,0:T(4,128)(2,1)S(1)}, bf16[3,3,3,32]{3,2,1,0:T(4,128)(2,1)}, u32[]{:S(2)}) copy-start(bf16[3,3,3,32]{3,2,1,0:T(4,128)(2,1)} %first.1) | copy-start | bytes 5188
  3.6 39.9 %copy-start.4 = (bf16[3,3,3,32]{3,2,1,0:T(4,128)(2,1)S(1)}, bf16[3,3,3,32]{3,2,1,0:T(4,128)(2,1)}, u32[]{:S(2)}) copy-start(bf16[3,3,3,32]{3,2,1,0:T(4,128)(2,1)} %last.1) | copy-start | bytes 5188
  14.0 5.5 %collective-permute-start.3 = (bf16[320,128]{1,0:T(8,128)(2,1)S(1)}, bf16[320,128]{1,0:T(8,128)(2,1)S(1)}, u32[]{:S(2)}, u32[]{:S(2)}) collective-permute-start(bf16[320,128]{1,0:T(8,128)(2,1)S(1)} %get-tuple-element.42), channel_id=1, source_target_pairs={{0,16},{16,0},{1,17},{17,1},{2,18},{18,2},{3,19},{19,3},{4,20},{20... | collective-permute-start | bytes 245768 | tf_op jit(solution)/shard_map/ppermute | solution.py:689
  19.6 4.6 %collective-permute-start.4 = (bf16[320,128]{1,0:T(8,128)(2,1)S(1)}, bf16[320,128]{1,0:T(8,128)(2,1)S(1)}, u32[]{:S(2)}, u32[]{:S(2)}) collective-permute-start(bf16[320,128]{1,0:T(8,128)(2,1)S(1)} %get-tuple-element.78), channel_id=1, source_target_pairs={{0,4},{4,8},{8,12},{12,0},{1,5},{5,9},{9,13},{13,1},{2,6},{6,10},{... | collective-permute-start | bytes 245768 | tf_op jit(solution)/shard_map/ppermute | solution.py:698
  20.9 3.3 %collective-permute-start.6 = (bf16[320,128]{1,0:T(8,128)(2,1)S(1)}, bf16[320,128]{1,0:T(8,128)(2,1)S(1)}, u32[]{:S(2)}, u32[]{:S(2)}) collective-permute-start(bf16[320,128]{1,0:T(8,128)(2,1)S(1)} %get-tuple-element.79), channel_id=1, source_target_pairs={{0,12},{4,0},{8,4},{12,8},{1,13},{5,1},{9,5},{13,9},{2,14},{6,2},{... | collective-permute-start | bytes 245768 | tf_op jit(solution)/shard_map/ppermute | solution.py:700
  22.5 5.1 %collective-permute-start.5 = (bf16[256,128]{1,0:T(8,128)(2,1)S(1)}, bf16[256,128]{1,0:T(8,128)(2,1)S(1)}, u32[]{:S(2)}, u32[]{:S(2)}) collective-permute-start(bf16[256,128]{1,0:T(8,128)(2,1)S(1)} %add_convert_fusion.5), channel_id=1, source_target_pairs={{0,8},{4,12},{8,0},{12,4},{1,9},{5,13},{9,1},{13,5},{2,10},{6,14},... | collective-permute-start | bytes 196616 | tf_op jit(solution)/shard_map/ppermute | solution.py:699
  27.6 6.5 %collective-permute-start.8 = (bf16[256,128]{1,0:T(8,128)(2,1)S(1)}, bf16[256,128]{1,0:T(8,128)(2,1)S(1)}, u32[]{:S(2)}, u32[]{:S(2)}) collective-permute-start(bf16[256,128]{1,0:T(8,128)(2,1)S(1)} %add_convert_fusion.4), channel_id=1, source_target_pairs={{0,2},{1,3},{2,0},{3,1},{4,6},{5,7},{6,4},{7,5},{8,10},{9,11},{10,... | collective-permute-start | bytes 196616 | tf_op jit(solution)/shard_map/ppermute | solution.py:699
  31.3 5.0 %collective-permute-start.7 = (bf16[320,128]{1,0:T(8,128)(2,1)S(1)}, bf16[320,128]{1,0:T(8,128)(2,1)S(1)}, u32[]{:S(2)}, u32[]{:S(2)}) collective-permute-start(bf16[320,128]{1,0:T(8,128)(2,1)S(1)} %get-tuple-element.76), channel_id=1, source_target_pairs={{0,1},{1,2},{2,3},{3,0},{4,5},{5,6},{6,7},{7,4},{8,9},{9,10},{10,1... | collective-permute-start | bytes 245768 | tf_op jit(solution)/shard_map/ppermute | solution.py:698
  32.1 4.2 %collective-permute-start.9 = (bf16[320,128]{1,0:T(8,128)(2,1)S(1)}, bf16[320,128]{1,0:T(8,128)(2,1)S(1)}, u32[]{:S(2)}, u32[]{:S(2)}) collective-permute-start(bf16[320,128]{1,0:T(8,128)(2,1)S(1)} %get-tuple-element.77), channel_id=1, source_target_pairs={{0,3},{1,0},{2,1},{3,2},{4,7},{5,4},{6,5},{7,6},{8,11},{9,8},{10,9... | collective-permute-start | bytes 245768 | tf_op jit(solution)/shard_map/ppermute | solution.py:700
  40.9 6.5 %collective-permute-start.10 = (bf16[256,128]{1,0:T(8,128)(2,1)S(1)}, bf16[256,128]{1,0:T(8,128)(2,1)S(1)}, u32[]{:S(2)}, u32[]{:S(2)}) collective-permute-start(bf16[256,128]{1,0:T(8,128)(2,1)S(1)} %get-tuple-element.57), channel_id=1, source_target_pairs={{0,16},{16,0},{1,17},{17,1},{2,18},{18,2},{3,19},{19,3},{4,20},{20... | collective-permute-start | bytes 196616 | tf_op jit(solution)/shard_map/ppermute | solution.py:681
  47.4 5.6 %collective-permute-start.13 = (bf16[256,128]{1,0:T(8,128)(2,1)S(1)}, bf16[256,128]{1,0:T(8,128)(2,1)S(1)}, u32[]{:S(2)}, u32[]{:S(2)}) collective-permute-start(bf16[256,128]{1,0:T(8,128)(2,1)S(1)} %add_convert_fusion.2), channel_id=1, source_target_pairs={{0,8},{4,12},{8,0},{12,4},{1,9},{5,13},{9,1},{13,5},{2,10},{6,14},... | collective-permute-start | bytes 196616 | tf_op jit(solution)/shard_map/ppermute | solution.py:681
  48.9 4.1 %collective-permute-start.12 = (bf16[256,128]{1,0:T(8,128)(2,1)S(1)}, bf16[256,128]{1,0:T(8,128)(2,1)S(1)}, u32[]{:S(2)}, u32[]{:S(2)}) collective-permute-start(bf16[256,128]{1,0:T(8,128)(2,1)S(1)} %add_convert_fusion.2), channel_id=1, source_target_pairs={{0,12},{4,0},{8,4},{12,8},{1,13},{5,1},{9,5},{13,9},{2,14},{6,2},{... | collective-permute-start | bytes 196616 | tf_op jit(solution)/shard_map/ppermute | solution.py:681
  49.7 4.3 %collective-permute-start.11 = (bf16[256,128]{1,0:T(8,128)(2,1)S(1)}, bf16[256,128]{1,0:T(8,128)(2,1)S(1)}, u32[]{:S(2)}, u32[]{:S(2)}) collective-permute-start(bf16[256,128]{1,0:T(8,128)(2,1)S(1)} %add_convert_fusion.2), channel_id=1, source_target_pairs={{0,4},{4,8},{8,12},{12,0},{1,5},{5,9},{9,13},{13,1},{2,6},{6,10},{... | collective-permute-start | bytes 196616 | tf_op jit(solution)/shard_map/ppermute | solution.py:681
  54.1 8.9 %collective-permute-start.16 = (bf16[256,128]{1,0:T(8,128)(2,1)S(1)}, bf16[256,128]{1,0:T(8,128)(2,1)S(1)}, u32[]{:S(2)}, u32[]{:S(2)}) collective-permute-start(bf16[256,128]{1,0:T(8,128)(2,1)S(1)} %add_convert_fusion.1), channel_id=1, source_target_pairs={{0,2},{1,3},{2,0},{3,1},{4,6},{5,7},{6,4},{7,5},{8,10},{9,11},{10,... | collective-permute-start | bytes 196616 | tf_op jit(solution)/shard_map/ppermute | solution.py:681
  55.4 7.6 %collective-permute-start.15 = (bf16[256,128]{1,0:T(8,128)(2,1)S(1)}, bf16[256,128]{1,0:T(8,128)(2,1)S(1)}, u32[]{:S(2)}, u32[]{:S(2)}) collective-permute-start(bf16[256,128]{1,0:T(8,128)(2,1)S(1)} %add_convert_fusion.1), channel_id=1, source_target_pairs={{0,3},{1,0},{2,1},{3,2},{4,7},{5,4},{6,5},{7,6},{8,11},{9,8},{10,9... | collective-permute-start | bytes 196616 | tf_op jit(solution)/shard_map/ppermute | solution.py:681
  57.1 5.9 %collective-permute-start.14 = (bf16[256,128]{1,0:T(8,128)(2,1)S(1)}, bf16[256,128]{1,0:T(8,128)(2,1)S(1)}, u32[]{:S(2)}, u32[]{:S(2)}) collective-permute-start(bf16[256,128]{1,0:T(8,128)(2,1)S(1)} %add_convert_fusion.1), channel_id=1, source_target_pairs={{0,1},{1,2},{2,3},{3,0},{4,5},{5,6},{6,7},{7,4},{8,9},{9,10},{10,1... | collective-permute-start | bytes 196616 | tf_op jit(solution)/shard_map/ppermute | solution.py:681
